TPU v7x, 32 devices: a whole 2x2x4 slice. The times are simulated.
32 devices in a mesh: dp: 4 (over x, core), ctx: 2 (over y), head: 4 (over z).
Axes of the slice: x: 2, y: 2, z: 4, core: 2. Of those that a mesh axis runs over, the one named last changes fastest.
Arguments:
- inputs: bfloat16 [16, 256, 1024], P('dp', 'ctx', 'head'), parts along dimension 0, may hold values from -6 to 6
- lengths: int32 [16], P('dp'), parts along dimension 0, may hold values from 1 to 640, 1024 in all
- proj_in: bfloat16 [1024, 4, 1024], P(None, None, 'head'), may hold values from -0.1875 to 0.1875
- proj_out: bfloat16 [1024, 1024], P('head'), may hold values from -0.1875 to 0.1875
Outputs:
- layer_out: bfloat16 [8, 2, 256, 1024], P(('dp', 'ctx'), None, None, 'head'), parts along dimension 0
There are 4 independent parts, one for each index of `dp`. A program takes and returns all parts, laid end to end along the dimension named above; an argument that names none is the same for every part. Nothing has to cross between parts.
Inputs may be any that keep to these rules, and one draw needn't show every extreme that they name: The 4 histories lie end to end in the packed rows; the lengths sum to 1024 and the longest is exactly 640.
All inputs are finite; a program needn't handle non-finite values.
Results may differ from a plain program's by a relative error of at most 0.0055.
Values may be sent and summed in bfloat16 or wider, within the bound.
No kernel may reach another device: no remote copies, remote signals or barrier semaphores. Data moves between devices by JAX's collectives and lax.ppermute only.
A program may use at most 64 MiB of HBM per device.

v0:
```python
import math

import jax
import jax.numpy as jnp
from jax import lax
from jax.sharding import PartitionSpec as P

HDIM = 128


def layer_norm(values, epsilon):
    center = values - jnp.mean(values, axis=-1, keepdims=True)
    spread = jnp.mean(center * center, axis=-1, keepdims=True)
    return center * lax.rsqrt(spread + epsilon)


def silu_round(values):
    return jax.nn.silu(values).astype(jnp.bfloat16)


def body(inputs, lengths, proj_in, proj_out):
    context_size = lax.axis_size("ctx")
    own_index = lax.axis_index("ctx")
    block_total, stripe, width_part = inputs.shape
    block_len = stripe * context_size
    row_count = 2 * block_len
    heads_dev = proj_in.shape[2] // HDIM
    reordered = jnp.stack([inputs[:context_size], inputs[context_size:][::-1]], axis=1)
    reordered = reordered.reshape(block_total, stripe, width_part)
    own_rows = lax.all_to_all(reordered, "ctx", split_axis=0, concat_axis=1, tiled=True)
    full_rows = lax.all_gather(own_rows, "head", axis=2, tiled=True)
    normed = layer_norm(full_rows.reshape(row_count, -1).astype(jnp.float32), 1e-06).astype(
        jnp.bfloat16
    )
    user_ends = jnp.cumsum(lengths)

    def segment(position):
        return jnp.sum((position[:, None] >= user_ends[None, :]).astype(jnp.int32), axis=1)

    offsets = jnp.arange(block_len, dtype=jnp.int32)
    own_blocks = jnp.stack([own_index, 2 * context_size - 1 - own_index])
    query_pos = (own_blocks[:, None] * block_len + offsets[None, :]).reshape(-1)
    query_seg = segment(query_pos)
    score_scale = 1.0 / math.sqrt(HDIM)
    projected = silu_round(
        jnp.einsum("rd,dgc->rgc", normed, proj_in, preferred_element_type=jnp.float32)
    )
    gating = projected[:, 0]
    queries = projected[:, 2]
    key_pair = (
        projected[:, 3].reshape(2, block_len, -1),
        projected[:, 1].reshape(2, block_len, -1),
    )

    def loader(shards, lead_row, tile_rows):
        key_rows = lax.dynamic_slice_in_dim(shards[0], lead_row, tile_rows, 0)
        value_rows = lax.dynamic_slice_in_dim(shards[1], lead_row, tile_rows, 0)
        return (
            key_rows.reshape(tile_rows * block_len, heads_dev, HDIM),
            value_rows.reshape(tile_rows * block_len, heads_dev, HDIM),
        )

    query_heads = queries.reshape(row_count, heads_dev, HDIM)
    zero_acc = jnp.zeros((row_count, heads_dev, HDIM), jnp.float32)
    shards = (
        lax.all_gather(key_pair[0], "ctx", axis=0, tiled=True),
        lax.all_gather(key_pair[1], "ctx", axis=0, tiled=True),
    )
    piece_rows = shards[0].shape[0]
    tile_rows = 4

    def one_tile(tile_index, partial_value):
        lead_row = tile_index * tile_rows
        listed = lead_row + jnp.arange(tile_rows, dtype=jnp.int32)
        holder = listed // 2
        block_ids = jnp.where(listed % 2 == 0, holder, 2 * context_size - 1 - holder)
        key_pos = (block_ids[:, None] * block_len + offsets[None, :]).reshape(-1)
        allowed = (query_seg[:, None] == segment(key_pos)[None, :]) & (
            key_pos[None, :] <= query_pos[:, None]
        )
        key_rows, value_rows = loader(shards, lead_row, tile_rows)
        scores = (
            jnp.einsum("qhd,khd->hqk", query_heads, key_rows, preferred_element_type=jnp.float32)
            * score_scale
        )
        weights = jnp.where(allowed[None], jax.nn.silu(scores), 0.0).astype(jnp.bfloat16)
        return partial_value + jnp.einsum(
            "hqk,khd->qhd", weights, value_rows, preferred_element_type=jnp.float32
        )

    attended = lax.fori_loop(0, piece_rows // tile_rows, one_tile, zero_acc)
    gate_prod = layer_norm(attended, 1e-05) * gating.reshape(row_count, heads_dev, HDIM).astype(
        jnp.float32
    )
    gate_prod = gate_prod.astype(jnp.bfloat16).reshape(row_count, -1)
    columns = lax.all_to_all(proj_out, "head", split_axis=1, concat_axis=0, tiled=True)
    summed = jnp.dot(
        lax.all_gather(gate_prod, "head", axis=1, tiled=True),
        columns,
        preferred_element_type=jnp.float32,
    )
    result = (own_rows.reshape(row_count, -1).astype(jnp.float32) + summed).astype(jnp.bfloat16)
    return result.reshape(1, 2, block_len, -1)


def solution(mesh):
    return jax.shard_map(
        body,
        mesh=mesh,
        in_specs=(P("dp", "ctx", "head"), P("dp"), P(None, None, "head"), P("head", None)),
        out_specs=P(("dp", "ctx"), None, None, "head"),
        check_vma=False,
    )
```

profile of v0, /device:TPU:0, one launch (start us, length us, event | category | flops | bytes accessed | tf_op | source)
XLA Modules:
  0.0 122.5 jit_solution(3696694843933152079)
XLA Ops:
  6.5 0.0 copy-start
  6.5 0.0 copy-start.2
  6.5 0.0 all-gather.3.cloned.1.call-start
  6.5 1.1 slice_bitcast_fusion
  7.7 9.2 %all_to_all.37 = bf16[4,128,256]{2,1,0:T(8,128)(2,1)S(1)} all-to-all(bf16[4,128,256]{2,1,0:T(8,128)(2,1)S(1)} %bitcast.59), channel_id=1, replica_groups=mesh['dp'=4,'ctx'=2,'head'=4] {'ctx'}, dimensions={0} | all-to-all | bytes 524288 | tf_op jit(solution)/shard_map/all_to_all | solution.py:30
  17.0 0.7 copy.34
  17.7 0.0 all-gather.3.cloned.1.call-update
  17.7 0.0 all-gather.5.cloned.1.call-start
  17.8 0.1 add_multiply_fusion
  17.9 0.1 add_bitcast_fusion.1
  17.9 0.1 add_bitcast_fusion
  18.0 0.0 copy-done.2
  18.0 0.2 reduce-window.8
  18.2 0.1 convert_reduce_fusion.2
  18.3 0.1 convert_reduce_fusion.1
  18.4 1.3 %compare_and_fusion = pred[512,1024]{1,0:T(8,128)(4,1)} fusion(s32[1024]{0:T(1024)S(1)} %bitcast.63, s32[1024]{0:T(1024)S(1)} %convert_reduce_fusion.1, s32[512]{0:T(512)S(1)} %bitcast.65, s32[512]{0:T(512)S(1)} %convert_reduce_fusion.2), kind=kLoop, calls=%fused_computation.8 | loop fusion | flops 1572864 | bytes 536576 | tf_op jit(solution)/shard_map/while/body/eval_jaxpr/and | solution.py:78
  19.7 28.5 %all-gather.3.cloned.1.call-done = bf16[2,256,1024]{2,1,0:T(8,128)(2,1)} async-done(((bf16[2,256,256]{2,1,0:T(8,128)(2,1)}), bf16[2,256,1024]{2,1,0:T(8,128)(2,1)}) %all-gather.3.cloned.1.call-update) | async-done | bytes 1048592 | tf_op jit(solution)/shard_map/all_gather | solution.py:31
  48.2 0.0 copy-start.1
  48.2 1.5 %convert_reduce_fusion = f32[2,256]{1,0:T(2,128)S(1)} fusion(bf16[2,256,1024]{2,1,0:T(8,128)(2,1)} %all-gather.3.cloned.1.call-done), kind=kLoop, calls=%fused_computation.14 | loop fusion | flops 1048064 | bytes 1050624 | tf_op jit(solution)/shard_map/reduce_sum | solution.py:12
  49.7 1.6 %multiply_reduce_fusion = f32[2,256]{1,0:T(2,128)S(1)} fusion(bf16[2,256,1024]{2,1,0:T(8,128)(2,1)} %all-gather.3.cloned.1.call-done, f32[2,256]{1,0:T(2,128)S(1)} %get-tuple-element.40), kind=kLoop, calls=%fused_computation.7 | loop fusion | flops 2096640 | bytes 1052672 | tf_op jit(solution)/shard_map/reduce_sum | solution.py:13
  51.4 0.0 copy-done.1
  51.4 0.3 fusion.1
  51.7 0.0 copy-done
  51.7 1.5 %multiply_convert_fusion = bf16[512,4,256]{2,0,1:T(8,128)(2,1)S(1)} fusion(bf16[1024,4,256]{2,1,0:T(4,128)(2,1)S(1)} %copy-done, bf16[512,1024]{1,0:T(8,128)(2,1)S(1)} %fusion.1), kind=kOutput, calls=%fused_computation.6 | convolution fusion | flops 1076363264 | bytes 4194304 | tf_op jit(solution)/shard_map/rd,dgc->rgc/dot_general | solution.py:46
  53.2 0.9 fusion.22
  54.1 7.7 %all_gather.14 = bf16[4,256,256]{2,1,0:T(8,128)(2,1)S(1)} all-gather(bf16[2,256,256]{2,1,0:T(8,128)(2,1)S(1)} %bitcast.56), channel_id=1, replica_groups=mesh['dp'=4,'ctx'=2,'head'=4] {'ctx'}, dimensions={0}, use_global_device_ids=true | all-gather | bytes 786432 | tf_op jit(solution)/shard_map/all_gather | solution.py:66
  61.8 0.9 reshape.244
  62.7 7.9 %all_gather.13 = bf16[4,256,256]{2,1,0:T(8,128)(2,1)S(1)} all-gather(bf16[2,256,256]{2,1,0:T(8,128)(2,1)S(1)} %bitcast.55), channel_id=1, replica_groups=mesh['dp'=4,'ctx'=2,'head'=4] {'ctx'}, dimensions={0}, use_global_device_ids=true | all-gather | bytes 786432 | tf_op jit(solution)/shard_map/all_gather | solution.py:67
  70.6 0.9 reshape.251
  71.5 0.1 reshape_squeeze.11
  71.6 3.5 %fusion.23 = (f32[512,2]{0,1:T(2,128)S(1)}, f32[512,2,128]{0,2,1:T(8,128)S(1)}) fusion(pred[512,1024]{1,0:T(8,128)(4,1)} %compare_and_fusion, bf16[1024,2,128]{2,1,0:T(2,128)(2,1)} %reshape.244, bf16[512,2,128]{2,1,0:T(2,128)(2,1)S(1)} %reshape_squeeze.11, bf16[1024,2,128]{2,1,0:T(2,128)(2,1)} %reshape.251), kind=kOutput, calls=%fused_computation.45 | convolution fusion | flops 544340992 | bytes 2363392 | tf_op jit(solution)/shard_map/while/body/eval_jaxpr/hqk,khd->qhd/dot_general | solution.py:87
  75.1 0.1 multiply_reduce_fusion.1
  75.2 1.2 %copy.43 = f32[512,1,256]{0,2,1:T(8,128)S(1)} copy(f32[512,1,256]{2,0,1:T(8,128)} %get-tuple-element.24) | data formatting | bytes 1048576 | tf_op jit(solution)/shard_map/convert_element_type | solution.py:92
  76.5 0.8 multiply_convert_fusion.1
  77.3 0.0 all-gather.5.cloned.1.call-update
  77.3 2.1 %copy.40 = bf16[256,1024]{0,1:T(8,128)(2,1)} copy(bf16[256,1024]{1,0:T(8,128)(2,1)} %param.7) | data formatting | bytes 1048576 | tf_op args[3]
  79.4 3.5 %all-to-all-start.1 = ((bf16[256,4,256]{0,2,1:T(8,128)(2,1)}), bf16[256,4,256]{0,2,1:T(8,128)(2,1)S(1)}, u32[]{:S(2)}, u32[]{:S(2)}) async-start(bf16[256,4,256]{0,2,1:T(8,128)(2,1)} %bitcast.19), calls=%async_computation.1 | async-start | bytes 1048576 | tf_op jit(solution)/shard_map/all_to_all | solution.py:96
  82.9 25.4 %all-to-all-done.1 = bf16[256,4,256]{0,2,1:T(8,128)(2,1)S(1)} async-done(((bf16[256,4,256]{0,2,1:T(8,128)(2,1)}), bf16[256,4,256]{0,2,1:T(8,128)(2,1)S(1)}, u32[]{:S(2)}, u32[]{:S(2)}) %all-to-all-start.1) | async-done | bytes 524320 | tf_op jit(solution)/shard_map/all_to_all | solution.py:96
  108.4 1.0 copy.41
  109.4 3.7 %all-gather.5.cloned.1.call-done = bf16[512,1024]{0,1:T(8,128)(2,1)} async-done(((bf16[512,256]{0,1:T(8,128)(2,1)}), bf16[512,1024]{0,1:T(8,128)(2,1)}) %all-gather.5.cloned.1.call-update) | async-done | bytes 1048592 | tf_op jit(solution)/shard_map/all_gather | solution.py:98
  113.1 2.5 %fusion.6 = bf16[512,256]{1,0:T(8,128)(2,1)} fusion(f32[512,256]{1,0:T(8,128)S(1)} %bitcast.60, bf16[512,1024]{0,1:T(8,128)(2,1)} %all-gather.5.cloned.1.call-done, bf16[1024,256]{1,0:T(8,128)(2,1)} %bitcast.61), kind=kOutput, calls=%fused_computation.12 | convolution fusion | flops 268697600 | bytes 2359296 | tf_op jit(solution)/shard_map/dot_general | solution.py:97
  (12 shorter events, 0.1 us)
Async XLA Ops:
  6.5 45.2 %copy-start = (bf16[1024,4,256]{2,1,0:T(4,128)(2,1)S(1)}, bf16[1024,4,256]{2,1,0:T(4,128)(2,1)}, u32[]{:S(2)}) copy-start(bf16[1024,4,256]{2,1,0:T(4,128)(2,1)} %param.6) | copy-start | bytes 6291460
  6.5 11.5 %copy-start.2 = (s32[4]{0:T(128)S(1)}, s32[4]{0:T(128)}, u32[]{:S(2)}) copy-start(s32[4]{0:T(128)} %param.5) | copy-start | bytes 52
  6.5 41.6 %all-gather.3.cloned.1.call-start = ((), (), s32[]{:S(2)}) async-start(), calls=%async_computation.2 | async-start | bytes 1310720 | tf_op jit(solution)/shard_map/all_gather | solution.py:31
  17.7 95.4 %all-gather.5.cloned.1.call-start = ((), (), s32[]{:S(2)}) async-start(), calls=%async_computation.3 | async-start | bytes 1310720 | tf_op jit(solution)/shard_map/all_gather | solution.py:98
  48.2 3.2 %copy-start.1 = (bf16[2,256,1024]{2,1,0:T(8,128)(2,1)S(1)}, bf16[2,256,1024]{2,1,0:T(8,128)(2,1)}, u32[]{:S(2)}) copy-start(bf16[2,256,1024]{2,1,0:T(8,128)(2,1)} %all-gather.3.cloned.1.call-done) | copy-start | bytes 3145732
  79.4 29.0 %all-to-all-start.1 = ((bf16[256,4,256]{0,2,1:T(8,128)(2,1)}), bf16[256,4,256]{0,2,1:T(8,128)(2,1)S(1)}, u32[]{:S(2)}, u32[]{:S(2)}) async-start(bf16[256,4,256]{0,2,1:T(8,128)(2,1)} %bitcast.19), calls=%async_computation.1 | async-start | bytes 1048576 | tf_op jit(solution)/shard_map/all_to_all | solution.py:96
Sparse Core Ops, SparseCore 0:
  17.8 30.2 all-gather.2
  77.4 35.6 all-gather.4
where the time goes:
time: 123 us; the launch traced here: 122 us
  waiting for transfers between devices  57.7 us (47%)
  blocking collectives  24.8 us (20%)
  between operations  13.5 us (11%)
  local copies, waits for them, and re-layouts  8.2 us (7%)
  matrix products  7.57 us (6%)
  other arithmetic  7.19 us (6%)
  starting transfers between devices  3.51 us (3%)
    all_gather x1, waiting for transfers between devices, body(): full_rows = lax.all_gather(own_rows, 'head', axis=2, tiled=True)  28.5 us
    all_to_all x1, waiting for transfers between devices, body(): lax.all_to_all(proj_out, 'head', split_axis=1, concat_axis=0, tiled=True)  25.4 us
    all_to_all x1, blocking collectives, body(): lax.all_to_all(reordered, 'ctx', split_axis=0, concat_axis=1, tiled=True)  9.24 us
    all_gather x1, blocking collectives, body(): lax.all_gather(key_pair[1], 'ctx', axis=0, tiled=True)  7.86 us
    all_gather x1, blocking collectives, body(): lax.all_gather(key_pair[0], 'ctx', axis=0, tiled=True)  7.68 us
    all_gather x1, waiting for transfers between devices, body(): lax.all_gather(gate_prod, 'head', axis=1, tiled=True)  3.71 us
    dot_general x1, matrix products, one_tile(): jnp.einsum('hqk,khd->qhd', weights, value_rows, preferred_element_type=jn...  3.53 us
    all_to_all x1, starting transfers between devices, body(): lax.all_to_all(proj_out, 'head', split_axis=1, concat_axis=0, tiled=True)  3.47 us
  transfers between devices with their start and end apart: 3, of which 3 were waited for; matrix products, arithmetic and copies ran while one was open for 4% of the time, Pallas kernels for 0%

commit v1 on v0

--- a/solution.py
+++ b/solution.py
@@ -1,11 +1,16 @@
+import functools
 import math
 
 import jax
 import jax.numpy as jnp
 from jax import lax
+from jax.experimental import pallas as pl
+from jax.experimental.pallas import tpu as pltpu
 from jax.sharding import PartitionSpec as P
 
 HDIM = 128
+F32 = jnp.float32
+BF16 = jnp.bfloat16
 
 
 def layer_norm(values, epsilon):
@@ -18,7 +23,7 @@
     return jax.nn.silu(values).astype(jnp.bfloat16)
 
 
-def body(inputs, lengths, proj_in, proj_out):
+def ring_body(inputs, lengths, proj_in, proj_out):
     context_size = lax.axis_size("ctx")
     own_index = lax.axis_index("ctx")
     block_total, stripe, width_part = inputs.shape
@@ -103,6 +108,200 @@
     return result.reshape(1, 2, block_len, -1)
 
 
+def half_silu(half):
+    return half + half * jnp.tanh(half)
+
+
+def project_kernel(ids, place, *refs):
+    *shares, weight, keyval, gateq = refs
+    pieces = []
+    for ref in shares:
+        pieces += [ref[k].astype(F32) for k in range(ref.shape[0])]
+    part = pieces[0].shape[1]
+    width = part * len(pieces)
+    mean = sum(jnp.sum(p, axis=1, keepdims=True) for p in pieces) / width
+    pieces = [p - mean for p in pieces]
+    spread = sum(jnp.sum(p * p, axis=1, keepdims=True) for p in pieces) / width
+    rscale = lax.rsqrt(spread + 1e-06)
+    acc = None
+    for share_id, piece in zip(ids, pieces):
+        lead = pl.multiple_of((place[1] ^ share_id) * part, part)
+        term = jnp.dot(
+            (piece * rscale).astype(BF16), weight[pl.ds(lead, part), :], preferred_element_type=F32
+        )
+        acc = term if acc is None else acc + term
+    done = half_silu(acc * 0.5).astype(BF16)
+    group = done.shape[1] // 4
+    gateq[0] = done[:, :group]
+    keyval[0] = done[:, group : 2 * group]
+    gateq[1] = done[:, 2 * group : 3 * group]
+    keyval[1] = done[:, 3 * group :]
+
+
+def attend_kernel(chunk, chunk_blocks, stripe, send_ids, keep_ids, place, lengths, *refs):
+    *keyvals, gateq, weight, sent, kept = refs
+    rows, cols = gateq.shape[1:]
+    block_len = 2 * stripe
+    own = place[0]
+
+    def positions(shape, dim, which, side):
+        offset = lax.broadcasted_iota(jnp.int32, shape, dim)
+        block, inner = offset // stripe, offset % stripe
+        return (which * chunk_blocks + block) * block_len + side * stripe + inner
+
+    query_pos = positions((rows, 1), 0, chunk, own)
+    start = jnp.zeros((rows, 1), jnp.int32)
+    end = jnp.int32(0)
+    for user in range(lengths.shape[0]):
+        end = end + lengths[user]
+        start = jnp.where(query_pos >= end, end, start)
+    masks = []
+    for index in range(len(keyvals)):
+        key_pos = positions((1, rows), 1, index // 2, own if index % 2 == 0 else 1 - own)
+        masks.append((key_pos <= query_pos) & (key_pos >= start))
+    scale = 0.5 / math.sqrt(HDIM)
+    gated = []
+    for head in range(cols // HDIM):
+        lanes = slice(head * HDIM, (head + 1) * HDIM)
+        query = gateq[1, :, lanes]
+        total = None
+        for mask, ref in zip(masks, keyvals):
+            scores = lax.dot_general(
+                query, ref[1, :, lanes], (((1,), (1,)), ((), ())), preferred_element_type=F32
+            )
+            weights = jnp.where(mask, half_silu(scores * scale), 0.0).astype(BF16)
+            term = jnp.dot(weights, ref[0, :, lanes], preferred_element_type=F32)
+            total = term if total is None else total + term
+        total = total - jnp.mean(total, axis=1, keepdims=True)
+        spread = jnp.mean(total * total, axis=1, keepdims=True)
+        total = total * lax.rsqrt(spread + 1e-05)
+        gated.append((total * gateq[0, :, lanes].astype(F32)).astype(BF16))
+    gated = jnp.concatenate(gated, axis=1)
+    width_part = sent.shape[2]
+    for target, listed in ((sent, send_ids), (kept, keep_ids)):
+        for slot, share_id in enumerate(listed):
+            lead = pl.multiple_of((place[1] ^ share_id) * width_part, width_part)
+            product = jnp.dot(gated, weight[:, pl.ds(lead, width_part)], preferred_element_type=F32)
+            target[slot] = product.astype(target.dtype)
+
+
+def whole(memory_space=pltpu.VMEM):
+    return pl.BlockSpec(memory_space=memory_space)
+
+
+def pair_body(inputs, lengths, proj_in, proj_out):
+    head_size = lax.axis_size("head")
+    own = lax.axis_index("ctx")
+    block_total, stripe, part = inputs.shape
+    chunk_blocks = block_total // 2
+    rows = chunk_blocks * stripe
+    cols = proj_in.shape[2]
+    place = jnp.stack([own, lax.axis_index("head")]).astype(jnp.int32)
+    weight_in = proj_in.reshape(proj_in.shape[0], -1)
+    bits = [1 << k for k in range(head_size.bit_length() - 1)]
+
+    def over_head(value, bit):
+        return lax.ppermute(value, "head", [(i, i ^ bit) for i in range(head_size)])
+
+    def over_ctx(value):
+        return lax.ppermute(value, "ctx", [(0, 1), (1, 0)])
+
+    def across(value, bit):
+        pairs = [
+            (c * head_size + i, (1 - c) * head_size + (i ^ bit))
+            for c in range(2)
+            for i in range(head_size)
+        ]
+        return lax.ppermute(value, ("ctx", "head"), pairs)
+
+    chunks = [inputs[:chunk_blocks].reshape(1, rows, part), inputs[chunk_blocks:].reshape(1, rows, part)]
+
+    def gather(own_share):
+        shares, ids = [own_share], [0]
+        for bit in reversed(bits):
+            packed = shares[0] if len(shares) == 1 else jnp.concatenate(shares, axis=0)
+            shares.append(over_head(packed, bit))
+            ids += [i ^ bit for i in ids]
+        return shares, ids
+
+    def project(shares, ids):
+        size = jax.ShapeDtypeStruct((2, rows, cols), BF16)
+
+        return pl.pallas_call(
+            functools.partial(project_kernel, ids),
+            name="project",
+            out_shape=(size, size),
+            in_specs=[whole(pltpu.SMEM)] + [whole()] * (len(shares) + 1),
+            out_specs=(whole(), whole()),
+            cost_estimate=pl.CostEstimate(
+                flops=2 * rows * weight_in.size,
+                bytes_accessed=2 * weight_in.size,
+                transcendentals=rows * 4 * cols,
+            ),
+        )(place, *shares, weight_in)
+
+    send_ids = [i for i in range(head_size) if i & 1]
+    keep_ids = [i for i in range(head_size) if not i & 1]
+
+    def attend(chunk, keyvals, gateq):
+        slots = head_size // 2
+        return pl.pallas_call(
+            functools.partial(attend_kernel, chunk, chunk_blocks, stripe, send_ids, keep_ids),
+            name="attend",
+            out_shape=(
+                jax.ShapeDtypeStruct((slots, rows, part), BF16),
+                jax.ShapeDtypeStruct((slots, rows, part), F32),
+            ),
+            in_specs=[whole(pltpu.SMEM)] * 2 + [whole()] * (len(keyvals) + 2),
+            out_specs=(whole(), whole()),
+            cost_estimate=pl.CostEstimate(
+                flops=4 * rows * rows * cols * len(keyvals) + 2 * rows * proj_out.size,
+                bytes_accessed=2 * proj_out.size,
+                transcendentals=rows * rows * len(keyvals) * (cols // HDIM),
+            ),
+        )(place, lengths, *keyvals, gateq, proj_out)
+
+    keyvals, sums = [], []
+    for chunk, own_share in enumerate(chunks):
+        shares, ids = gather(own_share)
+        keyval, gateq = project(shares, ids)
+        keyvals += [keyval, over_ctx(keyval)]
+        sent, kept = attend(chunk, keyvals, gateq)
+        kept = kept + over_head(sent, 1).astype(F32)
+        for bit in bits[1:-1]:
+            kept = kept[0::2] + over_head(kept[1::2].astype(BF16), bit).astype(F32)
+        sums.append(kept)
+    last = bits[-1]
+
+    def split(value, which):
+        return lax.dynamic_index_in_dim(value.reshape(chunk_blocks, stripe, part), which, 0, keepdims=False)
+
+    low, high = sums
+    full = low[0] + over_head(low[1].astype(BF16), last).astype(F32) + chunks[0][0].astype(F32)
+    full = full.astype(BF16)
+    stay_low, move_low = split(full, own), split(full, 1 - own)
+    base = high[0] + chunks[1][0].astype(F32)
+    away = high[1].astype(BF16)
+    stay_high = split(base, 1 - own) + over_head(split(away, 1 - own), last).astype(F32)
+    turned = across(split(away, own), last).astype(F32)
+    moved = over_ctx(jnp.stack([move_low, split(base, own).astype(BF16)]))
+    stay = jnp.stack([stay_low, stay_high.astype(BF16)])
+    come = jnp.stack([moved[0], (moved[1].astype(F32) + turned).astype(BF16)])
+    result = jnp.where(
+        own == 0, jnp.concatenate([stay, come], axis=1), jnp.concatenate([come, stay], axis=1)
+    )
+    return result[None]
+
+
+def body(inputs, lengths, proj_in, proj_out):
+    context_size = lax.axis_size("ctx")
+    head_size = lax.axis_size("head")
+    paired = context_size == 2 and inputs.shape[0] == 2 * context_size
+    if paired and head_size > 2 and head_size & (head_size - 1) == 0:
+        return pair_body(inputs, lengths, proj_in, proj_out)
+    return ring_body(inputs, lengths, proj_in, proj_out)
+
+
 def solution(mesh):
     return jax.shard_map(
         body,

time: 123 us -> 75.6 us (0.61)
  blocking collectives: 24.8 us -> 0 us
  waiting for transfers between devices: 57.7 us -> 34 us
  Pallas kernels: 0 us -> 14.6 us
  starting transfers between devices: 3.51 us -> 17 us
  between operations: 13.5 us -> 0.16 us
  matrix products: 7.57 us -> 0 us
  other arithmetic: 7.19 us -> 2.86 us
  local copies, waits for them, and re-layouts: 8.2 us -> 6.65 us
    ppermute x0 -> x12, waiting for transfers between devices: none -> 34 us  [the longest x8 24.7 us: over_head(): return lax.ppermute(value, 'head', [(i, i ^ bit) for i in range(head_size)])]
    all_gather x2 -> x0, waiting for transfers between devices: 32.2 us -> none  [the longest x1 28.5 us: body(): full_rows = lax.all_gather(own_rows, 'head', axis=2, tiled=True)]
    all_to_all x1 -> x0, waiting for transfers between devices: 25.4 us -> none  [body(): lax.all_to_all(proj_out, 'head', split_axis=1, concat_axis=0, tiled=True)]
    ppermute x0 -> x12, starting transfers between devices: none -> 17 us  [the longest x8 11.5 us: over_head(): return lax.ppermute(value, 'head', [(i, i ^ bit) for i in range(head_size)])]
    all_gather x2 -> x0, blocking collectives: 15.5 us -> none  [the longest x1 7.86 us: body(): lax.all_gather(key_pair[1], 'ctx', axis=0, tiled=True)]
    pallas_call x0 -> x4, Pallas kernels: none -> 14.6 us  [the longest x2 7.39 us: project(): pl.pallas_call(functools.partial(project_kernel, ids), name='project', ou...]
    all_to_all x1 -> x0, blocking collectives: 9.24 us -> none  [body(): lax.all_to_all(reordered, 'ctx', split_axis=0, concat_axis=1, tiled=True)]
    dot_general x3 -> x0, matrix products: 7.57 us -> none  [the longest x1 3.53 us: one_tile(): jnp.einsum('hqk,khd->qhd', weights, value_rows, preferred_element_type=jn...]
  transfers between devices with their start and end apart: 3 -> 12, of which waited for: 3 -> 8; matrix products, arithmetic and copies ran while one was open for 4% -> 7% of each run, Pallas kernels for 0% -> 14%
where the time goes in v1:
time: 75.6 us; the launch traced here: 75.3 us
  waiting for transfers between devices  34 us (45%)
  starting transfers between devices  17 us (22%)
  Pallas kernels  14.6 us (19%)
  local copies, waits for them, and re-layouts  6.65 us (9%)
  other arithmetic  2.86 us (4%)
    ppermute x8, waiting for transfers between devices, over_head(): return lax.ppermute(value, 'head', [(i, i ^ bit) for i in range(head_size)])  24.7 us
    ppermute x8, starting transfers between devices, over_head(): return lax.ppermute(value, 'head', [(i, i ^ bit) for i in range(head_size)])  11.5 us
    ppermute x3, waiting for transfers between devices, over_ctx(): return lax.ppermute(value, 'ctx', [(0, 1), (1, 0)])  9.3 us
    pallas_call x2, Pallas kernels, project(): pl.pallas_call(functools.partial(project_kernel, ids), name='project', ou...  7.39 us
    pallas_call x2, Pallas kernels, attend(): pl.pallas_call(functools.partial(attend_kernel, chunk, chunk_blocks, stri...  7.22 us
    unnamed x23, local copies, waits for them, and re-layouts  5.57 us
    ppermute x3, starting transfers between devices, over_ctx(): return lax.ppermute(value, 'ctx', [(0, 1), (1, 0)])  4.09 us
  transfers between devices with their start and end apart: 12, of which 8 were waited for; matrix products, arithmetic and copies ran while one was open for 7% of the time, Pallas kernels for 14%

profile of v1, /device:TPU:0, one launch (start us, length us, event | category | flops | bytes accessed | tf_op | source)
XLA Modules:
  0.0 75.3 jit_solution(13225824700048963283)
XLA Ops:
  0.0 1.0 %fusion.8 = (bf16[2,128,256]{2,1,0:T(8,128)(2,1)S(1)}, bf16[2,128,256]{2,1,0:T(8,128)(2,1)S(1)}) fusion(bf16[4,128,256]{2,1,0:T(8,128)(2,1)} %param.4), kind=kLoop, calls=%fused_computation.29 | loop fusion | bytes 524288 | tf_op jit(solution)/shard_map/slice | solution.py:217
  1.0 0.0 copy-start
  1.0 0.0 copy-start.2
  1.0 4.1 %collective-permute-start.5 = (bf16[1,256,256]{2,1,0:T(8,128)(2,1)S(1)}, bf16[1,256,256]{2,1,0:T(8,128)(2,1)S(1)}, u32[]{:S(2)}, u32[]{:S(2)}) collective-permute-start(bf16[1,256,256]{2,1,0:T(8,128)(2,1)S(1)} %bitcast.51), channel_id=1, source_target_pairs={{0,2},{1,3},{2,0},{3,1},{4,6},{5,7},{6,4},{7,5},{8,10},{9,11},{10,... | collective-permute-start | bytes 393224 | tf_op jit(solution)/shard_map/ppermute | solution.py:204
  5.1 0.1 collective-permute-start
  5.2 9.9 %collective-permute-done.5.refs_1_ = bf16[1,256,256]{2,1,0:T(8,128)(2,1)S(1)} collective-permute-done((bf16[1,256,256]{2,1,0:T(8,128)(2,1)S(1)}, bf16[1,256,256]{2,1,0:T(8,128)(2,1)S(1)}, u32[]{:S(2)}, u32[]{:S(2)}) %collective-permute-start.5) | collective-permute-done | bytes 131104 | tf_op jit(solution)/shard_map/ppermute | solution.py:204
  15.1 0.1 collective-permute-start.6
  15.2 1.9 %collective-permute-done.refs_1_ = bf16[1,256,256]{2,1,0:T(8,128)(2,1)S(1)} collective-permute-done((bf16[1,256,256]{2,1,0:T(8,128)(2,1)S(1)}, bf16[1,256,256]{2,1,0:T(8,128)(2,1)S(1)}, u32[]{:S(2)}, u32[]{:S(2)}) %collective-permute-start) | collective-permute-done | bytes 131104 | tf_op jit(solution)/shard_map/ppermute | solution.py:204
  17.2 0.7 collective-permute-start.1
  17.9 3.4 %copy.5 = bf16[128,8,4,256]{3,1,2,0:T(8,128)(2,1)} copy(bf16[128,8,4,256]{3,2,1,0:T(4,128)(2,1)} %bitcast.47) | data formatting | bytes 4194304
  21.3 0.0 copy-done
  21.3 0.0 copy-done.2
  21.3 0.0 copy-done.7
  21.3 0.0 copy-done.6
  21.3 0.6 pad_add_fusion.place
  22.0 2.4 %collective-permute-done.6.refs_2_ = bf16[2,256,256]{2,1,0:T(8,128)(2,1)S(1)} collective-permute-done((bf16[2,256,256]{2,1,0:T(8,128)(2,1)S(1)}, bf16[2,256,256]{2,1,0:T(8,128)(2,1)S(1)}, u32[]{:S(2)}, u32[]{:S(2)}) %collective-permute-start.6) | collective-permute-done | bytes 262176 | tf_op jit(solution)/shard_map/ppermute | solution.py:204
  24.4 0.7 copy-done.10
  25.1 3.7 %project.3 = (bf16[2,256,256]{2,1,0:T(8,128)(2,1)}, bf16[2,256,256]{2,1,0:T(8,128)(2,1)}) custom-call(s32[2]{0:T(128)} %pad_add_fusion.place, bf16[1,256,256]{2,1,0:T(8,128)(2,1)} %bitcast.53, bf16[1,256,256]{2,1,0:T(8,128)(2,1)} %copy-done.7, bf16[2,256,256]{2,1,0:T(8,128)(2,1)} %copy-done.10, bf16[1024,1024]{1,0:T(8,128)(2,1)} %bitcast.45), custom_call_target="tpu_custom_call" | custom-call | flops 536870912 | bytes 2097152 | tf_op jit(solution)/shard_map/project/pallas_call | solution.py:230
  28.8 1.8 %collective-permute-start.7 = (bf16[2,256,256]{2,1,0:T(8,128)(2,1)}, bf16[2,256,256]{2,1,0:T(8,128)(2,1)S(1)}, u32[]{:S(2)}, u32[]{:S(2)}) collective-permute-start(bf16[2,256,256]{2,1,0:T(8,128)(2,1)} %get-tuple-element.17.refs_2_), channel_id=1, source_target_pairs={{0,4},{4,0},{1,5},{5,1},{2,6},{6,2},{3,7},{7,3},{8,12},{12,8},{9,1... | collective-permute-start | bytes 786440 | tf_op jit(solution)/shard_map/ppermute | solution.py:207
  30.6 0.0 collective-permute-done.1.refs_2_
  30.6 0.7 copy-done.9
  31.3 3.7 %project.2 = (bf16[2,256,256]{2,1,0:T(8,128)(2,1)}, bf16[2,256,256]{2,1,0:T(8,128)(2,1)}) custom-call(s32[2]{0:T(128)} %pad_add_fusion.place, bf16[1,256,256]{2,1,0:T(8,128)(2,1)} %bitcast.50, bf16[1,256,256]{2,1,0:T(8,128)(2,1)} %copy-done.6, bf16[2,256,256]{2,1,0:T(8,128)(2,1)} %copy-done.9, bf16[1024,1024]{1,0:T(8,128)(2,1)} %bitcast.46), custom_call_target="tpu_custom_call" | custom-call | flops 536870912 | bytes 2097152 | tf_op jit(solution)/shard_map/project/pallas_call | solution.py:230
  35.0 0.2 collective-permute-start.2
  35.2 1.6 %collective-permute-done.7.refs_3_ = bf16[2,256,256]{2,1,0:T(8,128)(2,1)S(1)} collective-permute-done((bf16[2,256,256]{2,1,0:T(8,128)(2,1)}, bf16[2,256,256]{2,1,0:T(8,128)(2,1)S(1)}, u32[]{:S(2)}, u32[]{:S(2)}) %collective-permute-start.7) | collective-permute-done | bytes 262176 | tf_op jit(solution)/shard_map/ppermute | solution.py:207
  36.8 4.8 %collective-permute-done.2.refs_1_ = bf16[2,256,256]{2,1,0:T(8,128)(2,1)S(1)} collective-permute-done((bf16[2,256,256]{2,1,0:T(8,128)(2,1)}, bf16[2,256,256]{2,1,0:T(8,128)(2,1)S(1)}, u32[]{:S(2)}, u32[]{:S(2)}) %collective-permute-start.2) | collective-permute-done | bytes 262176 | tf_op jit(solution)/shard_map/ppermute | solution.py:207
  41.6 0.0 copy-done.8
  41.6 0.7 copy-done.3
  42.3 3.9 %attend.3 = (bf16[2,256,256]{2,1,0:T(8,128)(2,1)}, f32[2,256,256]{2,1,0:T(8,128)}) custom-call(s32[2]{0:T(128)} %pad_add_fusion.place, s32[4]{0:T(128)} %lengths.3, bf16[2,256,256]{2,1,0:T(8,128)(2,1)} %get-tuple-element.13.refs_0_, bf16[2,256,256]{2,1,0:T(8,128)(2,1)} %copy-done.3, bf16[2,256,256]{2,1,0:T(8,128)(2,1)} %get-tuple-element.17.refs_2_, ...), custom_call_target="tpu_custom_call" | custom-call | flops 402653184 | bytes 524288 | tf_op jit(solution)/shard_map/attend/pallas_call | solution.py:248
  46.2 0.0 collective-permute-start.8
  46.2 3.3 %attend.2 = (bf16[2,256,256]{2,1,0:T(8,128)(2,1)}, f32[2,256,256]{2,1,0:T(8,128)}) custom-call(s32[2]{0:T(128)} %pad_add_fusion.place, s32[4]{0:T(128)} %lengths.3, bf16[2,256,256]{2,1,0:T(8,128)(2,1)} %get-tuple-element.13.refs_0_, bf16[2,256,256]{2,1,0:T(8,128)(2,1)} %copy-done.3, bf16[2,256,256]{2,1,0:T(8,128)(2,1)} %get-tuple-element.14.refs_2_, ...), custom_call_target="tpu_custom_call" | custom-call | flops 268435456 | bytes 524288 | tf_op jit(solution)/shard_map/attend/pallas_call | solution.py:248
  49.5 2.0 %collective-permute-start.3 = (bf16[2,256,256]{2,1,0:T(8,128)(2,1)}, bf16[2,256,256]{2,1,0:T(8,128)(2,1)S(1)}, u32[]{:S(2)}, u32[]{:S(2)}) collective-permute-start(bf16[2,256,256]{2,1,0:T(8,128)(2,1)} %get-tuple-element.16), channel_id=1, source_target_pairs={{0,1},{1,0},{2,3},{3,2},{4,5},{5,4},{6,7},{7,6},{8,9},{9,8},{10,11... | collective-permute-start | bytes 786440 | tf_op jit(solution)/shard_map/ppermute | solution.py:204
  51.5 4.1 %collective-permute-done.8 = bf16[2,256,256]{2,1,0:T(8,128)(2,1)S(1)} collective-permute-done((bf16[2,256,256]{2,1,0:T(8,128)(2,1)}, bf16[2,256,256]{2,1,0:T(8,128)(2,1)S(1)}, u32[]{:S(2)}, u32[]{:S(2)}) %collective-permute-start.8) | collective-permute-done | bytes 262176 | tf_op jit(solution)/shard_map/ppermute | solution.py:204
  55.6 1.1 %convert_add_fusion = f32[2,256,256]{2,1,0:T(8,128)S(1)} fusion(f32[2,256,256]{2,1,0:T(8,128)} %get-tuple-element.19, bf16[2,256,256]{2,1,0:T(8,128)(2,1)S(1)} %collective-permute-done.8), kind=kLoop, calls=%fused_computation | loop fusion | flops 262144 | bytes 1310720 | tf_op jit(solution)/shard_map/add | solution.py:270
  56.8 1.8 %collective-permute-start.9 = (bf16[128,256]{1,0:T(8,128)(2,1)S(1)}, bf16[128,256]{1,0:T(8,128)(2,1)S(1)}, u32[]{:S(2)}, u32[]{:S(2)}) collective-permute-start(bf16[128,256]{1,0:T(8,128)(2,1)S(1)} %get-tuple-element.25), channel_id=1, source_target_pairs={{0,2},{1,3},{2,0},{3,1},{4,6},{5,7},{6,4},{7,5},{8,10},{9,11},{10,... | collective-permute-start | bytes 196616 | tf_op jit(solution)/shard_map/ppermute | solution.py:204
  58.6 1.4 %collective-permute-start.11 = (bf16[128,256]{1,0:T(8,128)(2,1)S(1)}, bf16[128,256]{1,0:T(8,128)(2,1)S(1)}, u32[]{:S(2)}, u32[]{:S(2)}) collective-permute-start(bf16[128,256]{1,0:T(8,128)(2,1)S(1)} %get-tuple-element.26), channel_id=1, source_target_pairs={{0,6},{1,7},{2,4},{3,5},{4,2},{5,3},{6,0},{7,1},{8,14},{9,15},{10,... | collective-permute-start | bytes 196616 | tf_op jit(solution)/shard_map/ppermute | solution.py:215
  60.0 0.0 collective-permute-done.3
  60.0 0.0 copy-done.5
  60.0 0.1 convert_add_fusion.1
  60.1 2.8 %collective-permute-start.4 = (bf16[256,256]{1,0:T(8,128)(2,1)S(1)}, bf16[256,256]{1,0:T(8,128)(2,1)S(1)}, u32[]{:S(2)}, u32[]{:S(2)}) collective-permute-start(bf16[256,256]{1,0:T(8,128)(2,1)S(1)} %fusion.3), channel_id=1, source_target_pairs={{0,2},{1,3},{2,0},{3,1},{4,6},{5,7},{6,4},{7,5},{8,10},{9,11},{10,... | collective-permute-start | bytes 393224 | tf_op jit(solution)/shard_map/ppermute | solution.py:204
  62.9 0.0 copy-done.4
  62.9 6.3 %collective-permute-done.4 = bf16[256,256]{1,0:T(8,128)(2,1)S(1)} collective-permute-done((bf16[256,256]{1,0:T(8,128)(2,1)S(1)}, bf16[256,256]{1,0:T(8,128)(2,1)S(1)}, u32[]{:S(2)}, u32[]{:S(2)}) %collective-permute-start.4) | collective-permute-done | bytes 131104 | tf_op jit(solution)/shard_map/ppermute | solution.py:204
  69.3 0.0 copy-done.1
  69.3 0.1 fusion.2
  69.4 2.1 %collective-permute-start.10 = (bf16[2,128,256]{2,1,0:T(8,128)(2,1)S(1)}, bf16[2,128,256]{2,1,0:T(8,128)(2,1)S(1)}, u32[]{:S(2)}, u32[]{:S(2)}) collective-permute-start(bf16[2,128,256]{2,1,0:T(8,128)(2,1)S(1)} %pad_maximum_fusion.2), channel_id=1, source_target_pairs={{0,4},{4,0},{1,5},{5,1},{2,6},{6,2},{3,7},{7,3},{8,12},{12,8},{9,1... | collective-permute-start | bytes 393224 | tf_op jit(solution)/shard_map/ppermute | solution.py:207
  71.5 0.0 collective-permute-done.9
  71.5 2.9 %collective-permute-done.10 = bf16[2,128,256]{2,1,0:T(8,128)(2,1)S(1)} collective-permute-done((bf16[2,128,256]{2,1,0:T(8,128)(2,1)S(1)}, bf16[2,128,256]{2,1,0:T(8,128)(2,1)S(1)}, u32[]{:S(2)}, u32[]{:S(2)}) %collective-permute-start.10) | collective-permute-done | bytes 131104 | tf_op jit(solution)/shard_map/ppermute | solution.py:207
  74.4 0.0 collective-permute-done.11
  74.5 0.8 %maximum_select_fusion = bf16[1,2,256,256]{3,2,1,0:T(8,128)(2,1)} fusion(bf16[1,2,128,256]{3,2,1,0:T(8,128)(2,1)S(1)} %maximum_bitcast_fusion.1, bf16[1,2,128,256]{3,2,1,0:T(8,128)(2,1)S(1)} %maximum_bitcast_fusion, pred[]{:T(512)S(6)} %eq.3), kind=kLoop, calls=%fused_computation.10 | loop fusion | flops 1179648 | bytes 524289 | tf_op jit(solution)/shard_map/jit(_where)/select_n | solution.py:290
  (23 shorter events, 0.3 us)
Async XLA Ops:
  1.0 20.3 %copy-start = (bf16[2,128,256]{2,1,0:T(8,128)(2,1)}, bf16[2,128,256]{2,1,0:T(8,128)(2,1)S(1)}, u32[]{:S(2)}) copy-start(bf16[2,128,256]{2,1,0:T(8,128)(2,1)S(1)} %get-tuple-element.22) | copy-start | bytes 393220
  1.0 20.3 %copy-start.2 = (bf16[2,128,256]{2,1,0:T(8,128)(2,1)}, bf16[2,128,256]{2,1,0:T(8,128)(2,1)S(1)}, u32[]{:S(2)}) copy-start(bf16[2,128,256]{2,1,0:T(8,128)(2,1)S(1)} %get-tuple-element.21) | copy-start | bytes 393220
  1.0 14.1 %collective-permute-start.5 = (bf16[1,256,256]{2,1,0:T(8,128)(2,1)S(1)}, bf16[1,256,256]{2,1,0:T(8,128)(2,1)S(1)}, u32[]{:S(2)}, u32[]{:S(2)}) collective-permute-start(bf16[1,256,256]{2,1,0:T(8,128)(2,1)S(1)} %bitcast.51), channel_id=1, source_target_pairs={{0,2},{1,3},{2,0},{3,1},{4,6},{5,7},{6,4},{7,5},{8,10},{9,11},{10,... | collective-permute-start | bytes 393224 | tf_op jit(solution)/shard_map/ppermute | solution.py:204
  5.1 12.0 %collective-permute-start = (bf16[1,256,256]{2,1,0:T(8,128)(2,1)S(1)}, bf16[1,256,256]{2,1,0:T(8,128)(2,1)S(1)}, u32[]{:S(2)}, u32[]{:S(2)}) collective-permute-start(bf16[1,256,256]{2,1,0:T(8,128)(2,1)S(1)} %bitcast.48), channel_id=1, source_target_pairs={{0,2},{1,3},{2,0},{3,1},{4,6},{5,7},{6,4},{7,5},{8,10},{9,11},{10,... | collective-permute-start | bytes 393224 | tf_op jit(solution)/shard_map/ppermute | solution.py:204
  15.1 6.2 %copy-start.7 = (bf16[1,256,256]{2,1,0:T(8,128)(2,1)}, bf16[1,256,256]{2,1,0:T(8,128)(2,1)S(1)}, u32[]{:S(2)}) copy-start(bf16[1,256,256]{2,1,0:T(8,128)(2,1)S(1)} %collective-permute-done.5.refs_1_) | copy-start | bytes 393220
  15.1 9.2 %collective-permute-start.6 = (bf16[2,256,256]{2,1,0:T(8,128)(2,1)S(1)}, bf16[2,256,256]{2,1,0:T(8,128)(2,1)S(1)}, u32[]{:S(2)}, u32[]{:S(2)}) collective-permute-start(bf16[2,256,256]{2,1,0:T(8,128)(2,1)S(1)} %pad_maximum_fusion.1), channel_id=1, source_target_pairs={{0,1},{1,0},{2,3},{3,2},{4,5},{5,4},{6,7},{7,6},{8,9},{9,8},{10,11... | collective-permute-start | bytes 786440 | tf_op jit(solution)/shard_map/ppermute | solution.py:204
  17.2 4.2 %copy-start.6 = (bf16[1,256,256]{2,1,0:T(8,128)(2,1)}, bf16[1,256,256]{2,1,0:T(8,128)(2,1)S(1)}, u32[]{:S(2)}) copy-start(bf16[1,256,256]{2,1,0:T(8,128)(2,1)S(1)} %collective-permute-done.refs_1_) | copy-start | bytes 393220
  17.2 13.4 %collective-permute-start.1 = (bf16[2,256,256]{2,1,0:T(8,128)(2,1)S(1)}, bf16[2,256,256]{2,1,0:T(8,128)(2,1)S(1)}, u32[]{:S(2)}, u32[]{:S(2)}) collective-permute-start(bf16[2,256,256]{2,1,0:T(8,128)(2,1)S(1)} %pad_maximum_fusion), channel_id=1, source_target_pairs={{0,1},{1,0},{2,3},{3,2},{4,5},{5,4},{6,7},{7,6},{8,9},{9,8},{10,11... | collective-permute-start | bytes 786440 | tf_op jit(solution)/shard_map/ppermute | solution.py:204
  24.4 0.7 copy-start.10
  28.8 8.0 %collective-permute-start.7 = (bf16[2,256,256]{2,1,0:T(8,128)(2,1)}, bf16[2,256,256]{2,1,0:T(8,128)(2,1)S(1)}, u32[]{:S(2)}, u32[]{:S(2)}) collective-permute-start(bf16[2,256,256]{2,1,0:T(8,128)(2,1)} %get-tuple-element.17.refs_2_), channel_id=1, source_target_pairs={{0,4},{4,0},{1,5},{5,1},{2,6},{6,2},{3,7},{7,3},{8,12},{12,8},{9,1... | collective-permute-start | bytes 786440 | tf_op jit(solution)/shard_map/ppermute | solution.py:207
  30.6 0.7 copy-start.9
  35.0 6.6 %collective-permute-start.2 = (bf16[2,256,256]{2,1,0:T(8,128)(2,1)}, bf16[2,256,256]{2,1,0:T(8,128)(2,1)S(1)}, u32[]{:S(2)}, u32[]{:S(2)}) collective-permute-start(bf16[2,256,256]{2,1,0:T(8,128)(2,1)} %get-tuple-element.13.refs_0_), channel_id=1, source_target_pairs={{0,4},{4,0},{1,5},{5,1},{2,6},{6,2},{3,7},{7,3},{8,12},{12,8},{9,1... | collective-permute-start | bytes 786440 | tf_op jit(solution)/shard_map/ppermute | solution.py:207
  36.8 4.8 %copy-start.8 = (bf16[2,256,256]{2,1,0:T(8,128)(2,1)}, bf16[2,256,256]{2,1,0:T(8,128)(2,1)S(1)}, u32[]{:S(2)}) copy-start(bf16[2,256,256]{2,1,0:T(8,128)(2,1)S(1)} %collective-permute-done.7.refs_3_) | copy-start | bytes 786436
  41.6 0.7 copy-start.3
  46.2 9.4 %collective-permute-start.8 = (bf16[2,256,256]{2,1,0:T(8,128)(2,1)}, bf16[2,256,256]{2,1,0:T(8,128)(2,1)S(1)}, u32[]{:S(2)}, u32[]{:S(2)}) collective-permute-start(bf16[2,256,256]{2,1,0:T(8,128)(2,1)} %get-tuple-element.20), channel_id=1, source_target_pairs={{0,1},{1,0},{2,3},{3,2},{4,5},{5,4},{6,7},{7,6},{8,9},{9,8},{10,11... | collective-permute-start | bytes 786440 | tf_op jit(solution)/shard_map/ppermute | solution.py:204
  49.5 10.5 %copy-start.5 = (f32[2,256,256]{2,1,0:T(8,128)S(1)}, f32[2,256,256]{2,1,0:T(8,128)}, u32[]{:S(2)}) copy-start(f32[2,256,256]{2,1,0:T(8,128)} %get-tuple-element.15) | copy-start | bytes 1572868
  49.5 13.4 %copy-start.4 = (bf16[4,128,256]{2,1,0:T(8,128)(2,1)S(1)}, bf16[4,128,256]{2,1,0:T(8,128)(2,1)}, u32[]{:S(2)}) copy-start(bf16[4,128,256]{2,1,0:T(8,128)(2,1)} %param.4) | copy-start | bytes 786436
  49.5 10.5 %collective-permute-start.3 = (bf16[2,256,256]{2,1,0:T(8,128)(2,1)}, bf16[2,256,256]{2,1,0:T(8,128)(2,1)S(1)}, u32[]{:S(2)}, u32[]{:S(2)}) collective-permute-start(bf16[2,256,256]{2,1,0:T(8,128)(2,1)} %get-tuple-element.16), channel_id=1, source_target_pairs={{0,1},{1,0},{2,3},{3,2},{4,5},{5,4},{6,7},{7,6},{8,9},{9,8},{10,11... | collective-permute-start | bytes 786440 | tf_op jit(solution)/shard_map/ppermute | solution.py:204
  55.6 13.6 %copy-start.1 = (bf16[2,128,256]{2,1,0:T(8,128)(2,1)S(1)}, bf16[2,128,256]{2,1,0:T(8,128)(2,1)}, u32[]{:S(2)}) copy-start(bf16[2,128,256]{2,1,0:T(8,128)(2,1)} %copy-done) | copy-start | bytes 393220
  56.8 14.6 %collective-permute-start.9 = (bf16[128,256]{1,0:T(8,128)(2,1)S(1)}, bf16[128,256]{1,0:T(8,128)(2,1)S(1)}, u32[]{:S(2)}, u32[]{:S(2)}) collective-permute-start(bf16[128,256]{1,0:T(8,128)(2,1)S(1)} %get-tuple-element.25), channel_id=1, source_target_pairs={{0,2},{1,3},{2,0},{3,1},{4,6},{5,7},{6,4},{7,5},{8,10},{9,11},{10,... | collective-permute-start | bytes 196616 | tf_op jit(solution)/shard_map/ppermute | solution.py:204
  58.6 15.8 %collective-permute-start.11 = (bf16[128,256]{1,0:T(8,128)(2,1)S(1)}, bf16[128,256]{1,0:T(8,128)(2,1)S(1)}, u32[]{:S(2)}, u32[]{:S(2)}) collective-permute-start(bf16[128,256]{1,0:T(8,128)(2,1)S(1)} %get-tuple-element.26), channel_id=1, source_target_pairs={{0,6},{1,7},{2,4},{3,5},{4,2},{5,3},{6,0},{7,1},{8,14},{9,15},{10,... | collective-permute-start | bytes 196616 | tf_op jit(solution)/shard_map/ppermute | solution.py:215
  60.1 9.1 %collective-permute-start.4 = (bf16[256,256]{1,0:T(8,128)(2,1)S(1)}, bf16[256,256]{1,0:T(8,128)(2,1)S(1)}, u32[]{:S(2)}, u32[]{:S(2)}) collective-permute-start(bf16[256,256]{1,0:T(8,128)(2,1)S(1)} %fusion.3), channel_id=1, source_target_pairs={{0,2},{1,3},{2,0},{3,1},{4,6},{5,7},{6,4},{7,5},{8,10},{9,11},{10,... | collective-permute-start | bytes 393224 | tf_op jit(solution)/shard_map/ppermute | solution.py:204
  69.4 5.0 %collective-permute-start.10 = (bf16[2,128,256]{2,1,0:T(8,128)(2,1)S(1)}, bf16[2,128,256]{2,1,0:T(8,128)(2,1)S(1)}, u32[]{:S(2)}, u32[]{:S(2)}) collective-permute-start(bf16[2,128,256]{2,1,0:T(8,128)(2,1)S(1)} %pad_maximum_fusion.2), channel_id=1, source_target_pairs={{0,4},{4,0},{1,5},{5,1},{2,6},{6,2},{3,7},{7,3},{8,12},{12,8},{9,1... | collective-permute-start | bytes 393224 | tf_op jit(solution)/shard_map/ppermute | solution.py:207

commit v2 on v0

--- a/solution.py
+++ b/solution.py
@@ -1,11 +1,18 @@
+import functools
 import math
 
 import jax
 import jax.numpy as jnp
 from jax import lax
+from jax.experimental import pallas as pl
+from jax.experimental.pallas import tpu as pltpu
 from jax.sharding import PartitionSpec as P
 
+
 HDIM = 128
+GRANT = 16 << 20
+F32 = jnp.float32
+BF16 = jnp.bfloat16
 
 
 def layer_norm(values, epsilon):
@@ -18,7 +25,7 @@
     return jax.nn.silu(values).astype(jnp.bfloat16)
 
 
-def body(inputs, lengths, proj_in, proj_out):
+def ring_body(inputs, lengths, proj_in, proj_out):
     context_size = lax.axis_size("ctx")
     own_index = lax.axis_index("ctx")
     block_total, stripe, width_part = inputs.shape
@@ -103,6 +110,224 @@
     return result.reshape(1, 2, block_len, -1)
 
 
+def half_silu(half):
+    return half + half * jnp.tanh(half)
+
+
+def project_kernel(place, own, near, far, mid, relay, weight, keyval, gateq):
+    pieces = [own[0].astype(F32), near[0].astype(F32), far[0].astype(F32)]
+    pieces.append(mid[0].astype(F32) + relay[0].astype(F32))
+    part = pieces[0].shape[1]
+    width = part * len(pieces)
+    mean = sum(jnp.sum(p, axis=1, keepdims=True) for p in pieces) / width
+    pieces = [p - mean for p in pieces]
+    spread = sum(jnp.sum(p * p, axis=1, keepdims=True) for p in pieces) / width
+    rscale = lax.rsqrt(spread + 1e-06)
+    acc = None
+    for share_id, piece in enumerate(pieces):
+        lead = pl.multiple_of((place[1] ^ share_id) * part, part)
+        term = jnp.dot(
+            (piece * rscale).astype(BF16), weight[pl.ds(lead, part), :], preferred_element_type=F32
+        )
+        acc = term if acc is None else acc + term
+    done = half_silu(acc * 0.5).astype(BF16)
+    group = done.shape[1] // 4
+    gateq[0] = done[:, :group]
+    keyval[0] = done[:, group : 2 * group]
+    gateq[1] = done[:, 2 * group : 3 * group]
+    keyval[1] = done[:, 3 * group :]
+
+
+def weighted_values(plan, place, lengths, gateq, keyvals, first=None):
+    chunk, chunk_blocks, stripe, origins = plan
+    rows, cols = gateq.shape[1:]
+    block_len = 2 * stripe
+
+    def positions(shape, dim, which, side):
+        offset = lax.broadcasted_iota(jnp.int32, shape, dim)
+        block, inner = offset // stripe, offset % stripe
+        return (which * chunk_blocks + block) * block_len + side * stripe + inner
+
+    query_pos = positions((rows, 1), 0, chunk, place[0])
+    start = jnp.zeros((rows, 1), jnp.int32)
+    end = jnp.int32(0)
+    for user in range(lengths.shape[0]):
+        end = end + lengths[user]
+        start = jnp.where(query_pos >= end, end, start)
+    masks = []
+    for which, side in origins:
+        key_pos = positions((1, rows), 1, which, place[0] ^ side)
+        masks.append((key_pos <= query_pos) & (key_pos >= start))
+    scale = 0.5 / math.sqrt(HDIM)
+    totals = []
+    for head in range(cols // HDIM):
+        lanes = slice(head * HDIM, (head + 1) * HDIM)
+        query = gateq[1, :, lanes]
+        total = None if first is None else first[:, lanes]
+        for mask, ref in zip(masks, keyvals):
+            scores = lax.dot_general(
+                query, ref[1, :, lanes], (((1,), (1,)), ((), ())), preferred_element_type=F32
+            )
+            weights = jnp.where(mask, half_silu(scores * scale), 0.0).astype(BF16)
+            term = jnp.dot(weights, ref[0, :, lanes], preferred_element_type=F32)
+            total = term if total is None else total + term
+        totals.append(total)
+    return totals
+
+
+def near_kernel(plan, place, lengths, *refs):
+    *keyvals, gateq, partial = refs
+    totals = weighted_values(plan, place, lengths, gateq, keyvals)
+    for head, total in enumerate(totals):
+        partial[:, head * HDIM : (head + 1) * HDIM] = total
+
+
+def attend_kernel(plan, splits, place, lengths, keyval, partial, gateq, weight, share, *refs):
+    *outputs, held = refs
+    chunk, _, stripe, _ = plan
+    part = share.shape[2]
+    totals = weighted_values(plan, place, lengths, gateq, [keyval], partial)
+    for head, total in enumerate(totals):
+        lanes = slice(head * HDIM, (head + 1) * HDIM)
+        total = total - jnp.mean(total, axis=1, keepdims=True)
+        spread = jnp.mean(total * total, axis=1, keepdims=True)
+        total = total * lax.rsqrt(spread + 1e-05)
+        held[:, lanes] = (total * gateq[0, :, lanes].astype(F32)).astype(BF16)
+    away = place[0] if chunk == 1 else 1 - place[0]
+    leads = [pl.multiple_of(away * stripe, stripe), pl.multiple_of((1 - away) * stripe, stripe)]
+    gated = [held[pl.ds(lead, stripe), :] for lead in leads]
+    shares = [share[0, pl.ds(lead, stripe), :] for lead in leads]
+    if splits == 1:
+        gated, shares = [jnp.concatenate(gated, axis=0)], [jnp.concatenate(shares, axis=0)]
+    for index in range(splits):
+        sent, kept = outputs[2 * index : 2 * index + 2]
+        for share_id in (1, 3, 2, 0):
+            lead = pl.multiple_of((place[1] ^ share_id) * part, part)
+            product = jnp.dot(
+                gated[index], weight[:, pl.ds(lead, part)], preferred_element_type=F32
+            )
+            if share_id == 0:
+                product = product + shares[index].astype(F32)
+            target = sent if share_id & 1 else kept
+            target[share_id >> 1] = product.astype(target.dtype)
+
+
+def whole(memory_space=pltpu.VMEM):
+    return pl.BlockSpec(memory_space=memory_space)
+
+
+def pair_body(inputs, lengths, proj_in, proj_out):
+    head_size = lax.axis_size("head")
+    own = lax.axis_index("ctx")
+    block_total, stripe, part = inputs.shape
+    chunk_blocks = block_total // 2
+    rows = chunk_blocks * stripe
+    cols = proj_in.shape[2]
+    place = jnp.stack([own, lax.axis_index("head")]).astype(jnp.int32)
+    weight_in = proj_in.reshape(proj_in.shape[0], -1)
+
+    def over_head(value, pairs):
+        if isinstance(pairs, int):
+            pairs = [(i, i ^ pairs) for i in range(head_size)]
+        return lax.ppermute(value, "head", pairs)
+
+    def over_ctx(value):
+        return lax.ppermute(value, "ctx", [(0, 1), (1, 0)])
+
+    def kernel_call(function, outs, args, scalars, cost, scratch=()):
+        return pl.pallas_call(
+            function,
+            compiler_params=pltpu.CompilerParams(vmem_limit_bytes=GRANT),
+            out_shape=tuple(jax.ShapeDtypeStruct(*out) for out in outs),
+            in_specs=[whole(pltpu.SMEM)] * scalars + [whole()] * (len(args) - scalars),
+            out_specs=tuple(whole() for _ in outs),
+            scratch_shapes=scratch,
+            cost_estimate=cost,
+        )(*args)
+
+    def cost(flops, transcendentals):
+        return pl.CostEstimate(flops=flops, bytes_accessed=1 << 20, transcendentals=transcendentals)
+
+    inner = [(1, 2), (2, 1)]
+    outer = [(1, 0), (2, 3)]
+
+    def gather(own_share):
+        far = over_head(own_share, 2)
+        near = over_head(own_share, 1)
+        mid = over_head(own_share, inner)
+        relay = over_head(far, outer)
+        return own_share, near, far, mid, relay
+
+    def project(shares):
+        size = ((2, rows, cols), BF16)
+        return kernel_call(
+            project_kernel,
+            (size, size),
+            (place, *shares, weight_in),
+            1,
+            cost(2 * rows * weight_in.size, rows * 4 * cols),
+        )
+
+    def near_part(chunk, origins, keyvals, gateq):
+        count = len(keyvals)
+        return kernel_call(
+            functools.partial(near_kernel, (chunk, chunk_blocks, stripe, origins)),
+            (((rows, cols), F32),),
+            (place, lengths, *keyvals, gateq),
+            2,
+            cost(4 * rows * rows * cols * count, rows * rows * count * (cols // HDIM)),
+        )[0]
+
+    def attend(chunk, keyval, partial, gateq, share, splits):
+        size = (2, rows // splits, part)
+        return kernel_call(
+            functools.partial(
+                attend_kernel, (chunk, chunk_blocks, stripe, [(chunk, 1)]), splits
+            ),
+            ((size, BF16), (size, F32)) * splits,
+            (place, lengths, keyval, partial, gateq, proj_out, share),
+            2,
+            cost(4 * rows * rows * cols + 2 * rows * proj_out.size, rows * rows * (cols // HDIM)),
+            [pltpu.VMEM((rows, cols), BF16)],
+        )
+
+    def total(sent, kept):
+        kept = kept + over_head(sent, 1).astype(F32)
+        far = over_head(kept[1].astype(BF16), 2)
+        return (kept[0] + far.astype(F32)).astype(BF16)
+
+    chunks = [inputs[:chunk_blocks].reshape(1, rows, part), inputs[chunk_blocks:].reshape(1, rows, part)]
+    low = gather(chunks[0])
+    low_keyval, low_gateq = project(low)
+    low_other = over_ctx(low_keyval)
+    high = gather(chunks[1])
+    high_keyval, high_gateq = project(high)
+    high_other = over_ctx(high_keyval)
+    low_first = near_part(0, [(0, 0)], [low_keyval], low_gateq)
+    sent, kept = attend(0, low_other, low_first, low_gateq, chunks[0], 1)
+    low_done = total(sent, kept)
+    origins = [(0, 0), (0, 1), (1, 0)]
+    high_first = near_part(1, origins, [low_keyval, low_other, high_keyval], high_gateq)
+    sent, kept, sent_stay, kept_stay = attend(1, high_other, high_first, high_gateq, chunks[1], 2)
+    high_move = total(sent, kept)
+    high_stay = total(sent_stay, kept_stay)
+    come = over_ctx(jnp.stack([low_done[:stripe], high_move]))
+    stay = jnp.stack([low_done[stripe:], high_stay])
+    result = jnp.where(
+        own == 0, jnp.concatenate([stay, come], axis=1), jnp.concatenate([come, stay], axis=1)
+    )
+    return result[None]
+
+
+def body(inputs, lengths, proj_in, proj_out):
+    context_size = lax.axis_size("ctx")
+    head_size = lax.axis_size("head")
+    paired = context_size == 2 and inputs.shape[0] == 2 * context_size
+    if paired and head_size == 4:
+        return pair_body(inputs, lengths, proj_in, proj_out)
+    return ring_body(inputs, lengths, proj_in, proj_out)
+
+
 def solution(mesh):
     return jax.shard_map(
         body,

time: 123 us -> 71.4 us (0.58)
  waiting for transfers between devices: 57.7 us -> 29.6 us
  blocking collectives: 24.8 us -> 0 us
  starting transfers between devices: 3.51 us -> 28.1 us
  between operations: 13.5 us -> 0.22 us
  Pallas kernels: 0 us -> 9.08 us
  matrix products: 7.57 us -> 0 us
  other arithmetic: 7.19 us -> 1.09 us
  local copies, waits for them, and re-layouts: 8.2 us -> 3.13 us
    all_gather x2 -> x0, waiting for transfers between devices: 32.2 us -> none  [the longest x1 28.5 us: body(): full_rows = lax.all_gather(own_rows, 'head', axis=2, tiled=True)]
    ppermute x0 -> x17, waiting for transfers between devices: none -> 29.6 us  [the longest x14 21.9 us: over_head(): return lax.ppermute(value, 'head', pairs)]
    ppermute x0 -> x17, starting transfers between devices: none -> 28.1 us  [the longest x14 23.3 us: over_head(): return lax.ppermute(value, 'head', pairs)]
    all_to_all x1 -> x0, waiting for transfers between devices: 25.4 us -> none  [body(): lax.all_to_all(proj_out, 'head', split_axis=1, concat_axis=0, tiled=True)]
    all_gather x2 -> x0, blocking collectives: 15.5 us -> none  [the longest x1 7.86 us: body(): lax.all_gather(key_pair[1], 'ctx', axis=0, tiled=True)]
    all_to_all x1 -> x0, blocking collectives: 9.24 us -> none  [body(): lax.all_to_all(reordered, 'ctx', split_axis=0, concat_axis=1, tiled=True)]
    pallas_call x0 -> x6, Pallas kernels: none -> 9.08 us  [kernel_call(): pl.pallas_call(function, compiler_params=pltpu.CompilerParams(vmem_limit_...]
    dot_general x3 -> x0, matrix products: 7.57 us -> none  [the longest x1 3.53 us: one_tile(): jnp.einsum('hqk,khd->qhd', weights, value_rows, preferred_element_type=jn...]
  transfers between devices with their start and end apart: 3 -> 17, of which waited for: 3 -> 9; matrix products, arithmetic and copies ran while one was open for 4% -> 3% of each run, Pallas kernels for 0% -> 11%
where the time goes in v2:
time: 71.4 us; the launch traced here: 71.2 us
  waiting for transfers between devices  29.6 us (41%)
  starting transfers between devices  28.1 us (39%)
  Pallas kernels  9.08 us (13%)
  local copies, waits for them, and re-layouts  3.13 us (4%)
  other arithmetic  1.09 us (2%)
    ppermute x14, starting transfers between devices, over_head(): return lax.ppermute(value, 'head', pairs)  23.3 us
    ppermute x14, waiting for transfers between devices, over_head(): return lax.ppermute(value, 'head', pairs)  21.9 us
    pallas_call x6, Pallas kernels, kernel_call(): pl.pallas_call(function, compiler_params=pltpu.CompilerParams(vmem_limit_...  9.08 us
    ppermute x3, waiting for transfers between devices, over_ctx(): return lax.ppermute(value, 'ctx', [(0, 1), (1, 0)])  7.68 us
    ppermute x3, starting transfers between devices, over_ctx(): return lax.ppermute(value, 'ctx', [(0, 1), (1, 0)])  4.75 us
    unnamed x5, local copies, waits for them, and re-layouts  2.1 us
  transfers between devices with their start and end apart: 17, of which 9 were waited for; matrix products, arithmetic and copies ran while one was open for 3% of the time, Pallas kernels for 11%

profile of v2, /device:TPU:0, one launch (start us, length us, event | category | flops | bytes accessed | tf_op | source)
XLA Modules:
  0.0 71.2 jit_solution(17730870773519181820)
XLA Ops:
  0.0 1.0 %fusion.11 = (bf16[2,128,256]{2,1,0:T(8,128)(2,1)S(1)}, bf16[2,128,256]{2,1,0:T(8,128)(2,1)S(1)}) fusion(bf16[4,128,256]{2,1,0:T(8,128)(2,1)} %param.4), kind=kLoop, calls=%fused_computation.26 | loop fusion | bytes 524288 | tf_op jit(solution)/shard_map/slice | solution.py:299
  1.0 4.1 %collective-permute-start.1 = (bf16[1,256,256]{2,1,0:T(8,128)(2,1)S(1)}, bf16[1,256,256]{2,1,0:T(8,128)(2,1)S(1)}, u32[]{:S(2)}, u32[]{:S(2)}) collective-permute-start(bf16[1,256,256]{2,1,0:T(8,128)(2,1)S(1)} %bitcast.47), channel_id=1, source_target_pairs={{0,2},{1,3},{2,0},{3,1},{4,6},{5,7},{6,4},{7,5},{8,10},{9,11},{10,... | collective-permute-start | bytes 393224 | tf_op jit(solution)/shard_map/ppermute | solution.py:232
  5.1 0.1 collective-permute-start.8
  5.2 0.7 collective-permute-start.2
  5.9 4.7 %collective-permute-start = (bf16[1,256,256]{2,1,0:T(8,128)(2,1)S(1)}, bf16[1,256,256]{2,1,0:T(8,128)(2,1)S(1)}, u32[]{:S(2)}, u32[]{:S(2)}) collective-permute-start(bf16[1,256,256]{2,1,0:T(8,128)(2,1)S(1)} %bitcast.49), channel_id=1, source_target_pairs={{0,1},{1,0},{2,3},{3,2},{4,5},{5,4},{6,7},{7,6},{8,9},{9,8},{10,11... | collective-permute-start | bytes 393224 | tf_op jit(solution)/shard_map/ppermute | solution.py:232
  10.6 4.6 %collective-permute-done.1.far = bf16[1,256,256]{2,1,0:T(8,128)(2,1)S(1)} collective-permute-done((bf16[1,256,256]{2,1,0:T(8,128)(2,1)S(1)}, bf16[1,256,256]{2,1,0:T(8,128)(2,1)S(1)}, u32[]{:S(2)}, u32[]{:S(2)}) %collective-permute-start.1) | collective-permute-done | bytes 131104 | tf_op jit(solution)/shard_map/ppermute | solution.py:232
  15.2 1.3 %collective-permute-start.3 = (bf16[1,256,256]{2,1,0:T(8,128)(2,1)S(1)}, bf16[1,256,256]{2,1,0:T(8,128)(2,1)S(1)}, u32[]{:S(2)}, u32[]{:S(2)}) collective-permute-start(bf16[1,256,256]{2,1,0:T(8,128)(2,1)S(1)} %collective-permute-done.1.far), channel_id=1, source_target_pairs={{1,0},{2,3},{5,4},{6,7},{9,8},{10,11},{13,12},{14,15},{17,16},{18,... | collective-permute-start | bytes 393224 | tf_op jit(solution)/shard_map/ppermute | solution.py:232
  16.5 0.7 collective-permute-start.9
  17.2 2.1 %copy.5 = bf16[128,8,4,256]{3,1,2,0:T(8,128)(2,1)S(1)} copy(bf16[128,8,4,256]{3,2,1,0:T(4,128)(2,1)} %bitcast.57) | data formatting | bytes 4194304
  19.2 0.0 collective-permute-done.8.far
  19.3 5.7 %collective-permute-start.7 = (bf16[1,256,256]{2,1,0:T(8,128)(2,1)S(1)}, bf16[1,256,256]{2,1,0:T(8,128)(2,1)S(1)}, u32[]{:S(2)}, u32[]{:S(2)}) collective-permute-start(bf16[1,256,256]{2,1,0:T(8,128)(2,1)S(1)} %bitcast.54), channel_id=1, source_target_pairs={{0,1},{1,0},{2,3},{3,2},{4,5},{5,4},{6,7},{7,6},{8,9},{9,8},{10,11... | collective-permute-start | bytes 393224 | tf_op jit(solution)/shard_map/ppermute | solution.py:232
  25.0 0.0 collective-permute-done.2.mid
  25.0 1.3 %collective-permute-start.10 = (bf16[1,256,256]{2,1,0:T(8,128)(2,1)S(1)}, bf16[1,256,256]{2,1,0:T(8,128)(2,1)S(1)}, u32[]{:S(2)}, u32[]{:S(2)}) collective-permute-start(bf16[1,256,256]{2,1,0:T(8,128)(2,1)S(1)} %collective-permute-done.8.far), channel_id=1, source_target_pairs={{1,0},{2,3},{5,4},{6,7},{9,8},{10,11},{13,12},{14,15},{17,16},{18,... | collective-permute-start | bytes 393224 | tf_op jit(solution)/shard_map/ppermute | solution.py:232
  26.3 0.1 pad_add_fusion.place
  26.4 0.0 collective-permute-done.near
  26.4 0.0 collective-permute-done.3.relay
  26.4 1.6 %shard_map.46 = (bf16[2,256,256]{2,1,0:T(8,128)(2,1)S(1)}, bf16[2,256,256]{2,1,0:T(8,128)(2,1)S(1)}) custom-call(s32[2]{0:T(128)S(1)} %pad_add_fusion.place, bf16[1,256,256]{2,1,0:T(8,128)(2,1)S(1)} %bitcast.50, bf16[1,256,256]{2,1,0:T(8,128)(2,1)S(1)} %collective-permute-done.near, bf16[1,256,256]{2,1,0:T(8,128)(2,1)S(1)} %collective-permute-done.1.far, ...), custom_call_target="tpu_custom_call" | custom-call | flops 536870912 | bytes 1048576 | tf_op jit(solution)/shard_map/pallas_call | solution.py:238
  28.0 0.0 copy-start
  28.0 1.6 %collective-permute-start.4 = (bf16[2,256,256]{2,1,0:T(8,128)(2,1)S(1)}, bf16[2,256,256]{2,1,0:T(8,128)(2,1)S(1)}, u32[]{:S(2)}, u32[]{:S(2)}) collective-permute-start(bf16[2,256,256]{2,1,0:T(8,128)(2,1)S(1)} %get-tuple-element.15.refs_0_), channel_id=1, source_target_pairs={{0,4},{4,0},{1,5},{5,1},{2,6},{6,2},{3,7},{7,3},{8,12},{12,8},{9,1... | collective-permute-start | bytes 786440 | tf_op jit(solution)/shard_map/ppermute | solution.py:235
  29.6 0.0 collective-permute-done.9.mid
  29.6 0.0 collective-permute-done.7.near
  29.6 2.3 %collective-permute-done.10.relay = bf16[1,256,256]{2,1,0:T(8,128)(2,1)S(1)} collective-permute-done((bf16[1,256,256]{2,1,0:T(8,128)(2,1)S(1)}, bf16[1,256,256]{2,1,0:T(8,128)(2,1)S(1)}, u32[]{:S(2)}, u32[]{:S(2)}) %collective-permute-start.10) | collective-permute-done | bytes 131104 | tf_op jit(solution)/shard_map/ppermute | solution.py:232
  31.8 1.6 %shard_map.49 = (bf16[2,256,256]{2,1,0:T(8,128)(2,1)S(1)}, bf16[2,256,256]{2,1,0:T(8,128)(2,1)S(1)}) custom-call(s32[2]{0:T(128)S(1)} %pad_add_fusion.place, bf16[1,256,256]{2,1,0:T(8,128)(2,1)S(1)} %bitcast.55, bf16[1,256,256]{2,1,0:T(8,128)(2,1)S(1)} %collective-permute-done.7.near, bf16[1,256,256]{2,1,0:T(8,128)(2,1)S(1)} %collective-permute-done.8.far, ...), custom_call_target="tpu_custom_call" | custom-call | flops 536870912 | bytes 1048576 | tf_op jit(solution)/shard_map/pallas_call | solution.py:238
  33.4 1.6 %collective-permute-start.11 = (bf16[2,256,256]{2,1,0:T(8,128)(2,1)S(1)}, bf16[2,256,256]{2,1,0:T(8,128)(2,1)S(1)}, u32[]{:S(2)}, u32[]{:S(2)}) collective-permute-start(bf16[2,256,256]{2,1,0:T(8,128)(2,1)S(1)} %get-tuple-element.19.refs_2_), channel_id=1, source_target_pairs={{0,4},{4,0},{1,5},{5,1},{2,6},{6,2},{3,7},{7,3},{8,12},{12,8},{9,1... | collective-permute-start | bytes 786440 | tf_op jit(solution)/shard_map/ppermute | solution.py:235
  35.0 1.6 %collective-permute-done.4.keyval.refs_1_ = bf16[2,256,256]{2,1,0:T(8,128)(2,1)S(1)} collective-permute-done((bf16[2,256,256]{2,1,0:T(8,128)(2,1)S(1)}, bf16[2,256,256]{2,1,0:T(8,128)(2,1)S(1)}, u32[]{:S(2)}, u32[]{:S(2)}) %collective-permute-start.4) | collective-permute-done | bytes 262176 | tf_op jit(solution)/shard_map/ppermute | solution.py:235
  36.7 0.0 copy-done.1
  36.7 1.7 %shard_map.50.partial = f32[256,256]{1,0:T(8,128)S(1)} custom-call(s32[2]{0:T(128)S(1)} %pad_add_fusion.place, s32[4]{0:T(128)S(1)} %copy-done.1, bf16[2,256,256]{2,1,0:T(8,128)(2,1)S(1)} %get-tuple-element.15.refs_0_, bf16[2,256,256]{2,1,0:T(8,128)(2,1)S(1)} %collective-permute-done.4.keyval.refs_1_, bf16[2,256,256]{2,1,0:T(8,128)(2,1)S(1)} %get-tuple-element.19.refs_2_, ...), custom_call_target="tpu_custom_call" | custom-call | flops 201326592 | bytes 1048576 | tf_op jit(solution)/shard_map/pallas_call | solution.py:238
  38.3 2.6 %collective-permute-done.11.keyval = bf16[2,256,256]{2,1,0:T(8,128)(2,1)S(1)} collective-permute-done((bf16[2,256,256]{2,1,0:T(8,128)(2,1)S(1)}, bf16[2,256,256]{2,1,0:T(8,128)(2,1)S(1)}, u32[]{:S(2)}, u32[]{:S(2)}) %collective-permute-start.11) | collective-permute-done | bytes 262176 | tf_op jit(solution)/shard_map/ppermute | solution.py:235
  41.0 0.0 copy-done
  41.0 1.6 %shard_map.51 = (bf16[2,128,256]{2,1,0:T(8,128)(2,1)S(1)}, f32[2,128,256]{2,1,0:T(8,128)S(1)}, bf16[2,128,256]{2,1,0:T(8,128)(2,1)S(1)}, f32[2,128,256]{2,1,0:T(8,128)S(1)}) custom-call(s32[2]{0:T(128)S(1)} %pad_add_fusion.place, s32[4]{0:T(128)S(1)} %copy-done.1, bf16[2,256,256]{2,1,0:T(8,128)(2,1)S(1)} %collective-permute-done.11.keyval, ...), custom_call_target="tpu_custom_call" | custom-call | flops 201326592 | bytes 1048576 | tf_op jit(solution)/shard_map/pallas_call | solution.py:238
  42.5 2.4 %collective-permute-start.12 = (bf16[2,128,256]{2,1,0:T(8,128)(2,1)S(1)}, bf16[2,128,256]{2,1,0:T(8,128)(2,1)S(1)}, u32[]{:S(2)}, u32[]{:S(2)}) collective-permute-start(bf16[2,128,256]{2,1,0:T(8,128)(2,1)S(1)} %get-tuple-element.22), channel_id=1, source_target_pairs={{0,1},{1,0},{2,3},{3,2},{4,5},{5,4},{6,7},{7,6},{8,9},{9,8},{10,11... | collective-permute-start | bytes 393224 | tf_op jit(solution)/shard_map/ppermute | solution.py:232
  45.0 1.1 %shard_map.47.partial = f32[256,256]{1,0:T(8,128)S(1)} custom-call(s32[2]{0:T(128)S(1)} %pad_add_fusion.place, s32[4]{0:T(128)S(1)} %copy-done.1, bf16[2,256,256]{2,1,0:T(8,128)(2,1)S(1)} %get-tuple-element.15.refs_0_, bf16[2,256,256]{2,1,0:T(8,128)(2,1)S(1)} %get-tuple-element.16.refs_1_.gateq), custom_call_target="tpu_custom_call" | custom-call | flops 67108864 | bytes 1048576 | tf_op jit(solution)/shard_map/pallas_call | solution.py:238
  46.1 0.1 collective-permute-start.14
  46.2 1.6 %shard_map.48 = (bf16[2,256,256]{2,1,0:T(8,128)(2,1)S(1)}, f32[2,256,256]{2,1,0:T(8,128)S(1)}) custom-call(s32[2]{0:T(128)S(1)} %pad_add_fusion.place, s32[4]{0:T(128)S(1)} %copy-done.1, bf16[2,256,256]{2,1,0:T(8,128)(2,1)S(1)} %collective-permute-done.4.keyval.refs_1_, f32[256,256]{1,0:T(8,128)S(1)} %shard_map.47.partial, ...), custom_call_target="tpu_custom_call" | custom-call | flops 201326592 | bytes 1048576 | tf_op jit(solution)/shard_map/pallas_call | solution.py:238
  47.8 2.1 %collective-permute-start.5 = (bf16[2,256,256]{2,1,0:T(8,128)(2,1)S(1)}, bf16[2,256,256]{2,1,0:T(8,128)(2,1)S(1)}, u32[]{:S(2)}, u32[]{:S(2)}) collective-permute-start(bf16[2,256,256]{2,1,0:T(8,128)(2,1)S(1)} %get-tuple-element.18), channel_id=1, source_target_pairs={{0,1},{1,0},{2,3},{3,2},{4,5},{5,4},{6,7},{7,6},{8,9},{9,8},{10,11... | collective-permute-start | bytes 786440 | tf_op jit(solution)/shard_map/ppermute | solution.py:232
  49.8 0.0 collective-permute-done.12
  49.9 0.1 collective-permute-start.13
  50.0 4.0 %collective-permute-done.14 = bf16[2,128,256]{2,1,0:T(8,128)(2,1)S(1)} collective-permute-done((bf16[2,128,256]{2,1,0:T(8,128)(2,1)S(1)}, bf16[2,128,256]{2,1,0:T(8,128)(2,1)S(1)}, u32[]{:S(2)}, u32[]{:S(2)}) %collective-permute-start.14) | collective-permute-done | bytes 131104 | tf_op jit(solution)/shard_map/ppermute | solution.py:232
  54.0 0.1 collective-permute-start.15
  54.1 4.3 %collective-permute-done.5 = bf16[2,256,256]{2,1,0:T(8,128)(2,1)S(1)} collective-permute-done((bf16[2,256,256]{2,1,0:T(8,128)(2,1)S(1)}, bf16[2,256,256]{2,1,0:T(8,128)(2,1)S(1)}, u32[]{:S(2)}, u32[]{:S(2)}) %collective-permute-start.5) | collective-permute-done | bytes 262176 | tf_op jit(solution)/shard_map/ppermute | solution.py:232
  58.4 0.1 convert_add_fusion
  58.4 0.1 collective-permute-start.6
  58.5 3.1 %collective-permute-done.15 = bf16[128,256]{1,0:T(8,128)(2,1)S(1)} collective-permute-done((bf16[128,256]{1,0:T(8,128)(2,1)S(1)}, bf16[128,256]{1,0:T(8,128)(2,1)S(1)}, u32[]{:S(2)}, u32[]{:S(2)}) %collective-permute-start.15) | collective-permute-done | bytes 65568 | tf_op jit(solution)/shard_map/ppermute | solution.py:232
  61.7 3.6 %collective-permute-done.6 = bf16[256,256]{1,0:T(8,128)(2,1)S(1)} collective-permute-done((bf16[256,256]{1,0:T(8,128)(2,1)S(1)}, bf16[256,256]{1,0:T(8,128)(2,1)S(1)}, u32[]{:S(2)}, u32[]{:S(2)}) %collective-permute-start.6) | collective-permute-done | bytes 131104 | tf_op jit(solution)/shard_map/ppermute | solution.py:232
  65.3 1.6 %collective-permute-start.16 = (bf16[2,128,256]{2,1,0:T(8,128)(2,1)S(1)}, bf16[2,128,256]{2,1,0:T(8,128)(2,1)S(1)}, u32[]{:S(2)}, u32[]{:S(2)}) collective-permute-start(bf16[2,128,256]{2,1,0:T(8,128)(2,1)S(1)} %pad_maximum_fusion), channel_id=1, source_target_pairs={{0,4},{4,0},{1,5},{5,1},{2,6},{6,2},{3,7},{7,3},{8,12},{12,8},{9,1... | collective-permute-start | bytes 393224 | tf_op jit(solution)/shard_map/ppermute | solution.py:235
  66.9 0.0 collective-permute-done.13
  67.0 3.4 %collective-permute-done.16 = bf16[2,128,256]{2,1,0:T(8,128)(2,1)S(1)} collective-permute-done((bf16[2,128,256]{2,1,0:T(8,128)(2,1)S(1)}, bf16[2,128,256]{2,1,0:T(8,128)(2,1)S(1)}, u32[]{:S(2)}, u32[]{:S(2)}) %collective-permute-start.16) | collective-permute-done | bytes 131104 | tf_op jit(solution)/shard_map/ppermute | solution.py:235
  70.4 0.8 %maximum_select_fusion = bf16[1,2,256,256]{3,2,1,0:T(8,128)(2,1)} fusion(bf16[1,2,128,256]{3,2,1,0:T(8,128)(2,1)S(1)} %bitcast.58, bf16[1,2,128,256]{3,2,1,0:T(8,128)(2,1)S(1)} %maximum_bitcast_fusion, pred[]{:T(512)S(6)} %eq.3), kind=kLoop, calls=%fused_computation.5 | loop fusion | flops 1179648 | bytes 524289 | tf_op jit(solution)/shard_map/jit(_where)/select_n | solution.py:316
  (12 shorter events, 0.2 us)
Async XLA Ops:
  1.0 14.2 %collective-permute-start.1 = (bf16[1,256,256]{2,1,0:T(8,128)(2,1)S(1)}, bf16[1,256,256]{2,1,0:T(8,128)(2,1)S(1)}, u32[]{:S(2)}, u32[]{:S(2)}) collective-permute-start(bf16[1,256,256]{2,1,0:T(8,128)(2,1)S(1)} %bitcast.47), channel_id=1, source_target_pairs={{0,2},{1,3},{2,0},{3,1},{4,6},{5,7},{6,4},{7,5},{8,10},{9,11},{10,... | collective-permute-start | bytes 393224 | tf_op jit(solution)/shard_map/ppermute | solution.py:232
  5.1 14.1 %collective-permute-start.8 = (bf16[1,256,256]{2,1,0:T(8,128)(2,1)S(1)}, bf16[1,256,256]{2,1,0:T(8,128)(2,1)S(1)}, u32[]{:S(2)}, u32[]{:S(2)}) collective-permute-start(bf16[1,256,256]{2,1,0:T(8,128)(2,1)S(1)} %bitcast.52), channel_id=1, source_target_pairs={{0,2},{1,3},{2,0},{3,1},{4,6},{5,7},{6,4},{7,5},{8,10},{9,11},{10,... | collective-permute-start | bytes 393224 | tf_op jit(solution)/shard_map/ppermute | solution.py:232
  5.2 19.8 %collective-permute-start.2 = (bf16[1,256,256]{2,1,0:T(8,128)(2,1)S(1)}, bf16[1,256,256]{2,1,0:T(8,128)(2,1)S(1)}, u32[]{:S(2)}, u32[]{:S(2)}) collective-permute-start(bf16[1,256,256]{2,1,0:T(8,128)(2,1)S(1)} %bitcast.48), channel_id=1, source_target_pairs={{1,2},{2,1},{5,6},{6,5},{9,10},{10,9},{13,14},{14,13},{17,18},{18,... | collective-permute-start | bytes 393224 | tf_op jit(solution)/shard_map/ppermute | solution.py:232
  5.9 20.5 %collective-permute-start = (bf16[1,256,256]{2,1,0:T(8,128)(2,1)S(1)}, bf16[1,256,256]{2,1,0:T(8,128)(2,1)S(1)}, u32[]{:S(2)}, u32[]{:S(2)}) collective-permute-start(bf16[1,256,256]{2,1,0:T(8,128)(2,1)S(1)} %bitcast.49), channel_id=1, source_target_pairs={{0,1},{1,0},{2,3},{3,2},{4,5},{5,4},{6,7},{7,6},{8,9},{9,8},{10,11... | collective-permute-start | bytes 393224 | tf_op jit(solution)/shard_map/ppermute | solution.py:232
  15.2 11.2 %collective-permute-start.3 = (bf16[1,256,256]{2,1,0:T(8,128)(2,1)S(1)}, bf16[1,256,256]{2,1,0:T(8,128)(2,1)S(1)}, u32[]{:S(2)}, u32[]{:S(2)}) collective-permute-start(bf16[1,256,256]{2,1,0:T(8,128)(2,1)S(1)} %collective-permute-done.1.far), channel_id=1, source_target_pairs={{1,0},{2,3},{5,4},{6,7},{9,8},{10,11},{13,12},{14,15},{17,16},{18,... | collective-permute-start | bytes 393224 | tf_op jit(solution)/shard_map/ppermute | solution.py:232
  16.5 13.1 %collective-permute-start.9 = (bf16[1,256,256]{2,1,0:T(8,128)(2,1)S(1)}, bf16[1,256,256]{2,1,0:T(8,128)(2,1)S(1)}, u32[]{:S(2)}, u32[]{:S(2)}) collective-permute-start(bf16[1,256,256]{2,1,0:T(8,128)(2,1)S(1)} %bitcast.53), channel_id=1, source_target_pairs={{1,2},{2,1},{5,6},{6,5},{9,10},{10,9},{13,14},{14,13},{17,18},{18,... | collective-permute-start | bytes 393224 | tf_op jit(solution)/shard_map/ppermute | solution.py:232
  19.3 10.3 %collective-permute-start.7 = (bf16[1,256,256]{2,1,0:T(8,128)(2,1)S(1)}, bf16[1,256,256]{2,1,0:T(8,128)(2,1)S(1)}, u32[]{:S(2)}, u32[]{:S(2)}) collective-permute-start(bf16[1,256,256]{2,1,0:T(8,128)(2,1)S(1)} %bitcast.54), channel_id=1, source_target_pairs={{0,1},{1,0},{2,3},{3,2},{4,5},{5,4},{6,7},{7,6},{8,9},{9,8},{10,11... | collective-permute-start | bytes 393224 | tf_op jit(solution)/shard_map/ppermute | solution.py:232
  25.0 6.9 %collective-permute-start.10 = (bf16[1,256,256]{2,1,0:T(8,128)(2,1)S(1)}, bf16[1,256,256]{2,1,0:T(8,128)(2,1)S(1)}, u32[]{:S(2)}, u32[]{:S(2)}) collective-permute-start(bf16[1,256,256]{2,1,0:T(8,128)(2,1)S(1)} %collective-permute-done.8.far), channel_id=1, source_target_pairs={{1,0},{2,3},{5,4},{6,7},{9,8},{10,11},{13,12},{14,15},{17,16},{18,... | collective-permute-start | bytes 393224 | tf_op jit(solution)/shard_map/ppermute | solution.py:232
  26.4 10.3 %copy-start.1 = (s32[4]{0:T(128)S(1)}, s32[4]{0:T(128)}, u32[]{:S(2)}) copy-start(s32[4]{0:T(128)} %lengths.7) | copy-start | bytes 52
  28.0 13.0 %copy-start = (bf16[256,1024]{1,0:T(8,128)(2,1)S(1)}, bf16[256,1024]{1,0:T(8,128)(2,1)}, u32[]{:S(2)}) copy-start(bf16[256,1024]{1,0:T(8,128)(2,1)} %weight.3) | copy-start | bytes 1572868
  28.0 8.7 %collective-permute-start.4 = (bf16[2,256,256]{2,1,0:T(8,128)(2,1)S(1)}, bf16[2,256,256]{2,1,0:T(8,128)(2,1)S(1)}, u32[]{:S(2)}, u32[]{:S(2)}) collective-permute-start(bf16[2,256,256]{2,1,0:T(8,128)(2,1)S(1)} %get-tuple-element.15.refs_0_), channel_id=1, source_target_pairs={{0,4},{4,0},{1,5},{5,1},{2,6},{6,2},{3,7},{7,3},{8,12},{12,8},{9,1... | collective-permute-start | bytes 786440 | tf_op jit(solution)/shard_map/ppermute | solution.py:235
  33.4 7.5 %collective-permute-start.11 = (bf16[2,256,256]{2,1,0:T(8,128)(2,1)S(1)}, bf16[2,256,256]{2,1,0:T(8,128)(2,1)S(1)}, u32[]{:S(2)}, u32[]{:S(2)}) collective-permute-start(bf16[2,256,256]{2,1,0:T(8,128)(2,1)S(1)} %get-tuple-element.19.refs_2_), channel_id=1, source_target_pairs={{0,4},{4,0},{1,5},{5,1},{2,6},{6,2},{3,7},{7,3},{8,12},{12,8},{9,1... | collective-permute-start | bytes 786440 | tf_op jit(solution)/shard_map/ppermute | solution.py:235
  42.5 7.3 %collective-permute-start.12 = (bf16[2,128,256]{2,1,0:T(8,128)(2,1)S(1)}, bf16[2,128,256]{2,1,0:T(8,128)(2,1)S(1)}, u32[]{:S(2)}, u32[]{:S(2)}) collective-permute-start(bf16[2,128,256]{2,1,0:T(8,128)(2,1)S(1)} %get-tuple-element.22), channel_id=1, source_target_pairs={{0,1},{1,0},{2,3},{3,2},{4,5},{5,4},{6,7},{7,6},{8,9},{9,8},{10,11... | collective-permute-start | bytes 393224 | tf_op jit(solution)/shard_map/ppermute | solution.py:232
  46.1 7.8 %collective-permute-start.14 = (bf16[2,128,256]{2,1,0:T(8,128)(2,1)S(1)}, bf16[2,128,256]{2,1,0:T(8,128)(2,1)S(1)}, u32[]{:S(2)}, u32[]{:S(2)}) collective-permute-start(bf16[2,128,256]{2,1,0:T(8,128)(2,1)S(1)} %get-tuple-element.24), channel_id=1, source_target_pairs={{0,1},{1,0},{2,3},{3,2},{4,5},{5,4},{6,7},{7,6},{8,9},{9,8},{10,11... | collective-permute-start | bytes 393224 | tf_op jit(solution)/shard_map/ppermute | solution.py:232
  47.8 10.6 %collective-permute-start.5 = (bf16[2,256,256]{2,1,0:T(8,128)(2,1)S(1)}, bf16[2,256,256]{2,1,0:T(8,128)(2,1)S(1)}, u32[]{:S(2)}, u32[]{:S(2)}) collective-permute-start(bf16[2,256,256]{2,1,0:T(8,128)(2,1)S(1)} %get-tuple-element.18), channel_id=1, source_target_pairs={{0,1},{1,0},{2,3},{3,2},{4,5},{5,4},{6,7},{7,6},{8,9},{9,8},{10,11... | collective-permute-start | bytes 786440 | tf_op jit(solution)/shard_map/ppermute | solution.py:232
  49.9 17.0 %collective-permute-start.13 = (bf16[128,256]{1,0:T(8,128)(2,1)S(1)}, bf16[128,256]{1,0:T(8,128)(2,1)S(1)}, u32[]{:S(2)}, u32[]{:S(2)}) collective-permute-start(bf16[128,256]{1,0:T(8,128)(2,1)S(1)} %fusion.8), channel_id=1, source_target_pairs={{0,2},{1,3},{2,0},{3,1},{4,6},{5,7},{6,4},{7,5},{8,10},{9,11},{10,... | collective-permute-start | bytes 196616 | tf_op jit(solution)/shard_map/ppermute | solution.py:232
  54.0 7.7 %collective-permute-start.15 = (bf16[128,256]{1,0:T(8,128)(2,1)S(1)}, bf16[128,256]{1,0:T(8,128)(2,1)S(1)}, u32[]{:S(2)}, u32[]{:S(2)}) collective-permute-start(bf16[128,256]{1,0:T(8,128)(2,1)S(1)} %fusion.10), channel_id=1, source_target_pairs={{0,2},{1,3},{2,0},{3,1},{4,6},{5,7},{6,4},{7,5},{8,10},{9,11},{10,... | collective-permute-start | bytes 196616 | tf_op jit(solution)/shard_map/ppermute | solution.py:232
  58.4 6.8 %collective-permute-start.6 = (bf16[256,256]{1,0:T(8,128)(2,1)S(1)}, bf16[256,256]{1,0:T(8,128)(2,1)S(1)}, u32[]{:S(2)}, u32[]{:S(2)}) collective-permute-start(bf16[256,256]{1,0:T(8,128)(2,1)S(1)} %fusion.2), channel_id=1, source_target_pairs={{0,2},{1,3},{2,0},{3,1},{4,6},{5,7},{6,4},{7,5},{8,10},{9,11},{10,... | collective-permute-start | bytes 393224 | tf_op jit(solution)/shard_map/ppermute | solution.py:232
  65.3 5.0 %collective-permute-start.16 = (bf16[2,128,256]{2,1,0:T(8,128)(2,1)S(1)}, bf16[2,128,256]{2,1,0:T(8,128)(2,1)S(1)}, u32[]{:S(2)}, u32[]{:S(2)}) collective-permute-start(bf16[2,128,256]{2,1,0:T(8,128)(2,1)S(1)} %pad_maximum_fusion), channel_id=1, source_target_pairs={{0,4},{4,0},{1,5},{5,1},{2,6},{6,2},{3,7},{7,3},{8,12},{12,8},{9,1... | collective-permute-start | bytes 393224 | tf_op jit(solution)/shard_map/ppermute | solution.py:235

commit v3 on v2

--- a/solution.py
+++ b/solution.py
@@ -139,14 +139,14 @@
 
 
 def weighted_values(plan, place, lengths, gateq, keyvals, first=None):
-    chunk, chunk_blocks, stripe, origins = plan
+    chunk, stripe, origins = plan
     rows, cols = gateq.shape[1:]
-    block_len = 2 * stripe
 
     def positions(shape, dim, which, side):
         offset = lax.broadcasted_iota(jnp.int32, shape, dim)
-        block, inner = offset // stripe, offset % stripe
-        return (which * chunk_blocks + block) * block_len + side * stripe + inner
+        block = side if which == 0 else 3 - side
+        inner = jnp.where(offset < stripe, offset + side * stripe, offset - side * stripe)
+        return block * rows + inner
 
     query_pos = positions((rows, 1), 0, chunk, place[0])
     start = jnp.zeros((rows, 1), jnp.int32)
@@ -182,9 +182,8 @@
         partial[:, head * HDIM : (head + 1) * HDIM] = total
 
 
-def attend_kernel(plan, splits, place, lengths, keyval, partial, gateq, weight, share, *refs):
+def attend_kernel(plan, place, lengths, keyval, partial, gateq, weight, share, *refs):
     *outputs, held = refs
-    chunk, _, stripe, _ = plan
     part = share.shape[2]
     totals = weighted_values(plan, place, lengths, gateq, [keyval], partial)
     for head, total in enumerate(totals):
@@ -193,23 +192,13 @@
         spread = jnp.mean(total * total, axis=1, keepdims=True)
         total = total * lax.rsqrt(spread + 1e-05)
         held[:, lanes] = (total * gateq[0, :, lanes].astype(F32)).astype(BF16)
-    away = place[0] if chunk == 1 else 1 - place[0]
-    leads = [pl.multiple_of(away * stripe, stripe), pl.multiple_of((1 - away) * stripe, stripe)]
-    gated = [held[pl.ds(lead, stripe), :] for lead in leads]
-    shares = [share[0, pl.ds(lead, stripe), :] for lead in leads]
-    if splits == 1:
-        gated, shares = [jnp.concatenate(gated, axis=0)], [jnp.concatenate(shares, axis=0)]
-    for index in range(splits):
-        sent, kept = outputs[2 * index : 2 * index + 2]
-        for share_id in (1, 3, 2, 0):
-            lead = pl.multiple_of((place[1] ^ share_id) * part, part)
-            product = jnp.dot(
-                gated[index], weight[:, pl.ds(lead, part)], preferred_element_type=F32
-            )
-            if share_id == 0:
-                product = product + shares[index].astype(F32)
-            target = sent if share_id & 1 else kept
-            target[share_id >> 1] = product.astype(target.dtype)
+    gated = held[...]
+    for share_id in (2, 3, 1, 0):
+        lead = pl.multiple_of((place[1] ^ share_id) * part, part)
+        product = jnp.dot(gated, weight[:, pl.ds(lead, part)], preferred_element_type=F32)
+        if share_id == 0:
+            product = product + share[0].astype(F32)
+        outputs[share_id][...] = product.astype(outputs[share_id].dtype)
 
 
 def whole(memory_space=pltpu.VMEM):
@@ -219,9 +208,8 @@
 def pair_body(inputs, lengths, proj_in, proj_out):
     head_size = lax.axis_size("head")
     own = lax.axis_index("ctx")
-    block_total, stripe, part = inputs.shape
-    chunk_blocks = block_total // 2
-    rows = chunk_blocks * stripe
+    _, stripe, part = inputs.shape
+    rows = 2 * stripe
     cols = proj_in.shape[2]
     place = jnp.stack([own, lax.axis_index("head")]).astype(jnp.int32)
     weight_in = proj_in.reshape(proj_in.shape[0], -1)
@@ -248,13 +236,24 @@
     def cost(flops, transcendentals):
         return pl.CostEstimate(flops=flops, bytes_accessed=1 << 20, transcendentals=transcendentals)
 
+    weights = []
     inner = [(1, 2), (2, 1)]
     outer = [(1, 0), (2, 3)]
 
-    def gather(own_share):
+    def settle(chunk):
+        stay = own if chunk == 0 else 1 - own
+        blocks = inputs[chunk * 2 : chunk * 2 + 2]
+        home = lax.dynamic_index_in_dim(blocks, stay, 0, keepdims=True)
+        away = lax.dynamic_index_in_dim(blocks, 1 - stay, 0, keepdims=True)
+        return jnp.concatenate([home, over_ctx(away)], axis=1)
+
+    def gather(own_share, tag):
         far = over_head(own_share, 2)
         near = over_head(own_share, 1)
         mid = over_head(own_share, inner)
+        if tag == "a":
+            far, weight = lax.optimization_barrier((far, weight_in))
+            weights.append(weight)
         relay = over_head(far, outer)
         return own_share, near, far, mid, relay
 
@@ -263,7 +262,7 @@
         return kernel_call(
             project_kernel,
             (size, size),
-            (place, *shares, weight_in),
+            (place, *shares, weights[0]),
             1,
             cost(2 * rows * weight_in.size, rows * 4 * cols),
         )
@@ -271,52 +270,41 @@
     def near_part(chunk, origins, keyvals, gateq):
         count = len(keyvals)
         return kernel_call(
-            functools.partial(near_kernel, (chunk, chunk_blocks, stripe, origins)),
+            functools.partial(near_kernel, (chunk, stripe, origins)),
             (((rows, cols), F32),),
             (place, lengths, *keyvals, gateq),
             2,
             cost(4 * rows * rows * cols * count, rows * rows * count * (cols // HDIM)),
         )[0]
 
-    def attend(chunk, keyval, partial, gateq, share, splits):
-        size = (2, rows // splits, part)
+    def attend(chunk, keyval, partial, gateq, share):
+        size = (rows, part)
         return kernel_call(
-            functools.partial(
-                attend_kernel, (chunk, chunk_blocks, stripe, [(chunk, 1)]), splits
-            ),
-            ((size, BF16), (size, F32)) * splits,
+            functools.partial(attend_kernel, (chunk, stripe, [(chunk, 1)])),
+            ((size, F32),) + ((size, BF16),) * 3,
             (place, lengths, keyval, partial, gateq, proj_out, share),
             2,
             cost(4 * rows * rows * cols + 2 * rows * proj_out.size, rows * rows * (cols // HDIM)),
             [pltpu.VMEM((rows, cols), BF16)],
         )
 
-    def total(sent, kept):
-        kept = kept + over_head(sent, 1).astype(F32)
-        far = over_head(kept[1].astype(BF16), 2)
-        return (kept[0] + far.astype(F32)).astype(BF16)
-
-    chunks = [inputs[:chunk_blocks].reshape(1, rows, part), inputs[chunk_blocks:].reshape(1, rows, part)]
-    low = gather(chunks[0])
-    low_keyval, low_gateq = project(low)
+    def total(kept, *sent):
+        for share_id in (2, 3, 1):
+            kept = kept + over_head(sent[share_id - 1], share_id).astype(F32)
+        return kept.astype(BF16)
+
+    shares = [settle(0), settle(1)]
+    low_keyval, low_gateq = project(gather(shares[0], "a"))
     low_other = over_ctx(low_keyval)
-    high = gather(chunks[1])
-    high_keyval, high_gateq = project(high)
+    high_keyval, high_gateq = project(gather(shares[1], "b"))
     high_other = over_ctx(high_keyval)
     low_first = near_part(0, [(0, 0)], [low_keyval], low_gateq)
-    sent, kept = attend(0, low_other, low_first, low_gateq, chunks[0], 1)
-    low_done = total(sent, kept)
+    low_done = total(*attend(0, low_other, low_first, low_gateq, shares[0]))
     origins = [(0, 0), (0, 1), (1, 0)]
     high_first = near_part(1, origins, [low_keyval, low_other, high_keyval], high_gateq)
-    sent, kept, sent_stay, kept_stay = attend(1, high_other, high_first, high_gateq, chunks[1], 2)
-    high_move = total(sent, kept)
-    high_stay = total(sent_stay, kept_stay)
-    come = over_ctx(jnp.stack([low_done[:stripe], high_move]))
-    stay = jnp.stack([low_done[stripe:], high_stay])
-    result = jnp.where(
-        own == 0, jnp.concatenate([stay, come], axis=1), jnp.concatenate([come, stay], axis=1)
-    )
-    return result[None]
+    high_done = total(*attend(1, high_other, high_first, high_gateq, shares[1]))
+    both = jnp.stack([low_done, high_done]).reshape(2, 2, stripe, part)
+    return jnp.where(own == 0, both, both[:, ::-1]).reshape(1, 2, rows, part)
 
 
 def body(inputs, lengths, proj_in, proj_out):

time: 71.4 us -> 61.6 us (0.86)
  waiting for transfers between devices: 29.6 us -> 19.7 us
  starting transfers between devices: 28.1 us -> 26.2 us
  Pallas kernels: 9.08 us -> 10.2 us
  local copies, waits for them, and re-layouts: 3.13 us -> 4.05 us
    ppermute x14, waiting for transfers between devices: 21.9 us -> 16.5 us  [over_head(): return lax.ppermute(value, 'head', pairs)]
    ppermute x3 -> x4, waiting for transfers between devices: 7.68 us -> 3.2 us  [over_ctx(): return lax.ppermute(value, 'ctx', [(0, 1), (1, 0)])]
    ppermute x14, starting transfers between devices: 23.3 us -> 22.2 us  [over_head(): return lax.ppermute(value, 'head', pairs)]
    pallas_call x6, Pallas kernels: 9.08 us -> 10.2 us  [kernel_call(): pl.pallas_call(function, compiler_params=pltpu.CompilerParams(vmem_limit_...]
    unnamed x5 -> x9, local copies, waits for them, and re-layouts: 2.1 us -> 3.04 us
    ppermute x3 -> x4, starting transfers between devices: 4.75 us -> 4.07 us  [over_ctx(): return lax.ppermute(value, 'ctx', [(0, 1), (1, 0)])]
  transfers between devices with their start and end apart: 17 -> 18, of which waited for: 9 -> 8; matrix products, arithmetic and copies ran while one was open for 3% -> 4% of each run, Pallas kernels for 11% -> 17%
where the time goes in v3:
time: 61.6 us; the launch traced here: 61.3 us
  starting transfers between devices  26.2 us (43%)
  waiting for transfers between devices  19.7 us (32%)
  Pallas kernels  10.2 us (17%)
  local copies, waits for them, and re-layouts  4.05 us (7%)
  other arithmetic  1.01 us (2%)
    ppermute x14, starting transfers between devices, over_head(): return lax.ppermute(value, 'head', pairs)  22.2 us
    ppermute x14, waiting for transfers between devices, over_head(): return lax.ppermute(value, 'head', pairs)  16.5 us
    pallas_call x6, Pallas kernels, kernel_call(): pl.pallas_call(function, compiler_params=pltpu.CompilerParams(vmem_limit_...  10.2 us
    ppermute x4, starting transfers between devices, over_ctx(): return lax.ppermute(value, 'ctx', [(0, 1), (1, 0)])  4.07 us
    ppermute x4, waiting for transfers between devices, over_ctx(): return lax.ppermute(value, 'ctx', [(0, 1), (1, 0)])  3.2 us
    unnamed x9, local copies, waits for them, and re-layouts  3.04 us
  transfers between devices with their start and end apart: 18, of which 8 were waited for; matrix products, arithmetic and copies ran while one was open for 4% of the time, Pallas kernels for 17%

profile of v3, /device:TPU:0, one launch (start us, length us, event | category | flops | bytes accessed | tf_op | source)
XLA Modules:
  0.0 61.3 jit_solution(17941545362316323004)
XLA Ops:
  0.0 1.0 %fusion = (bf16[2,128,256]{2,1,0:T(8,128)(2,1)S(1)}, bf16[2,128,256]{2,1,0:T(8,128)(2,1)S(1)}) fusion(bf16[4,128,256]{2,1,0:T(8,128)(2,1)} %param.4), kind=kLoop, calls=%fused_computation.11 | loop fusion | bytes 524288 | tf_op jit(solution)/shard_map/slice | solution.py:245
  1.0 3.1 %collective-permute-start = (bf16[1,128,256]{2,1,0:T(8,128)(2,1)S(1)}, bf16[1,128,256]{2,1,0:T(8,128)(2,1)S(1)}, u32[]{:S(2)}, u32[]{:S(2)}) collective-permute-start(bf16[1,128,256]{2,1,0:T(8,128)(2,1)S(1)} %get-tuple-element.36), channel_id=1, source_target_pairs={{0,4},{4,0},{1,5},{5,1},{2,6},{6,2},{3,7},{7,3},{8,12},{12,8},{9,1... | collective-permute-start | bytes 196616 | tf_op jit(solution)/shard_map/ppermute | solution.py:223
  4.1 0.1 collective-permute-start.9
  4.2 2.2 %collective-permute-done = bf16[1,128,256]{2,1,0:T(8,128)(2,1)S(1)} collective-permute-done((bf16[1,128,256]{2,1,0:T(8,128)(2,1)S(1)}, bf16[1,128,256]{2,1,0:T(8,128)(2,1)S(1)}, u32[]{:S(2)}, u32[]{:S(2)}) %collective-permute-start) | collective-permute-done | bytes 65568 | tf_op jit(solution)/shard_map/ppermute | solution.py:223
  6.4 3.7 %collective-permute-start.2 = (bf16[1,256,256]{2,1,0:T(8,128)(2,1)S(1)}, bf16[1,256,256]{2,1,0:T(8,128)(2,1)S(1)}, u32[]{:S(2)}, u32[]{:S(2)}) collective-permute-start(bf16[1,256,256]{2,1,0:T(8,128)(2,1)S(1)} %pad_maximum_fusion.1.own.share), channel_id=1, source_target_pairs={{0,2},{1,3},{2,0},{3,1},{4,6},{5,7},{6,4},{7,5},{8,10},{9,11},{10,... | collective-permute-start | bytes 393224 | tf_op jit(solution)/shard_map/ppermute | solution.py:220
  10.0 2.1 %copy.5 = bf16[128,8,4,256]{3,1,2,0:T(8,128)(2,1)S(1)} copy(bf16[128,8,4,256]{3,2,1,0:T(4,128)(2,1)} %bitcast.9) | data formatting | bytes 4194304
  12.1 0.7 %collective-permute-start.3 = (bf16[1,256,256]{2,1,0:T(8,128)(2,1)S(1)}, bf16[1,256,256]{2,1,0:T(8,128)(2,1)S(1)}, u32[]{:S(2)}, u32[]{:S(2)}) collective-permute-start(bf16[1,256,256]{2,1,0:T(8,128)(2,1)S(1)} %pad_maximum_fusion.1.own.share), channel_id=1, source_target_pairs={{1,2},{2,1},{5,6},{6,5},{9,10},{10,9},{13,14},{14,13},{17,18},{18,... | collective-permute-start | bytes 393224 | tf_op jit(solution)/shard_map/ppermute | solution.py:220
  12.8 2.9 %collective-permute-start.1 = (bf16[1,256,256]{2,1,0:T(8,128)(2,1)S(1)}, bf16[1,256,256]{2,1,0:T(8,128)(2,1)S(1)}, u32[]{:S(2)}, u32[]{:S(2)}) collective-permute-start(bf16[1,256,256]{2,1,0:T(8,128)(2,1)S(1)} %pad_maximum_fusion.1.own.share), channel_id=1, source_target_pairs={{0,1},{1,0},{2,3},{3,2},{4,5},{5,4},{6,7},{7,6},{8,9},{9,8},{10,11... | collective-permute-start | bytes 393224 | tf_op jit(solution)/shard_map/ppermute | solution.py:220
  15.7 0.0 collective-permute-done.9
  15.7 1.5 %collective-permute-start.11 = (bf16[1,256,256]{2,1,0:T(8,128)(2,1)S(1)}, bf16[1,256,256]{2,1,0:T(8,128)(2,1)S(1)}, u32[]{:S(2)}, u32[]{:S(2)}) collective-permute-start(bf16[1,256,256]{2,1,0:T(8,128)(2,1)S(1)} %pad_maximum_fusion.2.own.share), channel_id=1, source_target_pairs={{0,2},{1,3},{2,0},{3,1},{4,6},{5,7},{6,4},{7,5},{8,10},{9,11},{10,... | collective-permute-start | bytes 393224 | tf_op jit(solution)/shard_map/ppermute | solution.py:220
  17.2 0.0 collective-permute-done.2.far
  17.2 1.3 %collective-permute-start.4 = (bf16[1,256,256]{2,1,0:T(8,128)(2,1)S(1)}, bf16[1,256,256]{2,1,0:T(8,128)(2,1)S(1)}, u32[]{:S(2)}, u32[]{:S(2)}) collective-permute-start(bf16[1,256,256]{2,1,0:T(8,128)(2,1)S(1)} %collective-permute-done.2.far), channel_id=1, source_target_pairs={{1,0},{2,3},{5,4},{6,7},{9,8},{10,11},{13,12},{14,15},{17,16},{18,... | collective-permute-start | bytes 393224 | tf_op jit(solution)/shard_map/ppermute | solution.py:220
  18.5 0.1 pad_add_fusion.place
  18.6 0.8 %collective-permute-start.12 = (bf16[1,256,256]{2,1,0:T(8,128)(2,1)S(1)}, bf16[1,256,256]{2,1,0:T(8,128)(2,1)S(1)}, u32[]{:S(2)}, u32[]{:S(2)}) collective-permute-start(bf16[1,256,256]{2,1,0:T(8,128)(2,1)S(1)} %pad_maximum_fusion.2.own.share), channel_id=1, source_target_pairs={{1,2},{2,1},{5,6},{6,5},{9,10},{10,9},{13,14},{14,13},{17,18},{18,... | collective-permute-start | bytes 393224 | tf_op jit(solution)/shard_map/ppermute | solution.py:220
  19.4 5.4 %collective-permute-done.11.far = bf16[1,256,256]{2,1,0:T(8,128)(2,1)S(1)} collective-permute-done((bf16[1,256,256]{2,1,0:T(8,128)(2,1)S(1)}, bf16[1,256,256]{2,1,0:T(8,128)(2,1)S(1)}, u32[]{:S(2)}, u32[]{:S(2)}) %collective-permute-start.11) | collective-permute-done | bytes 131104 | tf_op jit(solution)/shard_map/ppermute | solution.py:220
  24.8 1.3 %collective-permute-start.10 = (bf16[1,256,256]{2,1,0:T(8,128)(2,1)S(1)}, bf16[1,256,256]{2,1,0:T(8,128)(2,1)S(1)}, u32[]{:S(2)}, u32[]{:S(2)}) collective-permute-start(bf16[1,256,256]{2,1,0:T(8,128)(2,1)S(1)} %pad_maximum_fusion.2.own.share), channel_id=1, source_target_pairs={{0,1},{1,0},{2,3},{3,2},{4,5},{5,4},{6,7},{7,6},{8,9},{9,8},{10,11... | collective-permute-start | bytes 393224 | tf_op jit(solution)/shard_map/ppermute | solution.py:220
  26.1 0.0 collective-permute-done.3.mid
  26.1 1.3 %collective-permute-start.13 = (bf16[1,256,256]{2,1,0:T(8,128)(2,1)S(1)}, bf16[1,256,256]{2,1,0:T(8,128)(2,1)S(1)}, u32[]{:S(2)}, u32[]{:S(2)}) collective-permute-start(bf16[1,256,256]{2,1,0:T(8,128)(2,1)S(1)} %collective-permute-done.11.far), channel_id=1, source_target_pairs={{1,0},{2,3},{5,4},{6,7},{9,8},{10,11},{13,12},{14,15},{17,16},{18,... | collective-permute-start | bytes 393224 | tf_op jit(solution)/shard_map/ppermute | solution.py:220
  27.4 0.0 collective-permute-done.1.near
  27.4 1.6 %shard_map.46 = (bf16[2,256,256]{2,1,0:T(8,128)(2,1)S(1)}, bf16[2,256,256]{2,1,0:T(8,128)(2,1)S(1)}) custom-call(s32[2]{0:T(128)S(1)} %pad_add_fusion.place, bf16[1,256,256]{2,1,0:T(8,128)(2,1)S(1)} %pad_maximum_fusion.1.own.share, bf16[1,256,256]{2,1,0:T(8,128)(2,1)S(1)} %collective-permute-done.1.near, ...), custom_call_target="tpu_custom_call" | custom-call | flops 536870912 | bytes 1048576 | tf_op jit(solution)/shard_map/pallas_call | solution.py:226
  29.0 0.0 copy-start
  29.1 0.5 collective-permute-start.5
  29.5 0.2 collective-permute-done.10.near
  29.8 3.2 %collective-permute-done.13.relay = bf16[1,256,256]{2,1,0:T(8,128)(2,1)S(1)} collective-permute-done((bf16[1,256,256]{2,1,0:T(8,128)(2,1)S(1)}, bf16[1,256,256]{2,1,0:T(8,128)(2,1)S(1)}, u32[]{:S(2)}, u32[]{:S(2)}) %collective-permute-start.13) | collective-permute-done | bytes 131104 | tf_op jit(solution)/shard_map/ppermute | solution.py:220
  33.0 2.3 %shard_map.49 = (bf16[2,256,256]{2,1,0:T(8,128)(2,1)}, bf16[2,256,256]{2,1,0:T(8,128)(2,1)S(1)}) custom-call(s32[2]{0:T(128)S(1)} %pad_add_fusion.place, bf16[1,256,256]{2,1,0:T(8,128)(2,1)S(1)} %pad_maximum_fusion.2.own.share, bf16[1,256,256]{2,1,0:T(8,128)(2,1)S(1)} %collective-permute-done.10.near, bf16[1,256,256]{2,1,0:T(8,128)(2,1)S(1)} %collective-permute-done.11.far, ...), custom_call_target="tpu_custom_call" | custom-call | flops 536870912 | bytes 1048576 | tf_op jit(solution)/shard_map/pallas_call | solution.py:226
  35.3 0.4 collective-permute-start.14
  35.7 1.1 %shard_map.47.partial = f32[256,256]{1,0:T(8,128)S(1)} custom-call(s32[2]{0:T(128)S(1)} %pad_add_fusion.place, s32[4]{0:T(128)S(1)} %copy-done.3, bf16[2,256,256]{2,1,0:T(8,128)(2,1)S(1)} %get-tuple-element.21.refs_0_, bf16[2,256,256]{2,1,0:T(8,128)(2,1)S(1)} %get-tuple-element.22.refs_1_.gateq), custom_call_target="tpu_custom_call" | custom-call | flops 67108864 | bytes 1048576 | tf_op jit(solution)/shard_map/pallas_call | solution.py:226
  36.8 1.0 %collective-permute-done.5.keyval.refs_1_ = bf16[2,256,256]{2,1,0:T(8,128)(2,1)S(1)} collective-permute-done((bf16[2,256,256]{2,1,0:T(8,128)(2,1)S(1)}, bf16[2,256,256]{2,1,0:T(8,128)(2,1)S(1)}, u32[]{:S(2)}, u32[]{:S(2)}) %collective-permute-start.5) | collective-permute-done | bytes 262176 | tf_op jit(solution)/shard_map/ppermute | solution.py:223
  37.9 1.6 %shard_map.48 = (f32[256,256]{1,0:T(8,128)S(1)}, bf16[256,256]{1,0:T(8,128)(2,1)S(1)}, bf16[256,256]{1,0:T(8,128)(2,1)S(1)}, bf16[256,256]{1,0:T(8,128)(2,1)S(1)}) custom-call(s32[2]{0:T(128)S(1)} %pad_add_fusion.place, s32[4]{0:T(128)S(1)} %copy-done.3, bf16[2,256,256]{2,1,0:T(8,128)(2,1)S(1)} %collective-permute-done.5.keyval.refs_1_, ...), custom_call_target="tpu_custom_call" | custom-call | flops 201326592 | bytes 1048576 | tf_op jit(solution)/shard_map/pallas_call | solution.py:226
  39.5 3.4 %collective-permute-start.6 = (bf16[256,256]{1,0:T(8,128)(2,1)S(1)}, bf16[256,256]{1,0:T(8,128)(2,1)S(1)}, u32[]{:S(2)}, u32[]{:S(2)}) collective-permute-start(bf16[256,256]{1,0:T(8,128)(2,1)S(1)} %get-tuple-element.24), channel_id=1, source_target_pairs={{0,2},{1,3},{2,0},{3,1},{4,6},{5,7},{6,4},{7,5},{8,10},{9,11},{10,... | collective-permute-start | bytes 393224 | tf_op jit(solution)/shard_map/ppermute | solution.py:220
  42.9 0.8 %collective-permute-start.7 = (bf16[256,256]{1,0:T(8,128)(2,1)S(1)}, bf16[256,256]{1,0:T(8,128)(2,1)S(1)}, u32[]{:S(2)}, u32[]{:S(2)}) collective-permute-start(bf16[256,256]{1,0:T(8,128)(2,1)S(1)} %get-tuple-element.25), channel_id=1, source_target_pairs={{0,3},{1,2},{2,1},{3,0},{4,7},{5,6},{6,5},{7,4},{8,11},{9,10},{10,... | collective-permute-start | bytes 393224 | tf_op jit(solution)/shard_map/ppermute | solution.py:220
  43.7 0.0 collective-permute-start.8
  43.7 0.9 %copy-done.2 = bf16[2,256,256]{2,1,0:T(8,128)(2,1)S(1)} copy-done((bf16[2,256,256]{2,1,0:T(8,128)(2,1)S(1)}, bf16[2,256,256]{2,1,0:T(8,128)(2,1)}, u32[]{:S(2)}) %copy-start.2) | copy-done | bytes 262168
  44.7 2.0 %shard_map.50.partial = f32[256,256]{1,0:T(8,128)S(1)} custom-call(s32[2]{0:T(128)S(1)} %pad_add_fusion.place, s32[4]{0:T(128)S(1)} %copy-done.3, bf16[2,256,256]{2,1,0:T(8,128)(2,1)S(1)} %copy-done.2, bf16[2,256,256]{2,1,0:T(8,128)(2,1)S(1)} %collective-permute-done.5.keyval.refs_1_, bf16[2,256,256]{2,1,0:T(8,128)(2,1)} %get-tuple-element.27.refs_2_, ...), custom_call_target="tpu_custom_call" | custom-call | flops 201326592 | bytes 1048576 | tf_op jit(solution)/shard_map/pallas_call | solution.py:226
  46.7 0.0 collective-permute-done.14.keyval
  46.7 1.6 %shard_map.51 = (f32[256,256]{1,0:T(8,128)S(1)}, bf16[256,256]{1,0:T(8,128)(2,1)S(1)}, bf16[256,256]{1,0:T(8,128)(2,1)S(1)}, bf16[256,256]{1,0:T(8,128)(2,1)S(1)}) custom-call(s32[2]{0:T(128)S(1)} %pad_add_fusion.place, s32[4]{0:T(128)S(1)} %copy-done.3, bf16[2,256,256]{2,1,0:T(8,128)(2,1)S(1)} %collective-permute-done.14.keyval, ...), custom_call_target="tpu_custom_call" | custom-call | flops 201326592 | bytes 1048576 | tf_op jit(solution)/shard_map/pallas_call | solution.py:226
  48.3 3.6 %collective-permute-start.15 = (bf16[256,256]{1,0:T(8,128)(2,1)S(1)}, bf16[256,256]{1,0:T(8,128)(2,1)S(1)}, u32[]{:S(2)}, u32[]{:S(2)}) collective-permute-start(bf16[256,256]{1,0:T(8,128)(2,1)S(1)} %get-tuple-element.30), channel_id=1, source_target_pairs={{0,2},{1,3},{2,0},{3,1},{4,6},{5,7},{6,4},{7,5},{8,10},{9,11},{10,... | collective-permute-start | bytes 393224 | tf_op jit(solution)/shard_map/ppermute | solution.py:220
  51.9 0.8 %collective-permute-start.16 = (bf16[256,256]{1,0:T(8,128)(2,1)S(1)}, bf16[256,256]{1,0:T(8,128)(2,1)S(1)}, u32[]{:S(2)}, u32[]{:S(2)}) collective-permute-start(bf16[256,256]{1,0:T(8,128)(2,1)S(1)} %get-tuple-element.31), channel_id=1, source_target_pairs={{0,3},{1,2},{2,1},{3,0},{4,7},{5,6},{6,5},{7,4},{8,11},{9,10},{10,... | collective-permute-start | bytes 393224 | tf_op jit(solution)/shard_map/ppermute | solution.py:220
  52.8 0.0 collective-permute-done.6
  52.8 0.0 collective-permute-start.17
  52.8 0.0 collective-permute-done.7
  52.8 1.1 %collective-permute-done.8 = bf16[256,256]{1,0:T(8,128)(2,1)S(1)} collective-permute-done((bf16[256,256]{1,0:T(8,128)(2,1)S(1)}, bf16[256,256]{1,0:T(8,128)(2,1)S(1)}, u32[]{:S(2)}, u32[]{:S(2)}) %collective-permute-start.8) | collective-permute-done | bytes 131104 | tf_op jit(solution)/shard_map/ppermute | solution.py:220
  53.9 0.1 add_convert_fusion.1
  54.0 5.9 %collective-permute-done.15 = bf16[256,256]{1,0:T(8,128)(2,1)S(1)} collective-permute-done((bf16[256,256]{1,0:T(8,128)(2,1)S(1)}, bf16[256,256]{1,0:T(8,128)(2,1)S(1)}, u32[]{:S(2)}, u32[]{:S(2)}) %collective-permute-start.15) | collective-permute-done | bytes 131104 | tf_op jit(solution)/shard_map/ppermute | solution.py:220
  59.9 0.0 collective-permute-done.16
  59.9 0.6 collective-permute-done.17
  60.5 0.1 add_convert_fusion
  60.6 0.8 %reverse_select_fusion = bf16[2,2,128,256]{3,2,1,0:T(8,128)(2,1)} fusion(bf16[2,2,128,256]{3,2,1,0:T(8,128)(2,1)S(1)} %pad_maximum_fusion, pred[]{:T(512)S(6)} %eq.3), kind=kLoop, calls=%fused_computation | loop fusion | flops 131072 | bytes 524289 | tf_op jit(solution)/shard_map/jit(_where)/select_n | solution.py:307
  (13 shorter events, 0.1 us)
Async XLA Ops:
  1.0 5.3 %collective-permute-start = (bf16[1,128,256]{2,1,0:T(8,128)(2,1)S(1)}, bf16[1,128,256]{2,1,0:T(8,128)(2,1)S(1)}, u32[]{:S(2)}, u32[]{:S(2)}) collective-permute-start(bf16[1,128,256]{2,1,0:T(8,128)(2,1)S(1)} %get-tuple-element.36), channel_id=1, source_target_pairs={{0,4},{4,0},{1,5},{5,1},{2,6},{6,2},{3,7},{7,3},{8,12},{12,8},{9,1... | collective-permute-start | bytes 196616 | tf_op jit(solution)/shard_map/ppermute | solution.py:223
  4.1 11.6 %collective-permute-start.9 = (bf16[1,128,256]{2,1,0:T(8,128)(2,1)S(1)}, bf16[1,128,256]{2,1,0:T(8,128)(2,1)S(1)}, u32[]{:S(2)}, u32[]{:S(2)}) collective-permute-start(bf16[1,128,256]{2,1,0:T(8,128)(2,1)S(1)} %get-tuple-element.38), channel_id=1, source_target_pairs={{0,4},{4,0},{1,5},{5,1},{2,6},{6,2},{3,7},{7,3},{8,12},{12,8},{9,1... | collective-permute-start | bytes 196616 | tf_op jit(solution)/shard_map/ppermute | solution.py:223
  6.4 10.9 %collective-permute-start.2 = (bf16[1,256,256]{2,1,0:T(8,128)(2,1)S(1)}, bf16[1,256,256]{2,1,0:T(8,128)(2,1)S(1)}, u32[]{:S(2)}, u32[]{:S(2)}) collective-permute-start(bf16[1,256,256]{2,1,0:T(8,128)(2,1)S(1)} %pad_maximum_fusion.1.own.share), channel_id=1, source_target_pairs={{0,2},{1,3},{2,0},{3,1},{4,6},{5,7},{6,4},{7,5},{8,10},{9,11},{10,... | collective-permute-start | bytes 393224 | tf_op jit(solution)/shard_map/ppermute | solution.py:220
  12.1 14.0 %collective-permute-start.3 = (bf16[1,256,256]{2,1,0:T(8,128)(2,1)S(1)}, bf16[1,256,256]{2,1,0:T(8,128)(2,1)S(1)}, u32[]{:S(2)}, u32[]{:S(2)}) collective-permute-start(bf16[1,256,256]{2,1,0:T(8,128)(2,1)S(1)} %pad_maximum_fusion.1.own.share), channel_id=1, source_target_pairs={{1,2},{2,1},{5,6},{6,5},{9,10},{10,9},{13,14},{14,13},{17,18},{18,... | collective-permute-start | bytes 393224 | tf_op jit(solution)/shard_map/ppermute | solution.py:220
  12.8 14.7 %collective-permute-start.1 = (bf16[1,256,256]{2,1,0:T(8,128)(2,1)S(1)}, bf16[1,256,256]{2,1,0:T(8,128)(2,1)S(1)}, u32[]{:S(2)}, u32[]{:S(2)}) collective-permute-start(bf16[1,256,256]{2,1,0:T(8,128)(2,1)S(1)} %pad_maximum_fusion.1.own.share), channel_id=1, source_target_pairs={{0,1},{1,0},{2,3},{3,2},{4,5},{5,4},{6,7},{7,6},{8,9},{9,8},{10,11... | collective-permute-start | bytes 393224 | tf_op jit(solution)/shard_map/ppermute | solution.py:220
  15.7 9.1 %collective-permute-start.11 = (bf16[1,256,256]{2,1,0:T(8,128)(2,1)S(1)}, bf16[1,256,256]{2,1,0:T(8,128)(2,1)S(1)}, u32[]{:S(2)}, u32[]{:S(2)}) collective-permute-start(bf16[1,256,256]{2,1,0:T(8,128)(2,1)S(1)} %pad_maximum_fusion.2.own.share), channel_id=1, source_target_pairs={{0,2},{1,3},{2,0},{3,1},{4,6},{5,7},{6,4},{7,5},{8,10},{9,11},{10,... | collective-permute-start | bytes 393224 | tf_op jit(solution)/shard_map/ppermute | solution.py:220
  17.2 10.2 %collective-permute-start.4 = (bf16[1,256,256]{2,1,0:T(8,128)(2,1)S(1)}, bf16[1,256,256]{2,1,0:T(8,128)(2,1)S(1)}, u32[]{:S(2)}, u32[]{:S(2)}) collective-permute-start(bf16[1,256,256]{2,1,0:T(8,128)(2,1)S(1)} %collective-permute-done.2.far), channel_id=1, source_target_pairs={{1,0},{2,3},{5,4},{6,7},{9,8},{10,11},{13,12},{14,15},{17,16},{18,... | collective-permute-start | bytes 393224 | tf_op jit(solution)/shard_map/ppermute | solution.py:220
  18.6 17.1 %copy-start.3 = (s32[4]{0:T(128)S(1)}, s32[4]{0:T(128)}, u32[]{:S(2)}) copy-start(s32[4]{0:T(128)} %lengths.7) | copy-start | bytes 52
  18.6 11.0 %collective-permute-start.12 = (bf16[1,256,256]{2,1,0:T(8,128)(2,1)S(1)}, bf16[1,256,256]{2,1,0:T(8,128)(2,1)S(1)}, u32[]{:S(2)}, u32[]{:S(2)}) collective-permute-start(bf16[1,256,256]{2,1,0:T(8,128)(2,1)S(1)} %pad_maximum_fusion.2.own.share), channel_id=1, source_target_pairs={{1,2},{2,1},{5,6},{6,5},{9,10},{10,9},{13,14},{14,13},{17,18},{18,... | collective-permute-start | bytes 393224 | tf_op jit(solution)/shard_map/ppermute | solution.py:220
  24.8 5.0 %collective-permute-start.10 = (bf16[1,256,256]{2,1,0:T(8,128)(2,1)S(1)}, bf16[1,256,256]{2,1,0:T(8,128)(2,1)S(1)}, u32[]{:S(2)}, u32[]{:S(2)}) collective-permute-start(bf16[1,256,256]{2,1,0:T(8,128)(2,1)S(1)} %pad_maximum_fusion.2.own.share), channel_id=1, source_target_pairs={{0,1},{1,0},{2,3},{3,2},{4,5},{5,4},{6,7},{7,6},{8,9},{9,8},{10,11... | collective-permute-start | bytes 393224 | tf_op jit(solution)/shard_map/ppermute | solution.py:220
  26.1 6.9 %collective-permute-start.13 = (bf16[1,256,256]{2,1,0:T(8,128)(2,1)S(1)}, bf16[1,256,256]{2,1,0:T(8,128)(2,1)S(1)}, u32[]{:S(2)}, u32[]{:S(2)}) collective-permute-start(bf16[1,256,256]{2,1,0:T(8,128)(2,1)S(1)} %collective-permute-done.11.far), channel_id=1, source_target_pairs={{1,0},{2,3},{5,4},{6,7},{9,8},{10,11},{13,12},{14,15},{17,16},{18,... | collective-permute-start | bytes 393224 | tf_op jit(solution)/shard_map/ppermute | solution.py:220
  29.0 6.7 %copy-start.1 = (bf16[2,256,256]{2,1,0:T(8,128)(2,1)}, bf16[2,256,256]{2,1,0:T(8,128)(2,1)S(1)}, u32[]{:S(2)}) copy-start(bf16[2,256,256]{2,1,0:T(8,128)(2,1)S(1)} %get-tuple-element.21.refs_0_) | copy-start | bytes 786436
  29.0 8.8 %copy-start = (bf16[256,1024]{1,0:T(8,128)(2,1)S(1)}, bf16[256,1024]{1,0:T(8,128)(2,1)}, u32[]{:S(2)}) copy-start(bf16[256,1024]{1,0:T(8,128)(2,1)} %weight.3) | copy-start | bytes 1572868
  29.1 8.8 %collective-permute-start.5 = (bf16[2,256,256]{2,1,0:T(8,128)(2,1)S(1)}, bf16[2,256,256]{2,1,0:T(8,128)(2,1)S(1)}, u32[]{:S(2)}, u32[]{:S(2)}) collective-permute-start(bf16[2,256,256]{2,1,0:T(8,128)(2,1)S(1)} %get-tuple-element.21.refs_0_), channel_id=1, source_target_pairs={{0,4},{4,0},{1,5},{5,1},{2,6},{6,2},{3,7},{7,3},{8,12},{12,8},{9,1... | collective-permute-start | bytes 786440 | tf_op jit(solution)/shard_map/ppermute | solution.py:223
  35.3 11.4 %collective-permute-start.14 = (bf16[2,256,256]{2,1,0:T(8,128)(2,1)}, bf16[2,256,256]{2,1,0:T(8,128)(2,1)S(1)}, u32[]{:S(2)}, u32[]{:S(2)}) collective-permute-start(bf16[2,256,256]{2,1,0:T(8,128)(2,1)} %get-tuple-element.27.refs_2_), channel_id=1, source_target_pairs={{0,4},{4,0},{1,5},{5,1},{2,6},{6,2},{3,7},{7,3},{8,12},{12,8},{9,1... | collective-permute-start | bytes 786440 | tf_op jit(solution)/shard_map/ppermute | solution.py:223
  39.5 13.3 %collective-permute-start.6 = (bf16[256,256]{1,0:T(8,128)(2,1)S(1)}, bf16[256,256]{1,0:T(8,128)(2,1)S(1)}, u32[]{:S(2)}, u32[]{:S(2)}) collective-permute-start(bf16[256,256]{1,0:T(8,128)(2,1)S(1)} %get-tuple-element.24), channel_id=1, source_target_pairs={{0,2},{1,3},{2,0},{3,1},{4,6},{5,7},{6,4},{7,5},{8,10},{9,11},{10,... | collective-permute-start | bytes 393224 | tf_op jit(solution)/shard_map/ppermute | solution.py:220
  42.9 9.9 %collective-permute-start.7 = (bf16[256,256]{1,0:T(8,128)(2,1)S(1)}, bf16[256,256]{1,0:T(8,128)(2,1)S(1)}, u32[]{:S(2)}, u32[]{:S(2)}) collective-permute-start(bf16[256,256]{1,0:T(8,128)(2,1)S(1)} %get-tuple-element.25), channel_id=1, source_target_pairs={{0,3},{1,2},{2,1},{3,0},{4,7},{5,6},{6,5},{7,4},{8,11},{9,10},{10,... | collective-permute-start | bytes 393224 | tf_op jit(solution)/shard_map/ppermute | solution.py:220
  43.7 10.2 %collective-permute-start.8 = (bf16[256,256]{1,0:T(8,128)(2,1)S(1)}, bf16[256,256]{1,0:T(8,128)(2,1)S(1)}, u32[]{:S(2)}, u32[]{:S(2)}) collective-permute-start(bf16[256,256]{1,0:T(8,128)(2,1)S(1)} %get-tuple-element.26), channel_id=1, source_target_pairs={{0,1},{1,0},{2,3},{3,2},{4,5},{5,4},{6,7},{7,6},{8,9},{9,8},{10,11... | collective-permute-start | bytes 393224 | tf_op jit(solution)/shard_map/ppermute | solution.py:220
  43.7 1.0 %copy-start.2 = (bf16[2,256,256]{2,1,0:T(8,128)(2,1)S(1)}, bf16[2,256,256]{2,1,0:T(8,128)(2,1)}, u32[]{:S(2)}) copy-start(bf16[2,256,256]{2,1,0:T(8,128)(2,1)} %copy-done.1) | copy-start | bytes 786436
  48.3 11.6 %collective-permute-start.15 = (bf16[256,256]{1,0:T(8,128)(2,1)S(1)}, bf16[256,256]{1,0:T(8,128)(2,1)S(1)}, u32[]{:S(2)}, u32[]{:S(2)}) collective-permute-start(bf16[256,256]{1,0:T(8,128)(2,1)S(1)} %get-tuple-element.30), channel_id=1, source_target_pairs={{0,2},{1,3},{2,0},{3,1},{4,6},{5,7},{6,4},{7,5},{8,10},{9,11},{10,... | collective-permute-start | bytes 393224 | tf_op jit(solution)/shard_map/ppermute | solution.py:220
  51.9 8.0 %collective-permute-start.16 = (bf16[256,256]{1,0:T(8,128)(2,1)S(1)}, bf16[256,256]{1,0:T(8,128)(2,1)S(1)}, u32[]{:S(2)}, u32[]{:S(2)}) collective-permute-start(bf16[256,256]{1,0:T(8,128)(2,1)S(1)} %get-tuple-element.31), channel_id=1, source_target_pairs={{0,3},{1,2},{2,1},{3,0},{4,7},{5,6},{6,5},{7,4},{8,11},{9,10},{10,... | collective-permute-start | bytes 393224 | tf_op jit(solution)/shard_map/ppermute | solution.py:220
  52.8 7.7 %collective-permute-start.17 = (bf16[256,256]{1,0:T(8,128)(2,1)S(1)}, bf16[256,256]{1,0:T(8,128)(2,1)S(1)}, u32[]{:S(2)}, u32[]{:S(2)}) collective-permute-start(bf16[256,256]{1,0:T(8,128)(2,1)S(1)} %get-tuple-element.32), channel_id=1, source_target_pairs={{0,1},{1,0},{2,3},{3,2},{4,5},{5,4},{6,7},{7,6},{8,9},{9,8},{10,11... | collective-permute-start | bytes 393224 | tf_op jit(solution)/shard_map/ppermute | solution.py:220

commit v4 on v3

--- a/solution.py
+++ b/solution.py
@@ -10,7 +10,8 @@
 
 
 HDIM = 128
-GRANT = 16 << 20
+GRANT = 8 << 20
+GA, GB, RA, RB = ('spread', 'halving', 'halving', 'direct')
 F32 = jnp.float32
 BF16 = jnp.bfloat16
 
@@ -114,9 +115,11 @@
     return half + half * jnp.tanh(half)
 
 
-def project_kernel(place, own, near, far, mid, relay, weight, keyval, gateq):
-    pieces = [own[0].astype(F32), near[0].astype(F32), far[0].astype(F32)]
-    pieces.append(mid[0].astype(F32) + relay[0].astype(F32))
+def project_kernel(ids, place, *refs):
+    *shares, weight, keyval, gateq = refs
+    pieces = [ref[k].astype(F32) for ref in shares for k in range(ref.shape[0])]
+    if len(pieces) > len(ids):
+        pieces[-2:] = [pieces[-2] + pieces[-1]]
     part = pieces[0].shape[1]
     width = part * len(pieces)
     mean = sum(jnp.sum(p, axis=1, keepdims=True) for p in pieces) / width
@@ -124,7 +127,7 @@
     spread = sum(jnp.sum(p * p, axis=1, keepdims=True) for p in pieces) / width
     rscale = lax.rsqrt(spread + 1e-06)
     acc = None
-    for share_id, piece in enumerate(pieces):
+    for share_id, piece in zip(ids, pieces):
         lead = pl.multiple_of((place[1] ^ share_id) * part, part)
         term = jnp.dot(
             (piece * rscale).astype(BF16), weight[pl.ds(lead, part), :], preferred_element_type=F32
@@ -144,9 +147,10 @@
 
     def positions(shape, dim, which, side):
         offset = lax.broadcasted_iota(jnp.int32, shape, dim)
-        block = side if which == 0 else 3 - side
+        if which == 0:
+            return offset + side * stripe + jnp.where(offset < stripe, 0, stripe)
         inner = jnp.where(offset < stripe, offset + side * stripe, offset - side * stripe)
-        return block * rows + inner
+        return (3 - side) * rows + inner
 
     query_pos = positions((rows, 1), 0, chunk, place[0])
     start = jnp.zeros((rows, 1), jnp.int32)
@@ -182,8 +186,9 @@
         partial[:, head * HDIM : (head + 1) * HDIM] = total
 
 
-def attend_kernel(plan, place, lengths, keyval, partial, gateq, weight, share, *refs):
+def attend_kernel(plan, layout, place, lengths, keyval, partial, gateq, weight, share, *refs):
     *outputs, held = refs
+    chunk, stripe, _ = plan
     part = share.shape[2]
     totals = weighted_values(plan, place, lengths, gateq, [keyval], partial)
     for head, total in enumerate(totals):
@@ -192,13 +197,25 @@
         spread = jnp.mean(total * total, axis=1, keepdims=True)
         total = total * lax.rsqrt(spread + 1e-05)
         held[:, lanes] = (total * gateq[0, :, lanes].astype(F32)).astype(BF16)
-    gated = held[...]
-    for share_id in (2, 3, 1, 0):
-        lead = pl.multiple_of((place[1] ^ share_id) * part, part)
-        product = jnp.dot(gated, weight[:, pl.ds(lead, part)], preferred_element_type=F32)
-        if share_id == 0:
-            product = product + share[0].astype(F32)
-        outputs[share_id][...] = product.astype(outputs[share_id].dtype)
+    leads = [0, stripe]
+    if chunk == 0:
+        away = 1 - place[0]
+        leads = [pl.multiple_of(away * stripe, stripe), pl.multiple_of((1 - away) * stripe, stripe)]
+    gated = [held[pl.ds(lead, stripe), :] for lead in leads]
+    shares = [share[0, pl.ds(lead, stripe), :] for lead in leads]
+    if layout != "split":
+        gated, shares = [jnp.concatenate(gated, axis=0)], [jnp.concatenate(shares, axis=0)]
+    for index, (left, right) in enumerate(zip(gated, shares)):
+        for share_id in (2, 3, 1, 0):
+            lead = pl.multiple_of((place[1] ^ share_id) * part, part)
+            product = jnp.dot(left, weight[:, pl.ds(lead, part)], preferred_element_type=F32)
+            if share_id == 0:
+                product = product + right.astype(F32)
+            if layout == "direct":
+                outputs[share_id][...] = product.astype(outputs[share_id].dtype)
+            else:
+                target = outputs[2 * index + 1 - (share_id & 1)]
+                target[share_id >> 1] = product.astype(target.dtype)
 
 
 def whole(memory_space=pltpu.VMEM):
@@ -240,27 +257,26 @@
     inner = [(1, 2), (2, 1)]
     outer = [(1, 0), (2, 3)]
 
-    def settle(chunk):
-        stay = own if chunk == 0 else 1 - own
-        blocks = inputs[chunk * 2 : chunk * 2 + 2]
-        home = lax.dynamic_index_in_dim(blocks, stay, 0, keepdims=True)
-        away = lax.dynamic_index_in_dim(blocks, 1 - stay, 0, keepdims=True)
-        return jnp.concatenate([home, over_ctx(away)], axis=1)
-
-    def gather(own_share, tag):
+    def gather(own_share, tag, way):
         far = over_head(own_share, 2)
+        if tag == "a":
+            after, weight = lax.optimization_barrier((far, weight_in))
+            weights.append(weight)
+        else:
+            after = far
+        if way == "halving":
+            both = jnp.concatenate([own_share, after], axis=0)
+            return (own_share, far, over_head(both, 1)), (0, 2, 1, 3)
         near = over_head(own_share, 1)
         mid = over_head(own_share, inner)
-        if tag == "a":
-            far, weight = lax.optimization_barrier((far, weight_in))
-            weights.append(weight)
-        relay = over_head(far, outer)
-        return own_share, near, far, mid, relay
-
-    def project(shares):
+        relay = over_head(after, outer)
+        return (own_share, near, far, mid, relay), (0, 1, 2, 3)
+
+    def project(gathered):
+        shares, ids = gathered
         size = ((2, rows, cols), BF16)
         return kernel_call(
-            project_kernel,
+            functools.partial(project_kernel, ids),
             (size, size),
             (place, *shares, weights[0]),
             1,
@@ -277,33 +293,51 @@
             cost(4 * rows * rows * cols * count, rows * rows * count * (cols // HDIM)),
         )[0]
 
-    def attend(chunk, keyval, partial, gateq, share):
-        size = (rows, part)
-        return kernel_call(
-            functools.partial(attend_kernel, (chunk, stripe, [(chunk, 1)])),
-            ((size, F32),) + ((size, BF16),) * 3,
+    def attend(chunk, keyval, partial, gateq, share, layout):
+        size = {"direct": (rows, part), "halving": (2, rows, part), "split": (2, stripe, part)}[layout]
+        outs = ((size, BF16), (size, F32))
+        outs = {
+            "direct": (outs[1],) + outs[:1] * 3,
+            "halving": outs,
+            "split": outs * 2,
+        }[layout]
+        results = kernel_call(
+            functools.partial(attend_kernel, (chunk, stripe, [(chunk, 1)]), layout),
+            outs,
             (place, lengths, keyval, partial, gateq, proj_out, share),
             2,
             cost(4 * rows * rows * cols + 2 * rows * proj_out.size, rows * rows * (cols // HDIM)),
             [pltpu.VMEM((rows, cols), BF16)],
         )
-
-    def total(kept, *sent):
-        for share_id in (2, 3, 1):
-            kept = kept + over_head(sent[share_id - 1], share_id).astype(F32)
-        return kept.astype(BF16)
-
-    shares = [settle(0), settle(1)]
-    low_keyval, low_gateq = project(gather(shares[0], "a"))
+        if layout == "direct":
+            kept = results[0]
+            for share_id in (2, 3, 1):
+                come = over_head(results[share_id], share_id)
+                kept = kept + come.astype(F32)
+            return kept.astype(BF16)
+        done = []
+        for index in range(len(results) // 2):
+            sent, kept = results[2 * index : 2 * index + 2]
+            kept = kept + over_head(sent, 1).astype(F32)
+            come = over_head(kept[1].astype(BF16), 2)
+            done.append((kept[0] + come.astype(F32)).astype(BF16))
+        return done[0] if len(done) == 1 else jnp.concatenate(done, axis=0)
+
+    low = inputs[:2].reshape(1, rows, part)
+    home = lax.dynamic_index_in_dim(inputs[2:], 1 - own, 0, keepdims=True)
+    away = lax.dynamic_index_in_dim(inputs[2:], own, 0, keepdims=True)
+    high = jnp.concatenate([home, over_ctx(away)], axis=1)
+    low_keyval, low_gateq = project(gather(low, "a", GA))
     low_other = over_ctx(low_keyval)
-    high_keyval, high_gateq = project(gather(shares[1], "b"))
+    high_keyval, high_gateq = project(gather(high, "b", GB))
     high_other = over_ctx(high_keyval)
     low_first = near_part(0, [(0, 0)], [low_keyval], low_gateq)
-    low_done = total(*attend(0, low_other, low_first, low_gateq, shares[0]))
+    low_done = attend(0, low_other, low_first, low_gateq, low, RA)
     origins = [(0, 0), (0, 1), (1, 0)]
     high_first = near_part(1, origins, [low_keyval, low_other, high_keyval], high_gateq)
-    high_done = total(*attend(1, high_other, high_first, high_gateq, shares[1]))
-    both = jnp.stack([low_done, high_done]).reshape(2, 2, stripe, part)
+    high_done = attend(1, high_other, high_first, high_gateq, high, RB)
+    come = over_ctx(low_done[:stripe])
+    both = jnp.concatenate([low_done[stripe:], come, high_done], axis=0).reshape(2, 2, stripe, part)
     return jnp.where(own == 0, both, both[:, ::-1]).reshape(1, 2, rows, part)
 
 

time: 61.6 us -> 56.7 us (0.920)
  waiting for transfers between devices: 19.7 us -> 15.4 us
  starting transfers between devices: 26.2 us -> 27.6 us
  Pallas kernels: 10.2 us -> 9.13 us
  local copies, waits for them, and re-layouts: 4.05 us -> 3.12 us
    ppermute x14 -> x11, waiting for transfers between devices: 16.5 us -> 12.3 us  [over_head(): return lax.ppermute(value, 'head', pairs)]
    ppermute x4, starting transfers between devices: 4.07 us -> 6.8 us  [over_ctx(): return lax.ppermute(value, 'ctx', [(0, 1), (1, 0)])]
    ppermute x14 -> x11, starting transfers between devices: 22.2 us -> 20.8 us  [over_head(): return lax.ppermute(value, 'head', pairs)]
    pallas_call x6, Pallas kernels: 10.2 us -> 9.13 us  [kernel_call(): pl.pallas_call(function, compiler_params=pltpu.CompilerParams(vmem_limit_...]
    unnamed x9 -> x5, local copies, waits for them, and re-layouts: 3.04 us -> 2.1 us
  transfers between devices with their start and end apart: 18 -> 15, of which waited for: 8 -> 6; matrix products, arithmetic and copies ran while one was open for 4% -> 4% of each run, Pallas kernels for 17% -> 16%
where the time goes in v4:
time: 56.7 us; the launch traced here: 56.5 us
  starting transfers between devices  27.6 us (49%)
  waiting for transfers between devices  15.4 us (27%)
  Pallas kernels  9.13 us (16%)
  local copies, waits for them, and re-layouts  3.12 us (6%)
  other arithmetic  1.04 us (2%)
    ppermute x11, starting transfers between devices, over_head(): return lax.ppermute(value, 'head', pairs)  20.8 us
    ppermute x11, waiting for transfers between devices, over_head(): return lax.ppermute(value, 'head', pairs)  12.3 us
    pallas_call x6, Pallas kernels, kernel_call(): pl.pallas_call(function, compiler_params=pltpu.CompilerParams(vmem_limit_...  9.13 us
    ppermute x4, starting transfers between devices, over_ctx(): return lax.ppermute(value, 'ctx', [(0, 1), (1, 0)])  6.8 us
    ppermute x4, waiting for transfers between devices, over_ctx(): return lax.ppermute(value, 'ctx', [(0, 1), (1, 0)])  3.09 us
    unnamed x5, local copies, waits for them, and re-layouts  2.1 us
  transfers between devices with their start and end apart: 15, of which 6 were waited for; matrix products, arithmetic and copies ran while one was open for 4% of the time, Pallas kernels for 16%

profile of v4, /device:TPU:0, one launch (start us, length us, event | category | flops | bytes accessed | tf_op | source)
XLA Modules:
  0.0 56.5 jit_solution(9896521333229432007)
XLA Ops:
  0.0 1.0 %fusion.3 = (bf16[2,128,256]{2,1,0:T(8,128)(2,1)S(1)}, bf16[2,128,256]{2,1,0:T(8,128)(2,1)S(1)}) fusion(bf16[4,128,256]{2,1,0:T(8,128)(2,1)} %param.4), kind=kLoop, calls=%fused_computation.14 | loop fusion | bytes 524288 | tf_op jit(solution)/shard_map/slice | solution.py:326
  1.0 4.1 %collective-permute-start.1 = (bf16[1,256,256]{2,1,0:T(8,128)(2,1)S(1)}, bf16[1,256,256]{2,1,0:T(8,128)(2,1)S(1)}, u32[]{:S(2)}, u32[]{:S(2)}) collective-permute-start(bf16[1,256,256]{2,1,0:T(8,128)(2,1)S(1)} %bitcast.17), channel_id=1, source_target_pairs={{0,2},{1,3},{2,0},{3,1},{4,6},{5,7},{6,4},{7,5},{8,10},{9,11},{10,... | collective-permute-start | bytes 393224 | tf_op jit(solution)/shard_map/ppermute | solution.py:237
  5.1 0.7 %collective-permute-start.2 = (bf16[1,256,256]{2,1,0:T(8,128)(2,1)S(1)}, bf16[1,256,256]{2,1,0:T(8,128)(2,1)S(1)}, u32[]{:S(2)}, u32[]{:S(2)}) collective-permute-start(bf16[1,256,256]{2,1,0:T(8,128)(2,1)S(1)} %bitcast.18), channel_id=1, source_target_pairs={{1,2},{2,1},{5,6},{6,5},{9,10},{10,9},{13,14},{14,13},{17,18},{18,... | collective-permute-start | bytes 393224 | tf_op jit(solution)/shard_map/ppermute | solution.py:237
  5.8 2.9 %collective-permute-start = (bf16[1,256,256]{2,1,0:T(8,128)(2,1)S(1)}, bf16[1,256,256]{2,1,0:T(8,128)(2,1)S(1)}, u32[]{:S(2)}, u32[]{:S(2)}) collective-permute-start(bf16[1,256,256]{2,1,0:T(8,128)(2,1)S(1)} %bitcast.19), channel_id=1, source_target_pairs={{0,1},{1,0},{2,3},{3,2},{4,5},{5,4},{6,7},{7,6},{8,9},{9,8},{10,11... | collective-permute-start | bytes 393224 | tf_op jit(solution)/shard_map/ppermute | solution.py:237
  8.7 1.6 %collective-permute-start.8 = (bf16[1,128,256]{2,1,0:T(8,128)(2,1)S(1)}, bf16[1,128,256]{2,1,0:T(8,128)(2,1)S(1)}, u32[]{:S(2)}, u32[]{:S(2)}) collective-permute-start(bf16[1,128,256]{2,1,0:T(8,128)(2,1)S(1)} %get-tuple-element.34), channel_id=1, source_target_pairs={{0,4},{4,0},{1,5},{5,1},{2,6},{6,2},{3,7},{7,3},{8,12},{12,8},{9,1... | collective-permute-start | bytes 196616 | tf_op jit(solution)/shard_map/ppermute | solution.py:240
  10.3 2.1 %copy.5 = bf16[128,8,4,256]{3,1,2,0:T(8,128)(2,1)S(1)} copy(bf16[128,8,4,256]{3,2,1,0:T(4,128)(2,1)} %bitcast.22) | data formatting | bytes 4194304
  12.4 0.0 copy-start.1
  12.4 0.0 collective-permute-done.1.refs_2_
  12.4 1.3 %collective-permute-start.3 = (bf16[1,256,256]{2,1,0:T(8,128)(2,1)S(1)}, bf16[1,256,256]{2,1,0:T(8,128)(2,1)S(1)}, u32[]{:S(2)}, u32[]{:S(2)}) collective-permute-start(bf16[1,256,256]{2,1,0:T(8,128)(2,1)S(1)} %collective-permute-done.1.refs_2_), channel_id=1, source_target_pairs={{1,0},{2,3},{5,4},{6,7},{9,8},{10,11},{13,12},{14,15},{17,16},{18,... | collective-permute-start | bytes 393224 | tf_op jit(solution)/shard_map/ppermute | solution.py:237
  13.7 0.1 pad_add_fusion.place
  13.8 0.0 collective-permute-done.8
  13.8 0.0 copy-start
  13.8 4.2 %collective-permute-start.9 = (bf16[1,256,256]{2,1,0:T(8,128)(2,1)S(1)}, bf16[1,256,256]{2,1,0:T(8,128)(2,1)S(1)}, u32[]{:S(2)}, u32[]{:S(2)}) collective-permute-start(bf16[1,256,256]{2,1,0:T(8,128)(2,1)S(1)} %pad_maximum_fusion.2.refs_0_.share), channel_id=1, source_target_pairs={{0,2},{1,3},{2,0},{3,1},{4,6},{5,7},{6,4},{7,5},{8,10},{9,11},{10,... | collective-permute-start | bytes 393224 | tf_op jit(solution)/shard_map/ppermute | solution.py:237
  18.0 0.0 collective-permute-done.2.refs_3_
  18.0 0.0 collective-permute-done.refs_1_
  18.0 1.4 %collective-permute-done.3.refs_4_ = bf16[1,256,256]{2,1,0:T(8,128)(2,1)S(1)} collective-permute-done((bf16[1,256,256]{2,1,0:T(8,128)(2,1)S(1)}, bf16[1,256,256]{2,1,0:T(8,128)(2,1)S(1)}, u32[]{:S(2)}, u32[]{:S(2)}) %collective-permute-start.3) | collective-permute-done | bytes 131104 | tf_op jit(solution)/shard_map/ppermute | solution.py:237
  19.3 1.6 %shard_map.46 = (bf16[2,256,256]{2,1,0:T(8,128)(2,1)S(1)}, bf16[2,256,256]{2,1,0:T(8,128)(2,1)S(1)}) custom-call(s32[2]{0:T(128)S(1)} %pad_add_fusion.place, bf16[1,256,256]{2,1,0:T(8,128)(2,1)S(1)} %bitcast.20, bf16[1,256,256]{2,1,0:T(8,128)(2,1)S(1)} %collective-permute-done.refs_1_, bf16[1,256,256]{2,1,0:T(8,128)(2,1)S(1)} %collective-permute-done.1.refs_2_, ...), custom_call_target="tpu_custom_call" | custom-call | flops 536870912 | bytes 1048576 | tf_op jit(solution)/shard_map/pallas_call | solution.py:243
  20.9 3.6 %collective-permute-start.4 = (bf16[2,256,256]{2,1,0:T(8,128)(2,1)S(1)}, bf16[2,256,256]{2,1,0:T(8,128)(2,1)S(1)}, u32[]{:S(2)}, u32[]{:S(2)}) collective-permute-start(bf16[2,256,256]{2,1,0:T(8,128)(2,1)S(1)} %get-tuple-element.19.refs_0_), channel_id=1, source_target_pairs={{0,4},{4,0},{1,5},{5,1},{2,6},{6,2},{3,7},{7,3},{8,12},{12,8},{9,1... | collective-permute-start | bytes 786440 | tf_op jit(solution)/shard_map/ppermute | solution.py:240
  24.5 0.0 collective-permute-done.9.refs_1_
  24.5 0.1 collective-permute-start.10
  24.6 0.0 copy-done.1
  24.6 1.1 %shard_map.47.partial = f32[256,256]{1,0:T(8,128)S(1)} custom-call(s32[2]{0:T(128)S(1)} %pad_add_fusion.place, s32[4]{0:T(128)S(1)} %copy-done.1, bf16[2,256,256]{2,1,0:T(8,128)(2,1)S(1)} %get-tuple-element.19.refs_0_, bf16[2,256,256]{2,1,0:T(8,128)(2,1)S(1)} %get-tuple-element.20.refs_1_.gateq), custom_call_target="tpu_custom_call" | custom-call | flops 67108864 | bytes 1048576 | tf_op jit(solution)/shard_map/pallas_call | solution.py:243
  25.8 3.1 %collective-permute-done.4.keyval.refs_1_ = bf16[2,256,256]{2,1,0:T(8,128)(2,1)S(1)} collective-permute-done((bf16[2,256,256]{2,1,0:T(8,128)(2,1)S(1)}, bf16[2,256,256]{2,1,0:T(8,128)(2,1)S(1)}, u32[]{:S(2)}, u32[]{:S(2)}) %collective-permute-start.4) | collective-permute-done | bytes 262176 | tf_op jit(solution)/shard_map/ppermute | solution.py:240
  28.9 0.0 copy-done
  28.9 1.6 %shard_map.48 = (bf16[2,256,256]{2,1,0:T(8,128)(2,1)S(1)}, f32[2,256,256]{2,1,0:T(8,128)S(1)}) custom-call(s32[2]{0:T(128)S(1)} %pad_add_fusion.place, s32[4]{0:T(128)S(1)} %copy-done.1, bf16[2,256,256]{2,1,0:T(8,128)(2,1)S(1)} %collective-permute-done.4.keyval.refs_1_, f32[256,256]{1,0:T(8,128)S(1)} %shard_map.47.partial, ...), custom_call_target="tpu_custom_call" | custom-call | flops 201326592 | bytes 1048576 | tf_op jit(solution)/shard_map/pallas_call | solution.py:243
  30.5 0.1 collective-permute-start.5
  30.5 3.2 %collective-permute-done.10.refs_2_ = bf16[2,256,256]{2,1,0:T(8,128)(2,1)S(1)} collective-permute-done((bf16[2,256,256]{2,1,0:T(8,128)(2,1)S(1)}, bf16[2,256,256]{2,1,0:T(8,128)(2,1)S(1)}, u32[]{:S(2)}, u32[]{:S(2)}) %collective-permute-start.10) | collective-permute-done | bytes 262176 | tf_op jit(solution)/shard_map/ppermute | solution.py:237
  33.8 1.6 %shard_map.49 = (bf16[2,256,256]{2,1,0:T(8,128)(2,1)S(1)}, bf16[2,256,256]{2,1,0:T(8,128)(2,1)S(1)}) custom-call(s32[2]{0:T(128)S(1)} %pad_add_fusion.place, bf16[1,256,256]{2,1,0:T(8,128)(2,1)S(1)} %pad_maximum_fusion.2.refs_0_.share, bf16[1,256,256]{2,1,0:T(8,128)(2,1)S(1)} %collective-permute-done.9.refs_1_, ...), custom_call_target="tpu_custom_call" | custom-call | flops 536870912 | bytes 1048576 | tf_op jit(solution)/shard_map/pallas_call | solution.py:243
  35.4 0.1 collective-permute-start.11
  35.5 2.2 %collective-permute-done.5 = bf16[2,256,256]{2,1,0:T(8,128)(2,1)S(1)} collective-permute-done((bf16[2,256,256]{2,1,0:T(8,128)(2,1)S(1)}, bf16[2,256,256]{2,1,0:T(8,128)(2,1)S(1)}, u32[]{:S(2)}, u32[]{:S(2)}) %collective-permute-start.5) | collective-permute-done | bytes 262176 | tf_op jit(solution)/shard_map/ppermute | solution.py:237
  37.7 0.1 convert_add_fusion
  37.8 3.3 %collective-permute-start.6 = (bf16[256,256]{1,0:T(8,128)(2,1)S(1)}, bf16[256,256]{1,0:T(8,128)(2,1)S(1)}, u32[]{:S(2)}, u32[]{:S(2)}) collective-permute-start(bf16[256,256]{1,0:T(8,128)(2,1)S(1)} %fusion.2), channel_id=1, source_target_pairs={{0,2},{1,3},{2,0},{3,1},{4,6},{5,7},{6,4},{7,5},{8,10},{9,11},{10,... | collective-permute-start | bytes 393224 | tf_op jit(solution)/shard_map/ppermute | solution.py:237
  41.1 1.7 %shard_map.50.partial = f32[256,256]{1,0:T(8,128)S(1)} custom-call(s32[2]{0:T(128)S(1)} %pad_add_fusion.place, s32[4]{0:T(128)S(1)} %copy-done.1, bf16[2,256,256]{2,1,0:T(8,128)(2,1)S(1)} %get-tuple-element.19.refs_0_, bf16[2,256,256]{2,1,0:T(8,128)(2,1)S(1)} %collective-permute-done.4.keyval.refs_1_, bf16[2,256,256]{2,1,0:T(8,128)(2,1)S(1)} %get-tuple-element.23.refs_2_, ...), custom_call_target="tpu_custom_call" | custom-call | flops 201326592 | bytes 1048576 | tf_op jit(solution)/shard_map/pallas_call | solution.py:243
  42.8 0.0 collective-permute-done.11.keyval
  42.8 1.6 %shard_map.51 = (f32[256,256]{1,0:T(8,128)S(1)}, bf16[256,256]{1,0:T(8,128)(2,1)S(1)}, bf16[256,256]{1,0:T(8,128)(2,1)S(1)}, bf16[256,256]{1,0:T(8,128)(2,1)S(1)}) custom-call(s32[2]{0:T(128)S(1)} %pad_add_fusion.place, s32[4]{0:T(128)S(1)} %copy-done.1, bf16[2,256,256]{2,1,0:T(8,128)(2,1)S(1)} %collective-permute-done.11.keyval, ...), custom_call_target="tpu_custom_call" | custom-call | flops 201326592 | bytes 1048576 | tf_op jit(solution)/shard_map/pallas_call | solution.py:243
  44.4 1.4 %collective-permute-start.12 = (bf16[256,256]{1,0:T(8,128)(2,1)S(1)}, bf16[256,256]{1,0:T(8,128)(2,1)S(1)}, u32[]{:S(2)}, u32[]{:S(2)}) collective-permute-start(bf16[256,256]{1,0:T(8,128)(2,1)S(1)} %get-tuple-element.26), channel_id=1, source_target_pairs={{0,2},{1,3},{2,0},{3,1},{4,6},{5,7},{6,4},{7,5},{8,10},{9,11},{10,... | collective-permute-start | bytes 393224 | tf_op jit(solution)/shard_map/ppermute | solution.py:237
  45.8 2.8 %collective-permute-start.13 = (bf16[256,256]{1,0:T(8,128)(2,1)S(1)}, bf16[256,256]{1,0:T(8,128)(2,1)S(1)}, u32[]{:S(2)}, u32[]{:S(2)}) collective-permute-start(bf16[256,256]{1,0:T(8,128)(2,1)S(1)} %get-tuple-element.27), channel_id=1, source_target_pairs={{0,3},{1,2},{2,1},{3,0},{4,7},{5,6},{6,5},{7,4},{8,11},{9,10},{10,... | collective-permute-start | bytes 393224 | tf_op jit(solution)/shard_map/ppermute | solution.py:237
  48.6 0.0 collective-permute-start.14
  48.6 0.0 collective-permute-done.6
  48.6 1.6 %collective-permute-start.7 = (bf16[128,256]{1,0:T(8,128)(2,1)S(1)}, bf16[128,256]{1,0:T(8,128)(2,1)S(1)}, u32[]{:S(2)}, u32[]{:S(2)}) collective-permute-start(bf16[128,256]{1,0:T(8,128)(2,1)S(1)} %get-tuple-element.32), channel_id=1, source_target_pairs={{0,4},{4,0},{1,5},{5,1},{2,6},{6,2},{3,7},{7,3},{8,12},{12,8},{9,1... | collective-permute-start | bytes 196616 | tf_op jit(solution)/shard_map/ppermute | solution.py:240
  50.2 5.1 %collective-permute-done.12 = bf16[256,256]{1,0:T(8,128)(2,1)S(1)} collective-permute-done((bf16[256,256]{1,0:T(8,128)(2,1)S(1)}, bf16[256,256]{1,0:T(8,128)(2,1)S(1)}, u32[]{:S(2)}, u32[]{:S(2)}) %collective-permute-start.12) | collective-permute-done | bytes 131104 | tf_op jit(solution)/shard_map/ppermute | solution.py:237
  55.3 0.0 collective-permute-done.13
  55.3 0.3 collective-permute-done.14
  55.6 0.1 add_convert_fusion
  55.7 0.0 collective-permute-done.7
  55.7 0.8 %reverse_select_fusion = bf16[2,2,128,256]{3,2,1,0:T(8,128)(2,1)} fusion(bf16[2,2,128,256]{3,2,1,0:T(8,128)(2,1)S(1)} %bitcast.23, pred[]{:T(512)S(6)} %eq.3), kind=kLoop, calls=%fused_computation.1 | loop fusion | flops 131072 | bytes 524289 | tf_op jit(solution)/shard_map/jit(_where)/select_n | solution.py:341
  (7 shorter events, 0.1 us)
Async XLA Ops:
  1.0 11.4 %collective-permute-start.1 = (bf16[1,256,256]{2,1,0:T(8,128)(2,1)S(1)}, bf16[1,256,256]{2,1,0:T(8,128)(2,1)S(1)}, u32[]{:S(2)}, u32[]{:S(2)}) collective-permute-start(bf16[1,256,256]{2,1,0:T(8,128)(2,1)S(1)} %bitcast.17), channel_id=1, source_target_pairs={{0,2},{1,3},{2,0},{3,1},{4,6},{5,7},{6,4},{7,5},{8,10},{9,11},{10,... | collective-permute-start | bytes 393224 | tf_op jit(solution)/shard_map/ppermute | solution.py:237
  5.1 12.8 %collective-permute-start.2 = (bf16[1,256,256]{2,1,0:T(8,128)(2,1)S(1)}, bf16[1,256,256]{2,1,0:T(8,128)(2,1)S(1)}, u32[]{:S(2)}, u32[]{:S(2)}) collective-permute-start(bf16[1,256,256]{2,1,0:T(8,128)(2,1)S(1)} %bitcast.18), channel_id=1, source_target_pairs={{1,2},{2,1},{5,6},{6,5},{9,10},{10,9},{13,14},{14,13},{17,18},{18,... | collective-permute-start | bytes 393224 | tf_op jit(solution)/shard_map/ppermute | solution.py:237
  5.8 12.2 %collective-permute-start = (bf16[1,256,256]{2,1,0:T(8,128)(2,1)S(1)}, bf16[1,256,256]{2,1,0:T(8,128)(2,1)S(1)}, u32[]{:S(2)}, u32[]{:S(2)}) collective-permute-start(bf16[1,256,256]{2,1,0:T(8,128)(2,1)S(1)} %bitcast.19), channel_id=1, source_target_pairs={{0,1},{1,0},{2,3},{3,2},{4,5},{5,4},{6,7},{7,6},{8,9},{9,8},{10,11... | collective-permute-start | bytes 393224 | tf_op jit(solution)/shard_map/ppermute | solution.py:237
  8.7 5.1 %collective-permute-start.8 = (bf16[1,128,256]{2,1,0:T(8,128)(2,1)S(1)}, bf16[1,128,256]{2,1,0:T(8,128)(2,1)S(1)}, u32[]{:S(2)}, u32[]{:S(2)}) collective-permute-start(bf16[1,128,256]{2,1,0:T(8,128)(2,1)S(1)} %get-tuple-element.34), channel_id=1, source_target_pairs={{0,4},{4,0},{1,5},{5,1},{2,6},{6,2},{3,7},{7,3},{8,12},{12,8},{9,1... | collective-permute-start | bytes 196616 | tf_op jit(solution)/shard_map/ppermute | solution.py:240
  12.4 12.3 %copy-start.1 = (s32[4]{0:T(128)S(1)}, s32[4]{0:T(128)}, u32[]{:S(2)}) copy-start(s32[4]{0:T(128)} %lengths.7) | copy-start | bytes 52
  12.4 7.0 %collective-permute-start.3 = (bf16[1,256,256]{2,1,0:T(8,128)(2,1)S(1)}, bf16[1,256,256]{2,1,0:T(8,128)(2,1)S(1)}, u32[]{:S(2)}, u32[]{:S(2)}) collective-permute-start(bf16[1,256,256]{2,1,0:T(8,128)(2,1)S(1)} %collective-permute-done.1.refs_2_), channel_id=1, source_target_pairs={{1,0},{2,3},{5,4},{6,7},{9,8},{10,11},{13,12},{14,15},{17,16},{18,... | collective-permute-start | bytes 393224 | tf_op jit(solution)/shard_map/ppermute | solution.py:237
  13.8 15.1 %copy-start = (bf16[256,1024]{1,0:T(8,128)(2,1)S(1)}, bf16[256,1024]{1,0:T(8,128)(2,1)}, u32[]{:S(2)}) copy-start(bf16[256,1024]{1,0:T(8,128)(2,1)} %weight.3) | copy-start | bytes 1572868
  13.8 10.7 %collective-permute-start.9 = (bf16[1,256,256]{2,1,0:T(8,128)(2,1)S(1)}, bf16[1,256,256]{2,1,0:T(8,128)(2,1)S(1)}, u32[]{:S(2)}, u32[]{:S(2)}) collective-permute-start(bf16[1,256,256]{2,1,0:T(8,128)(2,1)S(1)} %pad_maximum_fusion.2.refs_0_.share), channel_id=1, source_target_pairs={{0,2},{1,3},{2,0},{3,1},{4,6},{5,7},{6,4},{7,5},{8,10},{9,11},{10,... | collective-permute-start | bytes 393224 | tf_op jit(solution)/shard_map/ppermute | solution.py:237
  20.9 7.9 %collective-permute-start.4 = (bf16[2,256,256]{2,1,0:T(8,128)(2,1)S(1)}, bf16[2,256,256]{2,1,0:T(8,128)(2,1)S(1)}, u32[]{:S(2)}, u32[]{:S(2)}) collective-permute-start(bf16[2,256,256]{2,1,0:T(8,128)(2,1)S(1)} %get-tuple-element.19.refs_0_), channel_id=1, source_target_pairs={{0,4},{4,0},{1,5},{5,1},{2,6},{6,2},{3,7},{7,3},{8,12},{12,8},{9,1... | collective-permute-start | bytes 786440 | tf_op jit(solution)/shard_map/ppermute | solution.py:240
  24.5 9.2 %collective-permute-start.10 = (bf16[2,256,256]{2,1,0:T(8,128)(2,1)S(1)}, bf16[2,256,256]{2,1,0:T(8,128)(2,1)S(1)}, u32[]{:S(2)}, u32[]{:S(2)}) collective-permute-start(bf16[2,256,256]{2,1,0:T(8,128)(2,1)S(1)} %pad_maximum_fusion), channel_id=1, source_target_pairs={{0,1},{1,0},{2,3},{3,2},{4,5},{5,4},{6,7},{7,6},{8,9},{9,8},{10,11... | collective-permute-start | bytes 786440 | tf_op jit(solution)/shard_map/ppermute | solution.py:237
  30.5 7.2 %collective-permute-start.5 = (bf16[2,256,256]{2,1,0:T(8,128)(2,1)S(1)}, bf16[2,256,256]{2,1,0:T(8,128)(2,1)S(1)}, u32[]{:S(2)}, u32[]{:S(2)}) collective-permute-start(bf16[2,256,256]{2,1,0:T(8,128)(2,1)S(1)} %get-tuple-element.22), channel_id=1, source_target_pairs={{0,1},{1,0},{2,3},{3,2},{4,5},{5,4},{6,7},{7,6},{8,9},{9,8},{10,11... | collective-permute-start | bytes 786440 | tf_op jit(solution)/shard_map/ppermute | solution.py:237
  35.4 7.4 %collective-permute-start.11 = (bf16[2,256,256]{2,1,0:T(8,128)(2,1)S(1)}, bf16[2,256,256]{2,1,0:T(8,128)(2,1)S(1)}, u32[]{:S(2)}, u32[]{:S(2)}) collective-permute-start(bf16[2,256,256]{2,1,0:T(8,128)(2,1)S(1)} %get-tuple-element.23.refs_2_), channel_id=1, source_target_pairs={{0,4},{4,0},{1,5},{5,1},{2,6},{6,2},{3,7},{7,3},{8,12},{12,8},{9,1... | collective-permute-start | bytes 786440 | tf_op jit(solution)/shard_map/ppermute | solution.py:240
  37.8 10.8 %collective-permute-start.6 = (bf16[256,256]{1,0:T(8,128)(2,1)S(1)}, bf16[256,256]{1,0:T(8,128)(2,1)S(1)}, u32[]{:S(2)}, u32[]{:S(2)}) collective-permute-start(bf16[256,256]{1,0:T(8,128)(2,1)S(1)} %fusion.2), channel_id=1, source_target_pairs={{0,2},{1,3},{2,0},{3,1},{4,6},{5,7},{6,4},{7,5},{8,10},{9,11},{10,... | collective-permute-start | bytes 393224 | tf_op jit(solution)/shard_map/ppermute | solution.py:237
  44.4 10.9 %collective-permute-start.12 = (bf16[256,256]{1,0:T(8,128)(2,1)S(1)}, bf16[256,256]{1,0:T(8,128)(2,1)S(1)}, u32[]{:S(2)}, u32[]{:S(2)}) collective-permute-start(bf16[256,256]{1,0:T(8,128)(2,1)S(1)} %get-tuple-element.26), channel_id=1, source_target_pairs={{0,2},{1,3},{2,0},{3,1},{4,6},{5,7},{6,4},{7,5},{8,10},{9,11},{10,... | collective-permute-start | bytes 393224 | tf_op jit(solution)/shard_map/ppermute | solution.py:237
  45.8 9.5 %collective-permute-start.13 = (bf16[256,256]{1,0:T(8,128)(2,1)S(1)}, bf16[256,256]{1,0:T(8,128)(2,1)S(1)}, u32[]{:S(2)}, u32[]{:S(2)}) collective-permute-start(bf16[256,256]{1,0:T(8,128)(2,1)S(1)} %get-tuple-element.27), channel_id=1, source_target_pairs={{0,3},{1,2},{2,1},{3,0},{4,7},{5,6},{6,5},{7,4},{8,11},{9,10},{10,... | collective-permute-start | bytes 393224 | tf_op jit(solution)/shard_map/ppermute | solution.py:237
  48.6 7.1 %collective-permute-start.14 = (bf16[256,256]{1,0:T(8,128)(2,1)S(1)}, bf16[256,256]{1,0:T(8,128)(2,1)S(1)}, u32[]{:S(2)}, u32[]{:S(2)}) collective-permute-start(bf16[256,256]{1,0:T(8,128)(2,1)S(1)} %get-tuple-element.28), channel_id=1, source_target_pairs={{0,1},{1,0},{2,3},{3,2},{4,5},{5,4},{6,7},{7,6},{8,9},{9,8},{10,11... | collective-permute-start | bytes 393224 | tf_op jit(solution)/shard_map/ppermute | solution.py:237
  48.6 7.1 %collective-permute-start.7 = (bf16[128,256]{1,0:T(8,128)(2,1)S(1)}, bf16[128,256]{1,0:T(8,128)(2,1)S(1)}, u32[]{:S(2)}, u32[]{:S(2)}) collective-permute-start(bf16[128,256]{1,0:T(8,128)(2,1)S(1)} %get-tuple-element.32), channel_id=1, source_target_pairs={{0,4},{4,0},{1,5},{5,1},{2,6},{6,2},{3,7},{7,3},{8,12},{12,8},{9,1... | collective-permute-start | bytes 196616 | tf_op jit(solution)/shard_map/ppermute | solution.py:240

commit v5 on v3

--- a/solution.py
+++ b/solution.py
@@ -10,7 +10,7 @@
 
 
 HDIM = 128
-GRANT = 16 << 20
+GRANT = 8 << 20
 F32 = jnp.float32
 BF16 = jnp.bfloat16
 
@@ -114,50 +114,53 @@
     return half + half * jnp.tanh(half)
 
 
-def project_kernel(place, own, near, far, mid, relay, weight, keyval, gateq):
-    pieces = [own[0].astype(F32), near[0].astype(F32), far[0].astype(F32)]
-    pieces.append(mid[0].astype(F32) + relay[0].astype(F32))
-    part = pieces[0].shape[1]
+def project_kernel(ids, groups, *refs):
+    *shares, weight, target = refs
+    pieces = [ref[k].astype(F32) for ref in shares for k in range(ref.shape[0])]
+    if len(pieces) > len(ids):
+        pieces[-2:] = [pieces[-2] + pieces[-1]]
+    part, size = pieces[0].shape[1], target.shape[2]
     width = part * len(pieces)
     mean = sum(jnp.sum(p, axis=1, keepdims=True) for p in pieces) / width
     pieces = [p - mean for p in pieces]
     spread = sum(jnp.sum(p * p, axis=1, keepdims=True) for p in pieces) / width
     rscale = lax.rsqrt(spread + 1e-06)
-    acc = None
-    for share_id, piece in enumerate(pieces):
-        lead = pl.multiple_of((place[1] ^ share_id) * part, part)
-        term = jnp.dot(
-            (piece * rscale).astype(BF16), weight[pl.ds(lead, part), :], preferred_element_type=F32
-        )
-        acc = term if acc is None else acc + term
-    done = half_silu(acc * 0.5).astype(BF16)
-    group = done.shape[1] // 4
-    gateq[0] = done[:, :group]
-    keyval[0] = done[:, group : 2 * group]
-    gateq[1] = done[:, 2 * group : 3 * group]
-    keyval[1] = done[:, 3 * group :]
-
-
-def weighted_values(plan, place, lengths, gateq, keyvals, first=None):
+    pieces = [(p * rscale).astype(BF16) for p in pieces]
+    head = lax.axis_index("head")
+    for slot, group in enumerate(groups):
+        lanes = slice(group * size, (group + 1) * size)
+        acc = None
+        for share_id, piece in zip(ids, pieces):
+            lead = pl.multiple_of((head ^ share_id) * part, part)
+            term = jnp.dot(piece, weight[pl.ds(lead, part), lanes], preferred_element_type=F32)
+            acc = term if acc is None else acc + term
+        target[slot] = half_silu(acc * 0.5).astype(BF16)
+
+
+def positions(offset, which, side, stripe):
+    if which == 0:
+        return offset + side * stripe + jnp.where(offset < stripe, 0, stripe)
+    inner = jnp.where(offset < stripe, offset + side * stripe, offset - side * stripe)
+    return (3 - side) * 2 * stripe + inner
+
+
+def weighted_values(plan, lengths, gateq, keyvals, first=None):
     chunk, stripe, origins = plan
     rows, cols = gateq.shape[1:]
-
-    def positions(shape, dim, which, side):
-        offset = lax.broadcasted_iota(jnp.int32, shape, dim)
-        block = side if which == 0 else 3 - side
-        inner = jnp.where(offset < stripe, offset + side * stripe, offset - side * stripe)
-        return block * rows + inner
-
-    query_pos = positions((rows, 1), 0, chunk, place[0])
-    start = jnp.zeros((rows, 1), jnp.int32)
-    end = jnp.int32(0)
+    own = lax.axis_index("ctx")
+    query_pos = positions(lax.broadcasted_iota(jnp.int32, (rows, HDIM), 0), chunk, own, stripe)
+    start = jnp.zeros((rows, HDIM), jnp.int32)
+    end = jnp.zeros((1, HDIM), jnp.int32)
     for user in range(lengths.shape[0]):
-        end = end + lengths[user]
+        end = end + lengths[user : user + 1, :]
         start = jnp.where(query_pos >= end, end, start)
+    query_pos = jnp.concatenate([query_pos] * (rows // HDIM), axis=1)
+    lowest = jnp.concatenate([start] * (rows // HDIM), axis=1)
     masks = []
     for which, side in origins:
-        key_pos = positions((1, rows), 1, which, place[0] ^ side)
-        masks.append((key_pos <= query_pos) & (key_pos >= start))
+        offset = lax.broadcasted_iota(jnp.int32, (1, rows), 1)
+        key_pos = positions(offset, which, own ^ side, stripe)
+        masks.append((key_pos <= query_pos) & (key_pos >= lowest))
     scale = 0.5 / math.sqrt(HDIM)
     totals = []
     for head in range(cols // HDIM):
@@ -175,34 +178,40 @@
     return totals
 
 
-def near_kernel(plan, place, lengths, *refs):
+def near_kernel(plan, lengths, *refs):
     *keyvals, gateq, partial = refs
-    totals = weighted_values(plan, place, lengths, gateq, keyvals)
+    totals = weighted_values(plan, lengths, gateq, keyvals)
     for head, total in enumerate(totals):
         partial[:, head * HDIM : (head + 1) * HDIM] = total
 
 
-def attend_kernel(plan, place, lengths, keyval, partial, gateq, weight, share, *refs):
+def attend_kernel(plan, lengths, keyval, partial, gateq, weight, share, *refs):
     *outputs, held = refs
+    chunk, stripe, _ = plan
     part = share.shape[2]
-    totals = weighted_values(plan, place, lengths, gateq, [keyval], partial)
+    totals = weighted_values(plan, lengths, gateq, [keyval], partial)
     for head, total in enumerate(totals):
         lanes = slice(head * HDIM, (head + 1) * HDIM)
         total = total - jnp.mean(total, axis=1, keepdims=True)
         spread = jnp.mean(total * total, axis=1, keepdims=True)
         total = total * lax.rsqrt(spread + 1e-05)
         held[:, lanes] = (total * gateq[0, :, lanes].astype(F32)).astype(BF16)
-    gated = held[...]
+    leads = [0, stripe]
+    if chunk == 0:
+        away = 1 - lax.axis_index("ctx")
+        leads = [pl.multiple_of(away * stripe, stripe), pl.multiple_of((1 - away) * stripe, stripe)]
+    gated = jnp.concatenate([held[pl.ds(lead, stripe), :] for lead in leads], axis=0)
+    share = jnp.concatenate([share[0, pl.ds(lead, stripe), :] for lead in leads], axis=0)
     for share_id in (2, 3, 1, 0):
-        lead = pl.multiple_of((place[1] ^ share_id) * part, part)
+        lead = pl.multiple_of((lax.axis_index("head") ^ share_id) * part, part)
         product = jnp.dot(gated, weight[:, pl.ds(lead, part)], preferred_element_type=F32)
         if share_id == 0:
-            product = product + share[0].astype(F32)
+            product = product + share.astype(F32)
         outputs[share_id][...] = product.astype(outputs[share_id].dtype)
 
 
-def whole(memory_space=pltpu.VMEM):
-    return pl.BlockSpec(memory_space=memory_space)
+def whole():
+    return pl.BlockSpec(memory_space=pltpu.VMEM)
 
 
 def pair_body(inputs, lengths, proj_in, proj_out):
@@ -211,7 +220,7 @@
     _, stripe, part = inputs.shape
     rows = 2 * stripe
     cols = proj_in.shape[2]
-    place = jnp.stack([own, lax.axis_index("head")]).astype(jnp.int32)
+    lengths = jnp.broadcast_to(lengths[:, None], (lengths.shape[0], HDIM))
     weight_in = proj_in.reshape(proj_in.shape[0], -1)
 
     def over_head(value, pairs):
@@ -222,12 +231,12 @@
     def over_ctx(value):
         return lax.ppermute(value, "ctx", [(0, 1), (1, 0)])
 
-    def kernel_call(function, outs, args, scalars, cost, scratch=()):
+    def kernel_call(function, outs, args, cost, scratch=()):
         return pl.pallas_call(
             function,
             compiler_params=pltpu.CompilerParams(vmem_limit_bytes=GRANT),
             out_shape=tuple(jax.ShapeDtypeStruct(*out) for out in outs),
-            in_specs=[whole(pltpu.SMEM)] * scalars + [whole()] * (len(args) - scalars),
+            in_specs=[whole() for _ in args],
             out_specs=tuple(whole() for _ in outs),
             scratch_shapes=scratch,
             cost_estimate=cost,
@@ -240,71 +249,76 @@
     inner = [(1, 2), (2, 1)]
     outer = [(1, 0), (2, 3)]
 
-    def settle(chunk):
-        stay = own if chunk == 0 else 1 - own
-        blocks = inputs[chunk * 2 : chunk * 2 + 2]
-        home = lax.dynamic_index_in_dim(blocks, stay, 0, keepdims=True)
-        away = lax.dynamic_index_in_dim(blocks, 1 - stay, 0, keepdims=True)
-        return jnp.concatenate([home, over_ctx(away)], axis=1)
-
     def gather(own_share, tag):
         far = over_head(own_share, 2)
+        after = far
+        if tag == "a":
+            after, weight = lax.optimization_barrier((far, weight_in))
+            weights.append(weight)
         near = over_head(own_share, 1)
         mid = over_head(own_share, inner)
-        if tag == "a":
-            far, weight = lax.optimization_barrier((far, weight_in))
-            weights.append(weight)
-        relay = over_head(far, outer)
+        relay = over_head(after, outer)
         return own_share, near, far, mid, relay
 
-    def project(shares):
-        size = ((2, rows, cols), BF16)
+    def project(shares, groups):
         return kernel_call(
-            project_kernel,
-            (size, size),
-            (place, *shares, weights[0]),
-            1,
-            cost(2 * rows * weight_in.size, rows * 4 * cols),
-        )
+            functools.partial(project_kernel, range(head_size), groups),
+            (((2, rows, cols), BF16),),
+            (*shares, weights[0]),
+            cost(rows * weight_in.size, rows * 2 * cols),
+        )[0]
 
     def near_part(chunk, origins, keyvals, gateq):
         count = len(keyvals)
         return kernel_call(
             functools.partial(near_kernel, (chunk, stripe, origins)),
             (((rows, cols), F32),),
-            (place, lengths, *keyvals, gateq),
-            2,
+            (lengths, *keyvals, gateq),
             cost(4 * rows * rows * cols * count, rows * rows * count * (cols // HDIM)),
         )[0]
 
     def attend(chunk, keyval, partial, gateq, share):
-        size = (rows, part)
         return kernel_call(
             functools.partial(attend_kernel, (chunk, stripe, [(chunk, 1)])),
-            ((size, F32),) + ((size, BF16),) * 3,
-            (place, lengths, keyval, partial, gateq, proj_out, share),
-            2,
+            (((rows, part), F32),) + (((rows, part), BF16),) * 3,
+            (lengths, keyval, partial, gateq, proj_out, share),
             cost(4 * rows * rows * cols + 2 * rows * proj_out.size, rows * rows * (cols // HDIM)),
             [pltpu.VMEM((rows, cols), BF16)],
         )
 
-    def total(kept, *sent):
+    def total_relayed(kept, near, far, last):
+        given = over_head(last, [(0, 1), (3, 2)])
+        for come in (over_head(last, inner), over_head(near, 1), over_head(far + given, 2)):
+            kept = kept + come.astype(F32)
+        return kept.astype(BF16)
+
+    def total_direct(kept, *sent):
         for share_id in (2, 3, 1):
-            kept = kept + over_head(sent[share_id - 1], share_id).astype(F32)
+            come = over_head(sent[share_id - 1], share_id)
+            kept = kept + come.astype(F32)
         return kept.astype(BF16)
 
-    shares = [settle(0), settle(1)]
-    low_keyval, low_gateq = project(gather(shares[0], "a"))
+    flag = lax.optimization_barrier(jnp.full((1, part), own, jnp.int32))
+    low = inputs[:2].reshape(1, rows, part)
+    home = lax.dynamic_index_in_dim(inputs[2:], 1 - own, 0, keepdims=True)
+    away = lax.dynamic_index_in_dim(inputs[2:], own, 0, keepdims=True)
+    high = jnp.concatenate([home, over_ctx(away)], axis=1)
+    low_shares = gather(low, "a")
+    low_keyval = project(low_shares, (1, 3))
     low_other = over_ctx(low_keyval)
-    high_keyval, high_gateq = project(gather(shares[1], "b"))
+    low_gateq = project(low_shares, (0, 2))
+    high_shares = gather(high, "b")
+    high_keyval = project(high_shares, (1, 3))
     high_other = over_ctx(high_keyval)
+    high_gateq = project(high_shares, (0, 2))
     low_first = near_part(0, [(0, 0)], [low_keyval], low_gateq)
-    low_done = total(*attend(0, low_other, low_first, low_gateq, shares[0]))
+    low_done = total_relayed(*attend(0, low_other, low_first, low_gateq, low))
     origins = [(0, 0), (0, 1), (1, 0)]
     high_first = near_part(1, origins, [low_keyval, low_other, high_keyval], high_gateq)
-    high_done = total(*attend(1, high_other, high_first, high_gateq, shares[1]))
-    both = jnp.stack([low_done, high_done]).reshape(2, 2, stripe, part)
-    return jnp.where(own == 0, both, both[:, ::-1]).reshape(1, 2, rows, part)
+    high_done = total_direct(*attend(1, high_other, high_first, high_gateq, high))
+    come = over_ctx(low_done[:stripe])
+    both = jnp.concatenate([low_done[stripe:], come, high_done], axis=0).reshape(2, 2, stripe, part)
+    return jnp.where(flag == 0, both, both[:, ::-1]).reshape(1, 2, rows, part)
 
 
 def body(inputs, lengths, proj_in, proj_out):

time: 61.6 us -> 63.2 us (1.026)
  starting transfers between devices: 26.2 us -> 36.3 us
  waiting for transfers between devices: 19.7 us -> 15.5 us
  Pallas kernels: 10.2 us -> 6.76 us
  local copies, waits for them, and re-layouts: 4.05 us -> 3.17 us
    ppermute x14 -> x15, starting transfers between devices: 22.2 us -> 30.1 us  [over_head(): return lax.ppermute(value, 'head', pairs)]
    pallas_call x6 -> x8, Pallas kernels: 10.2 us -> 6.76 us  [kernel_call(): pl.pallas_call(function, compiler_params=pltpu.CompilerParams(vmem_limit_...]
    ppermute x14 -> x15, waiting for transfers between devices: 16.5 us -> 13.7 us  [over_head(): return lax.ppermute(value, 'head', pairs)]
    ppermute x4, starting transfers between devices: 4.07 us -> 6.21 us  [over_ctx(): return lax.ppermute(value, 'ctx', [(0, 1), (1, 0)])]
    ppermute x4, waiting for transfers between devices: 3.2 us -> 1.87 us  [over_ctx(): return lax.ppermute(value, 'ctx', [(0, 1), (1, 0)])]
    unnamed x9 -> x5, local copies, waits for them, and re-layouts: 3.04 us -> 2.09 us
  transfers between devices with their start and end apart: 18 -> 19, of which waited for: 8 -> 6; matrix products, arithmetic and copies ran while one was open for 4% -> 4% of each run, Pallas kernels for 17% -> 11%
where the time goes in v5:
time: 63.2 us; the launch traced here: 63 us
  starting transfers between devices  36.3 us (57%)
  waiting for transfers between devices  15.5 us (25%)
  Pallas kernels  6.76 us (11%)
  local copies, waits for them, and re-layouts  3.17 us (5%)
  other arithmetic  0.95 us (2%)
    ppermute x15, starting transfers between devices, over_head(): return lax.ppermute(value, 'head', pairs)  30.1 us
    ppermute x15, waiting for transfers between devices, over_head(): return lax.ppermute(value, 'head', pairs)  13.7 us
    pallas_call x8, Pallas kernels, kernel_call(): pl.pallas_call(function, compiler_params=pltpu.CompilerParams(vmem_limit_...  6.76 us
    ppermute x4, starting transfers between devices, over_ctx(): return lax.ppermute(value, 'ctx', [(0, 1), (1, 0)])  6.21 us
    unnamed x5, local copies, waits for them, and re-layouts  2.09 us
    ppermute x4, waiting for transfers between devices, over_ctx(): return lax.ppermute(value, 'ctx', [(0, 1), (1, 0)])  1.87 us
  transfers between devices with their start and end apart: 19, of which 6 were waited for; matrix products, arithmetic and copies ran while one was open for 4% of the time, Pallas kernels for 11%

profile of v5, /device:TPU:0, one launch (start us, length us, event | category | flops | bytes accessed | tf_op | source)
XLA Modules:
  0.0 63.0 jit_solution(9707301968666533749)
XLA Ops:
  0.0 1.0 %fusion = (bf16[2,128,256]{2,1,0:T(8,128)(2,1)S(1)}, bf16[2,128,256]{2,1,0:T(8,128)(2,1)S(1)}) fusion(bf16[4,128,256]{2,1,0:T(8,128)(2,1)} %param.4), kind=kLoop, calls=%fused_computation.8 | loop fusion | bytes 524288 | tf_op jit(solution)/shard_map/slice | solution.py:302
  1.0 4.1 %collective-permute-start.1 = (bf16[1,256,256]{2,1,0:T(8,128)(2,1)S(1)}, bf16[1,256,256]{2,1,0:T(8,128)(2,1)S(1)}, u32[]{:S(2)}, u32[]{:S(2)}) collective-permute-start(bf16[1,256,256]{2,1,0:T(8,128)(2,1)S(1)} %bitcast.9), channel_id=1, source_target_pairs={{0,2},{1,3},{2,0},{3,1},{4,6},{5,7},{6,4},{7,5},{8,10},{9,11},{10,... | collective-permute-start | bytes 393224 | tf_op jit(solution)/shard_map/ppermute | solution.py:229
  5.1 0.7 %collective-permute-start.2 = (bf16[1,256,256]{2,1,0:T(8,128)(2,1)S(1)}, bf16[1,256,256]{2,1,0:T(8,128)(2,1)S(1)}, u32[]{:S(2)}, u32[]{:S(2)}) collective-permute-start(bf16[1,256,256]{2,1,0:T(8,128)(2,1)S(1)} %bitcast.10), channel_id=1, source_target_pairs={{1,2},{2,1},{5,6},{6,5},{9,10},{10,9},{13,14},{14,13},{17,18},{18,... | collective-permute-start | bytes 393224 | tf_op jit(solution)/shard_map/ppermute | solution.py:229
  5.8 2.9 %collective-permute-start = (bf16[1,256,256]{2,1,0:T(8,128)(2,1)S(1)}, bf16[1,256,256]{2,1,0:T(8,128)(2,1)S(1)}, u32[]{:S(2)}, u32[]{:S(2)}) collective-permute-start(bf16[1,256,256]{2,1,0:T(8,128)(2,1)S(1)} %bitcast.11), channel_id=1, source_target_pairs={{0,1},{1,0},{2,3},{3,2},{4,5},{5,4},{6,7},{7,6},{8,9},{9,8},{10,11... | collective-permute-start | bytes 393224 | tf_op jit(solution)/shard_map/ppermute | solution.py:229
  8.7 2.1 %copy.5 = bf16[128,8,4,256]{3,1,2,0:T(8,128)(2,1)S(1)} copy(bf16[128,8,4,256]{3,2,1,0:T(4,128)(2,1)} %bitcast.15) | data formatting | bytes 4194304
  10.8 1.5 %collective-permute-done.1.refs_2_ = bf16[1,256,256]{2,1,0:T(8,128)(2,1)S(1)} collective-permute-done((bf16[1,256,256]{2,1,0:T(8,128)(2,1)S(1)}, bf16[1,256,256]{2,1,0:T(8,128)(2,1)S(1)}, u32[]{:S(2)}, u32[]{:S(2)}) %collective-permute-start.1) | collective-permute-done | bytes 131104 | tf_op jit(solution)/shard_map/ppermute | solution.py:229
  12.3 1.3 %collective-permute-start.3 = (bf16[1,256,256]{2,1,0:T(8,128)(2,1)S(1)}, bf16[1,256,256]{2,1,0:T(8,128)(2,1)S(1)}, u32[]{:S(2)}, u32[]{:S(2)}) collective-permute-start(bf16[1,256,256]{2,1,0:T(8,128)(2,1)S(1)} %collective-permute-done.1.refs_2_), channel_id=1, source_target_pairs={{1,0},{2,3},{5,4},{6,7},{9,8},{10,11},{13,12},{14,15},{17,16},{18,... | collective-permute-start | bytes 393224 | tf_op jit(solution)/shard_map/ppermute | solution.py:229
  13.6 1.9 %collective-permute-start.10 = (bf16[1,128,256]{2,1,0:T(8,128)(2,1)S(1)}, bf16[1,128,256]{2,1,0:T(8,128)(2,1)S(1)}, u32[]{:S(2)}, u32[]{:S(2)}) collective-permute-start(bf16[1,128,256]{2,1,0:T(8,128)(2,1)S(1)} %get-tuple-element.30), channel_id=1, source_target_pairs={{0,4},{4,0},{1,5},{5,1},{2,6},{6,2},{3,7},{7,3},{8,12},{12,8},{9,1... | collective-permute-start | bytes 196616 | tf_op jit(solution)/shard_map/ppermute | solution.py:232
  15.5 0.0 collective-permute-done.2.refs_3_
  15.5 3.6 %collective-permute-done.3.refs_4_ = bf16[1,256,256]{2,1,0:T(8,128)(2,1)S(1)} collective-permute-done((bf16[1,256,256]{2,1,0:T(8,128)(2,1)S(1)}, bf16[1,256,256]{2,1,0:T(8,128)(2,1)S(1)}, u32[]{:S(2)}, u32[]{:S(2)}) %collective-permute-start.3) | collective-permute-done | bytes 131104 | tf_op jit(solution)/shard_map/ppermute | solution.py:229
  19.1 0.7 %shard_map.46.refs_0_ = bf16[2,256,256]{2,1,0:T(8,128)(2,1)S(1)} custom-call(bf16[1,256,256]{2,1,0:T(8,128)(2,1)S(1)} %bitcast.12, bf16[1,256,256]{2,1,0:T(8,128)(2,1)S(1)} %collective-permute-done.refs_1_, bf16[1,256,256]{2,1,0:T(8,128)(2,1)S(1)} %collective-permute-done.1.refs_2_, bf16[1,256,256]{2,1,0:T(8,128)(2,1)S(1)} %collective-permute-done.2.refs_3_, ...), custom_call_target="tpu_custom_call" | custom-call | flops 268435456 | bytes 1048576 | tf_op jit(solution)/shard_map/pallas_call | solution.py:235
  19.9 0.0 copy-start.1
  19.9 0.0 copy-start
  19.9 1.9 %collective-permute-start.4 = (bf16[2,256,256]{2,1,0:T(8,128)(2,1)S(1)}, bf16[2,256,256]{2,1,0:T(8,128)(2,1)S(1)}, u32[]{:S(2)}, u32[]{:S(2)}) collective-permute-start(bf16[2,256,256]{2,1,0:T(8,128)(2,1)S(1)} %shard_map.46.refs_0_), channel_id=1, source_target_pairs={{0,4},{4,0},{1,5},{5,1},{2,6},{6,2},{3,7},{7,3},{8,12},{12,8},{9,1... | collective-permute-start | bytes 786440 | tf_op jit(solution)/shard_map/ppermute | solution.py:232
  21.8 0.0 collective-permute-done.10
  21.8 1.0 %collective-permute-start.12 = (bf16[1,256,256]{2,1,0:T(8,128)(2,1)S(1)}, bf16[1,256,256]{2,1,0:T(8,128)(2,1)S(1)}, u32[]{:S(2)}, u32[]{:S(2)}) collective-permute-start(bf16[1,256,256]{2,1,0:T(8,128)(2,1)S(1)} %pad_maximum_fusion.1.refs_0_.share), channel_id=1, source_target_pairs={{0,2},{1,3},{2,0},{3,1},{4,6},{5,7},{6,4},{7,5},{8,10},{9,11},{10,... | collective-permute-start | bytes 393224 | tf_op jit(solution)/shard_map/ppermute | solution.py:229
  22.8 0.7 %collective-permute-start.13 = (bf16[1,256,256]{2,1,0:T(8,128)(2,1)S(1)}, bf16[1,256,256]{2,1,0:T(8,128)(2,1)S(1)}, u32[]{:S(2)}, u32[]{:S(2)}) collective-permute-start(bf16[1,256,256]{2,1,0:T(8,128)(2,1)S(1)} %pad_maximum_fusion.1.refs_0_.share), channel_id=1, source_target_pairs={{1,2},{2,1},{5,6},{6,5},{9,10},{10,9},{13,14},{14,13},{17,18},{18,... | collective-permute-start | bytes 393224 | tf_op jit(solution)/shard_map/ppermute | solution.py:229
  23.5 3.8 %collective-permute-start.11 = (bf16[1,256,256]{2,1,0:T(8,128)(2,1)S(1)}, bf16[1,256,256]{2,1,0:T(8,128)(2,1)S(1)}, u32[]{:S(2)}, u32[]{:S(2)}) collective-permute-start(bf16[1,256,256]{2,1,0:T(8,128)(2,1)S(1)} %pad_maximum_fusion.1.refs_0_.share), channel_id=1, source_target_pairs={{0,1},{1,0},{2,3},{3,2},{4,5},{5,4},{6,7},{7,6},{8,9},{9,8},{10,11... | collective-permute-start | bytes 393224 | tf_op jit(solution)/shard_map/ppermute | solution.py:229
  27.3 3.1 %collective-permute-done.12.refs_2_ = bf16[1,256,256]{2,1,0:T(8,128)(2,1)S(1)} collective-permute-done((bf16[1,256,256]{2,1,0:T(8,128)(2,1)S(1)}, bf16[1,256,256]{2,1,0:T(8,128)(2,1)S(1)}, u32[]{:S(2)}, u32[]{:S(2)}) %collective-permute-start.12) | collective-permute-done | bytes 131104 | tf_op jit(solution)/shard_map/ppermute | solution.py:229
  30.4 1.3 %collective-permute-start.14 = (bf16[1,256,256]{2,1,0:T(8,128)(2,1)S(1)}, bf16[1,256,256]{2,1,0:T(8,128)(2,1)S(1)}, u32[]{:S(2)}, u32[]{:S(2)}) collective-permute-start(bf16[1,256,256]{2,1,0:T(8,128)(2,1)S(1)} %collective-permute-done.12.refs_2_), channel_id=1, source_target_pairs={{1,0},{2,3},{5,4},{6,7},{9,8},{10,11},{13,12},{14,15},{17,16},{18,... | collective-permute-start | bytes 393224 | tf_op jit(solution)/shard_map/ppermute | solution.py:229
  31.7 0.7 %shard_map.47.refs_1_.gateq = bf16[2,256,256]{2,1,0:T(8,128)(2,1)S(1)} custom-call(bf16[1,256,256]{2,1,0:T(8,128)(2,1)S(1)} %bitcast.13, bf16[1,256,256]{2,1,0:T(8,128)(2,1)S(1)} %collective-permute-done.refs_1_, bf16[1,256,256]{2,1,0:T(8,128)(2,1)S(1)} %collective-permute-done.1.refs_2_, bf16[1,256,256]{2,1,0:T(8,128)(2,1)S(1)} %collective-permute-done.2.refs_3_, ...), custom_call_target="tpu_custom_call" | custom-call | flops 268435456 | bytes 1048576 | tf_op jit(solution)/shard_map/pallas_call | solution.py:235
  32.5 0.1 broadcast_in_dim.19.lengths
  32.5 0.6 shard_map.48.partial
  33.1 0.0 collective-permute-done.4.keyval.refs_1_
  33.1 1.0 %shard_map.49 = (f32[256,256]{1,0:T(8,128)S(1)}, bf16[256,256]{1,0:T(8,128)(2,1)S(1)}, bf16[256,256]{1,0:T(8,128)(2,1)S(1)}, bf16[256,256]{1,0:T(8,128)(2,1)S(1)}) custom-call(s32[4,128]{1,0:T(4,128)S(1)} %broadcast_in_dim.19.lengths, bf16[2,256,256]{2,1,0:T(8,128)(2,1)S(1)} %collective-permute-done.4.keyval.refs_1_, f32[256,256]{1,0:T(8,128)S(1)} %shard_map.48.partial, ...), custom_call_target="tpu_custom_call" | custom-call | flops 201326592 | bytes 1048576 | tf_op jit(solution)/shard_map/pallas_call | solution.py:235
  34.2 4.6 %collective-permute-start.7 = (bf16[256,256]{1,0:T(8,128)(2,1)S(1)}, bf16[256,256]{1,0:T(8,128)(2,1)S(1)}, u32[]{:S(2)}, u32[]{:S(2)}) collective-permute-start(bf16[256,256]{1,0:T(8,128)(2,1)S(1)} %get-tuple-element.18), channel_id=1, source_target_pairs={{0,1},{3,2},{4,5},{7,6},{8,9},{11,10},{12,13},{15,14},{16,17},{19,... | collective-permute-start | bytes 393224 | tf_op jit(solution)/shard_map/ppermute | solution.py:229
  38.8 0.0 collective-permute-done.11.refs_1_
  38.8 0.0 collective-permute-done.14.refs_4_
  38.8 0.7 %shard_map.50.refs_2_ = bf16[2,256,256]{2,1,0:T(8,128)(2,1)S(1)} custom-call(bf16[1,256,256]{2,1,0:T(8,128)(2,1)S(1)} %pad_maximum_fusion.1.refs_0_.share, bf16[1,256,256]{2,1,0:T(8,128)(2,1)S(1)} %collective-permute-done.11.refs_1_, bf16[1,256,256]{2,1,0:T(8,128)(2,1)S(1)} %collective-permute-done.12.refs_2_, ...), custom_call_target="tpu_custom_call" | custom-call | flops 268435456 | bytes 1048576 | tf_op jit(solution)/shard_map/pallas_call | solution.py:235
  39.5 0.1 collective-permute-start.15
  39.6 0.7 %collective-permute-start.5 = (bf16[256,256]{1,0:T(8,128)(2,1)S(1)}, bf16[256,256]{1,0:T(8,128)(2,1)S(1)}, u32[]{:S(2)}, u32[]{:S(2)}) collective-permute-start(bf16[256,256]{1,0:T(8,128)(2,1)S(1)} %get-tuple-element.18), channel_id=1, source_target_pairs={{1,2},{2,1},{5,6},{6,5},{9,10},{10,9},{13,14},{14,13},{17,18},{18,... | collective-permute-start | bytes 393224 | tf_op jit(solution)/shard_map/ppermute | solution.py:229
  40.3 2.6 %collective-permute-start.6 = (bf16[256,256]{1,0:T(8,128)(2,1)S(1)}, bf16[256,256]{1,0:T(8,128)(2,1)S(1)}, u32[]{:S(2)}, u32[]{:S(2)}) collective-permute-start(bf16[256,256]{1,0:T(8,128)(2,1)S(1)} %get-tuple-element.19), channel_id=1, source_target_pairs={{0,1},{1,0},{2,3},{3,2},{4,5},{5,4},{6,7},{7,6},{8,9},{9,8},{10,11... | collective-permute-start | bytes 393224 | tf_op jit(solution)/shard_map/ppermute | solution.py:229
  42.9 3.0 %collective-permute-start.8 = (bf16[256,256]{1,0:T(8,128)(2,1)S(1)}, bf16[256,256]{1,0:T(8,128)(2,1)S(1)}, u32[]{:S(2)}, u32[]{:S(2)}) collective-permute-start(bf16[256,256]{1,0:T(8,128)(2,1)S(1)} %add.31), channel_id=1, source_target_pairs={{0,2},{1,3},{2,0},{3,1},{4,6},{5,7},{6,4},{7,5},{8,10},{9,11},{10,... | collective-permute-start | bytes 393224 | tf_op jit(solution)/shard_map/ppermute | solution.py:229
  45.9 0.7 %shard_map.51.refs_3_.gateq = bf16[2,256,256]{2,1,0:T(8,128)(2,1)S(1)} custom-call(bf16[1,256,256]{2,1,0:T(8,128)(2,1)S(1)} %pad_maximum_fusion.1.refs_0_.share, bf16[1,256,256]{2,1,0:T(8,128)(2,1)S(1)} %collective-permute-done.11.refs_1_, bf16[1,256,256]{2,1,0:T(8,128)(2,1)S(1)} %collective-permute-done.12.refs_2_, ...), custom_call_target="tpu_custom_call" | custom-call | flops 268435456 | bytes 1048576 | tf_op jit(solution)/shard_map/pallas_call | solution.py:235
  46.7 1.1 %shard_map.52.partial = f32[256,256]{1,0:T(8,128)S(1)} custom-call(s32[4,128]{1,0:T(4,128)S(1)} %broadcast_in_dim.19.lengths, bf16[2,256,256]{2,1,0:T(8,128)(2,1)S(1)} %shard_map.46.refs_0_, bf16[2,256,256]{2,1,0:T(8,128)(2,1)S(1)} %collective-permute-done.4.keyval.refs_1_, bf16[2,256,256]{2,1,0:T(8,128)(2,1)S(1)} %shard_map.50.refs_2_, ...), custom_call_target="tpu_custom_call" | custom-call | flops 201326592 | bytes 1048576 | tf_op jit(solution)/shard_map/pallas_call | solution.py:235
  47.8 0.0 collective-permute-done.15.keyval
  47.8 1.0 %shard_map.53 = (f32[256,256]{1,0:T(8,128)S(1)}, bf16[256,256]{1,0:T(8,128)(2,1)S(1)}, bf16[256,256]{1,0:T(8,128)(2,1)S(1)}, bf16[256,256]{1,0:T(8,128)(2,1)S(1)}) custom-call(s32[4,128]{1,0:T(4,128)S(1)} %broadcast_in_dim.19.lengths, bf16[2,256,256]{2,1,0:T(8,128)(2,1)S(1)} %collective-permute-done.15.keyval, f32[256,256]{1,0:T(8,128)S(1)} %shard_map.52.partial, ...), custom_call_target="tpu_custom_call" | custom-call | flops 201326592 | bytes 1048576 | tf_op jit(solution)/shard_map/pallas_call | solution.py:235
  48.8 0.1 collective-permute-start.16
  48.9 1.9 %collective-permute-start.17 = (bf16[256,256]{1,0:T(8,128)(2,1)S(1)}, bf16[256,256]{1,0:T(8,128)(2,1)S(1)}, u32[]{:S(2)}, u32[]{:S(2)}) collective-permute-start(bf16[256,256]{1,0:T(8,128)(2,1)S(1)} %get-tuple-element.23), channel_id=1, source_target_pairs={{0,3},{1,2},{2,1},{3,0},{4,7},{5,6},{6,5},{7,4},{8,11},{9,10},{10,... | collective-permute-start | bytes 393224 | tf_op jit(solution)/shard_map/ppermute | solution.py:229
  50.8 1.6 %collective-permute-start.18 = (bf16[256,256]{1,0:T(8,128)(2,1)S(1)}, bf16[256,256]{1,0:T(8,128)(2,1)S(1)}, u32[]{:S(2)}, u32[]{:S(2)}) collective-permute-start(bf16[256,256]{1,0:T(8,128)(2,1)S(1)} %get-tuple-element.24), channel_id=1, source_target_pairs={{0,1},{1,0},{2,3},{3,2},{4,5},{5,4},{6,7},{7,6},{8,9},{9,8},{10,11... | collective-permute-start | bytes 393224 | tf_op jit(solution)/shard_map/ppermute | solution.py:229
  52.4 0.0 collective-permute-done.5
  52.4 5.1 %collective-permute-done.8 = bf16[256,256]{1,0:T(8,128)(2,1)S(1)} collective-permute-done((bf16[256,256]{1,0:T(8,128)(2,1)S(1)}, bf16[256,256]{1,0:T(8,128)(2,1)S(1)}, u32[]{:S(2)}, u32[]{:S(2)}) %collective-permute-start.8) | collective-permute-done | bytes 131104 | tf_op jit(solution)/shard_map/ppermute | solution.py:229
  57.5 0.1 add_convert_fusion.1
  57.6 2.4 %collective-permute-start.9 = (bf16[128,256]{1,0:T(8,128)(2,1)S(1)}, bf16[128,256]{1,0:T(8,128)(2,1)S(1)}, u32[]{:S(2)}, u32[]{:S(2)}) collective-permute-start(bf16[128,256]{1,0:T(8,128)(2,1)S(1)} %get-tuple-element.28), channel_id=1, source_target_pairs={{0,4},{4,0},{1,5},{5,1},{2,6},{6,2},{3,7},{7,3},{8,12},{12,8},{9,1... | collective-permute-start | bytes 196616 | tf_op jit(solution)/shard_map/ppermute | solution.py:232
  59.9 0.3 collective-permute-done.16
  60.3 0.1 add_convert_fusion
  60.3 1.9 %collective-permute-done.9 = bf16[128,256]{1,0:T(8,128)(2,1)S(1)} collective-permute-done((bf16[128,256]{1,0:T(8,128)(2,1)S(1)}, bf16[128,256]{1,0:T(8,128)(2,1)S(1)}, u32[]{:S(2)}, u32[]{:S(2)}) %collective-permute-start.9) | collective-permute-done | bytes 65568 | tf_op jit(solution)/shard_map/ppermute | solution.py:232
  62.2 0.8 %reverse_select_fusion = bf16[2,2,128,256]{3,2,1,0:T(8,128)(2,1)} fusion(bf16[2,2,128,256]{3,2,1,0:T(8,128)(2,1)S(1)} %bitcast.16, pred[256]{0:T(512)(128)(4,1)S(1)} %compare_reduce_fusion), kind=kLoop, calls=%fused_computation | loop fusion | flops 131072 | bytes 524544 | tf_op jit(solution)/shard_map/jit(_where)/select_n | solution.py:321
  (15 shorter events, 0.1 us)
Async XLA Ops:
  1.0 11.3 %collective-permute-start.1 = (bf16[1,256,256]{2,1,0:T(8,128)(2,1)S(1)}, bf16[1,256,256]{2,1,0:T(8,128)(2,1)S(1)}, u32[]{:S(2)}, u32[]{:S(2)}) collective-permute-start(bf16[1,256,256]{2,1,0:T(8,128)(2,1)S(1)} %bitcast.9), channel_id=1, source_target_pairs={{0,2},{1,3},{2,0},{3,1},{4,6},{5,7},{6,4},{7,5},{8,10},{9,11},{10,... | collective-permute-start | bytes 393224 | tf_op jit(solution)/shard_map/ppermute | solution.py:229
  5.1 10.4 %collective-permute-start.2 = (bf16[1,256,256]{2,1,0:T(8,128)(2,1)S(1)}, bf16[1,256,256]{2,1,0:T(8,128)(2,1)S(1)}, u32[]{:S(2)}, u32[]{:S(2)}) collective-permute-start(bf16[1,256,256]{2,1,0:T(8,128)(2,1)S(1)} %bitcast.10), channel_id=1, source_target_pairs={{1,2},{2,1},{5,6},{6,5},{9,10},{10,9},{13,14},{14,13},{17,18},{18,... | collective-permute-start | bytes 393224 | tf_op jit(solution)/shard_map/ppermute | solution.py:229
  5.8 9.7 %collective-permute-start = (bf16[1,256,256]{2,1,0:T(8,128)(2,1)S(1)}, bf16[1,256,256]{2,1,0:T(8,128)(2,1)S(1)}, u32[]{:S(2)}, u32[]{:S(2)}) collective-permute-start(bf16[1,256,256]{2,1,0:T(8,128)(2,1)S(1)} %bitcast.11), channel_id=1, source_target_pairs={{0,1},{1,0},{2,3},{3,2},{4,5},{5,4},{6,7},{7,6},{8,9},{9,8},{10,11... | collective-permute-start | bytes 393224 | tf_op jit(solution)/shard_map/ppermute | solution.py:229
  12.3 6.8 %collective-permute-start.3 = (bf16[1,256,256]{2,1,0:T(8,128)(2,1)S(1)}, bf16[1,256,256]{2,1,0:T(8,128)(2,1)S(1)}, u32[]{:S(2)}, u32[]{:S(2)}) collective-permute-start(bf16[1,256,256]{2,1,0:T(8,128)(2,1)S(1)} %collective-permute-done.1.refs_2_), channel_id=1, source_target_pairs={{1,0},{2,3},{5,4},{6,7},{9,8},{10,11},{13,12},{14,15},{17,16},{18,... | collective-permute-start | bytes 393224 | tf_op jit(solution)/shard_map/ppermute | solution.py:229
  13.6 8.2 %collective-permute-start.10 = (bf16[1,128,256]{2,1,0:T(8,128)(2,1)S(1)}, bf16[1,128,256]{2,1,0:T(8,128)(2,1)S(1)}, u32[]{:S(2)}, u32[]{:S(2)}) collective-permute-start(bf16[1,128,256]{2,1,0:T(8,128)(2,1)S(1)} %get-tuple-element.30), channel_id=1, source_target_pairs={{0,4},{4,0},{1,5},{5,1},{2,6},{6,2},{3,7},{7,3},{8,12},{12,8},{9,1... | collective-permute-start | bytes 196616 | tf_op jit(solution)/shard_map/ppermute | solution.py:232
  19.9 12.6 %copy-start.1 = (s32[4]{0:T(128)S(1)}, s32[4]{0:T(128)}, u32[]{:S(2)}) copy-start(s32[4]{0:T(128)} %param.5) | copy-start | bytes 52
  19.9 13.3 %copy-start = (bf16[256,1024]{1,0:T(8,128)(2,1)S(1)}, bf16[256,1024]{1,0:T(8,128)(2,1)}, u32[]{:S(2)}) copy-start(bf16[256,1024]{1,0:T(8,128)(2,1)} %weight.3) | copy-start | bytes 1572868
  19.9 13.2 %collective-permute-start.4 = (bf16[2,256,256]{2,1,0:T(8,128)(2,1)S(1)}, bf16[2,256,256]{2,1,0:T(8,128)(2,1)S(1)}, u32[]{:S(2)}, u32[]{:S(2)}) collective-permute-start(bf16[2,256,256]{2,1,0:T(8,128)(2,1)S(1)} %shard_map.46.refs_0_), channel_id=1, source_target_pairs={{0,4},{4,0},{1,5},{5,1},{2,6},{6,2},{3,7},{7,3},{8,12},{12,8},{9,1... | collective-permute-start | bytes 786440 | tf_op jit(solution)/shard_map/ppermute | solution.py:232
  21.8 8.6 %collective-permute-start.12 = (bf16[1,256,256]{2,1,0:T(8,128)(2,1)S(1)}, bf16[1,256,256]{2,1,0:T(8,128)(2,1)S(1)}, u32[]{:S(2)}, u32[]{:S(2)}) collective-permute-start(bf16[1,256,256]{2,1,0:T(8,128)(2,1)S(1)} %pad_maximum_fusion.1.refs_0_.share), channel_id=1, source_target_pairs={{0,2},{1,3},{2,0},{3,1},{4,6},{5,7},{6,4},{7,5},{8,10},{9,11},{10,... | collective-permute-start | bytes 393224 | tf_op jit(solution)/shard_map/ppermute | solution.py:229
  22.8 15.9 %collective-permute-start.13 = (bf16[1,256,256]{2,1,0:T(8,128)(2,1)S(1)}, bf16[1,256,256]{2,1,0:T(8,128)(2,1)S(1)}, u32[]{:S(2)}, u32[]{:S(2)}) collective-permute-start(bf16[1,256,256]{2,1,0:T(8,128)(2,1)S(1)} %pad_maximum_fusion.1.refs_0_.share), channel_id=1, source_target_pairs={{1,2},{2,1},{5,6},{6,5},{9,10},{10,9},{13,14},{14,13},{17,18},{18,... | collective-permute-start | bytes 393224 | tf_op jit(solution)/shard_map/ppermute | solution.py:229
  23.5 15.3 %collective-permute-start.11 = (bf16[1,256,256]{2,1,0:T(8,128)(2,1)S(1)}, bf16[1,256,256]{2,1,0:T(8,128)(2,1)S(1)}, u32[]{:S(2)}, u32[]{:S(2)}) collective-permute-start(bf16[1,256,256]{2,1,0:T(8,128)(2,1)S(1)} %pad_maximum_fusion.1.refs_0_.share), channel_id=1, source_target_pairs={{0,1},{1,0},{2,3},{3,2},{4,5},{5,4},{6,7},{7,6},{8,9},{9,8},{10,11... | collective-permute-start | bytes 393224 | tf_op jit(solution)/shard_map/ppermute | solution.py:229
  30.4 8.4 %collective-permute-start.14 = (bf16[1,256,256]{2,1,0:T(8,128)(2,1)S(1)}, bf16[1,256,256]{2,1,0:T(8,128)(2,1)S(1)}, u32[]{:S(2)}, u32[]{:S(2)}) collective-permute-start(bf16[1,256,256]{2,1,0:T(8,128)(2,1)S(1)} %collective-permute-done.12.refs_2_), channel_id=1, source_target_pairs={{1,0},{2,3},{5,4},{6,7},{9,8},{10,11},{13,12},{14,15},{17,16},{18,... | collective-permute-start | bytes 393224 | tf_op jit(solution)/shard_map/ppermute | solution.py:229
  34.2 8.7 %collective-permute-start.7 = (bf16[256,256]{1,0:T(8,128)(2,1)S(1)}, bf16[256,256]{1,0:T(8,128)(2,1)S(1)}, u32[]{:S(2)}, u32[]{:S(2)}) collective-permute-start(bf16[256,256]{1,0:T(8,128)(2,1)S(1)} %get-tuple-element.18), channel_id=1, source_target_pairs={{0,1},{3,2},{4,5},{7,6},{8,9},{11,10},{12,13},{15,14},{16,17},{19,... | collective-permute-start | bytes 393224 | tf_op jit(solution)/shard_map/ppermute | solution.py:229
  39.5 8.2 %collective-permute-start.15 = (bf16[2,256,256]{2,1,0:T(8,128)(2,1)S(1)}, bf16[2,256,256]{2,1,0:T(8,128)(2,1)S(1)}, u32[]{:S(2)}, u32[]{:S(2)}) collective-permute-start(bf16[2,256,256]{2,1,0:T(8,128)(2,1)S(1)} %shard_map.50.refs_2_), channel_id=1, source_target_pairs={{0,4},{4,0},{1,5},{5,1},{2,6},{6,2},{3,7},{7,3},{8,12},{12,8},{9,1... | collective-permute-start | bytes 786440 | tf_op jit(solution)/shard_map/ppermute | solution.py:232
  39.6 12.8 %collective-permute-start.5 = (bf16[256,256]{1,0:T(8,128)(2,1)S(1)}, bf16[256,256]{1,0:T(8,128)(2,1)S(1)}, u32[]{:S(2)}, u32[]{:S(2)}) collective-permute-start(bf16[256,256]{1,0:T(8,128)(2,1)S(1)} %get-tuple-element.18), channel_id=1, source_target_pairs={{1,2},{2,1},{5,6},{6,5},{9,10},{10,9},{13,14},{14,13},{17,18},{18,... | collective-permute-start | bytes 393224 | tf_op jit(solution)/shard_map/ppermute | solution.py:229
  40.3 10.5 %collective-permute-start.6 = (bf16[256,256]{1,0:T(8,128)(2,1)S(1)}, bf16[256,256]{1,0:T(8,128)(2,1)S(1)}, u32[]{:S(2)}, u32[]{:S(2)}) collective-permute-start(bf16[256,256]{1,0:T(8,128)(2,1)S(1)} %get-tuple-element.19), channel_id=1, source_target_pairs={{0,1},{1,0},{2,3},{3,2},{4,5},{5,4},{6,7},{7,6},{8,9},{9,8},{10,11... | collective-permute-start | bytes 393224 | tf_op jit(solution)/shard_map/ppermute | solution.py:229
  42.9 14.6 %collective-permute-start.8 = (bf16[256,256]{1,0:T(8,128)(2,1)S(1)}, bf16[256,256]{1,0:T(8,128)(2,1)S(1)}, u32[]{:S(2)}, u32[]{:S(2)}) collective-permute-start(bf16[256,256]{1,0:T(8,128)(2,1)S(1)} %add.31), channel_id=1, source_target_pairs={{0,2},{1,3},{2,0},{3,1},{4,6},{5,7},{6,4},{7,5},{8,10},{9,11},{10,... | collective-permute-start | bytes 393224 | tf_op jit(solution)/shard_map/ppermute | solution.py:229
  48.8 11.4 %collective-permute-start.16 = (bf16[256,256]{1,0:T(8,128)(2,1)S(1)}, bf16[256,256]{1,0:T(8,128)(2,1)S(1)}, u32[]{:S(2)}, u32[]{:S(2)}) collective-permute-start(bf16[256,256]{1,0:T(8,128)(2,1)S(1)} %get-tuple-element.22), channel_id=1, source_target_pairs={{0,2},{1,3},{2,0},{3,1},{4,6},{5,7},{6,4},{7,5},{8,10},{9,11},{10,... | collective-permute-start | bytes 393224 | tf_op jit(solution)/shard_map/ppermute | solution.py:229
  48.9 11.3 %collective-permute-start.17 = (bf16[256,256]{1,0:T(8,128)(2,1)S(1)}, bf16[256,256]{1,0:T(8,128)(2,1)S(1)}, u32[]{:S(2)}, u32[]{:S(2)}) collective-permute-start(bf16[256,256]{1,0:T(8,128)(2,1)S(1)} %get-tuple-element.23), channel_id=1, source_target_pairs={{0,3},{1,2},{2,1},{3,0},{4,7},{5,6},{6,5},{7,4},{8,11},{9,10},{10,... | collective-permute-start | bytes 393224 | tf_op jit(solution)/shard_map/ppermute | solution.py:229
  50.8 9.4 %collective-permute-start.18 = (bf16[256,256]{1,0:T(8,128)(2,1)S(1)}, bf16[256,256]{1,0:T(8,128)(2,1)S(1)}, u32[]{:S(2)}, u32[]{:S(2)}) collective-permute-start(bf16[256,256]{1,0:T(8,128)(2,1)S(1)} %get-tuple-element.24), channel_id=1, source_target_pairs={{0,1},{1,0},{2,3},{3,2},{4,5},{5,4},{6,7},{7,6},{8,9},{9,8},{10,11... | collective-permute-start | bytes 393224 | tf_op jit(solution)/shard_map/ppermute | solution.py:229
  57.6 4.6 %collective-permute-start.9 = (bf16[128,256]{1,0:T(8,128)(2,1)S(1)}, bf16[128,256]{1,0:T(8,128)(2,1)S(1)}, u32[]{:S(2)}, u32[]{:S(2)}) collective-permute-start(bf16[128,256]{1,0:T(8,128)(2,1)S(1)} %get-tuple-element.28), channel_id=1, source_target_pairs={{0,4},{4,0},{1,5},{5,1},{2,6},{6,2},{3,7},{7,3},{8,12},{12,8},{9,1... | collective-permute-start | bytes 196616 | tf_op jit(solution)/shard_map/ppermute | solution.py:232

commit v6 on v5

--- a/solution.py
+++ b/solution.py
@@ -117,8 +117,6 @@
 def project_kernel(ids, groups, *refs):
     *shares, weight, target = refs
     pieces = [ref[k].astype(F32) for ref in shares for k in range(ref.shape[0])]
-    if len(pieces) > len(ids):
-        pieces[-2:] = [pieces[-2] + pieces[-1]]
     part, size = pieces[0].shape[1], target.shape[2]
     width = part * len(pieces)
     mean = sum(jnp.sum(p, axis=1, keepdims=True) for p in pieces) / width
@@ -245,26 +243,16 @@
     def cost(flops, transcendentals):
         return pl.CostEstimate(flops=flops, bytes_accessed=1 << 20, transcendentals=transcendentals)
 
-    weights = []
     inner = [(1, 2), (2, 1)]
-    outer = [(1, 0), (2, 3)]
-
-    def gather(own_share, tag):
-        far = over_head(own_share, 2)
-        after = far
-        if tag == "a":
-            after, weight = lax.optimization_barrier((far, weight_in))
-            weights.append(weight)
-        near = over_head(own_share, 1)
-        mid = over_head(own_share, inner)
-        relay = over_head(after, outer)
-        return own_share, near, far, mid, relay
+
+    def gather(own_share):
+        return (own_share,) + tuple(over_head(own_share, share_id) for share_id in (1, 2, 3))
 
     def project(shares, groups):
         return kernel_call(
             functools.partial(project_kernel, range(head_size), groups),
             (((2, rows, cols), BF16),),
-            (*shares, weights[0]),
+            (*shares, weight_in),
             cost(rows * weight_in.size, rows * 2 * cols),
         )[0]
 
@@ -303,11 +291,11 @@
     home = lax.dynamic_index_in_dim(inputs[2:], 1 - own, 0, keepdims=True)
     away = lax.dynamic_index_in_dim(inputs[2:], own, 0, keepdims=True)
     high = jnp.concatenate([home, over_ctx(away)], axis=1)
-    low_shares = gather(low, "a")
+    low_shares = gather(low)
     low_keyval = project(low_shares, (1, 3))
     low_other = over_ctx(low_keyval)
     low_gateq = project(low_shares, (0, 2))
-    high_shares = gather(high, "b")
+    high_shares = gather(high)
     high_keyval = project(high_shares, (1, 3))
     high_other = over_ctx(high_keyval)
     high_gateq = project(high_shares, (0, 2))

time: 63.2 us -> 56.6 us (0.90)
  starting transfers between devices: 36.3 us -> 26.2 us
  waiting for transfers between devices: 15.5 us -> 19 us
    ppermute x15 -> x13, starting transfers between devices: 30.1 us -> 20.7 us  [over_head(): return lax.ppermute(value, 'head', pairs)]
    ppermute x15 -> x13, waiting for transfers between devices: 13.7 us -> 17.6 us  [over_head(): return lax.ppermute(value, 'head', pairs)]
    ppermute x4, starting transfers between devices: 6.21 us -> 5.51 us  [over_ctx(): return lax.ppermute(value, 'ctx', [(0, 1), (1, 0)])]
  transfers between devices with their start and end apart: 19 -> 17, of which waited for: 6 -> 7; matrix products, arithmetic and copies ran while one was open for 4% -> 4% of each run, Pallas kernels for 11% -> 12%
where the time goes in v6:
time: 56.6 us; the launch traced here: 56.4 us
  starting transfers between devices  26.2 us (46%)
  waiting for transfers between devices  19 us (34%)
  Pallas kernels  6.82 us (12%)
  local copies, waits for them, and re-layouts  3.17 us (6%)
  other arithmetic  0.96 us (2%)
    ppermute x13, starting transfers between devices, over_head(): return lax.ppermute(value, 'head', pairs)  20.7 us
    ppermute x13, waiting for transfers between devices, over_head(): return lax.ppermute(value, 'head', pairs)  17.6 us
    pallas_call x8, Pallas kernels, kernel_call(): pl.pallas_call(function, compiler_params=pltpu.CompilerParams(vmem_limit_...  6.82 us
    ppermute x4, starting transfers between devices, over_ctx(): return lax.ppermute(value, 'ctx', [(0, 1), (1, 0)])  5.51 us
    unnamed x5, local copies, waits for them, and re-layouts  2.1 us
    ppermute x4, waiting for transfers between devices, over_ctx(): return lax.ppermute(value, 'ctx', [(0, 1), (1, 0)])  1.44 us
  transfers between devices with their start and end apart: 17, of which 7 were waited for; matrix products, arithmetic and copies ran while one was open for 4% of the time, Pallas kernels for 12%

profile of v6, /device:TPU:0, one launch (start us, length us, event | category | flops | bytes accessed | tf_op | source)
XLA Modules:
  0.0 56.4 jit_solution(3780721757364248072)
XLA Ops:
  0.0 1.0 %fusion = (bf16[2,128,256]{2,1,0:T(8,128)(2,1)S(1)}, bf16[2,128,256]{2,1,0:T(8,128)(2,1)S(1)}) fusion(bf16[4,128,256]{2,1,0:T(8,128)(2,1)} %param.4), kind=kLoop, calls=%fused_computation.8 | loop fusion | bytes 524288 | tf_op jit(solution)/shard_map/slice | solution.py:290
  1.0 5.1 %collective-permute-start.2 = (bf16[1,256,256]{2,1,0:T(8,128)(2,1)S(1)}, bf16[1,256,256]{2,1,0:T(8,128)(2,1)S(1)}, u32[]{:S(2)}, u32[]{:S(2)}) collective-permute-start(bf16[1,256,256]{2,1,0:T(8,128)(2,1)S(1)} %bitcast.9), channel_id=1, source_target_pairs={{0,3},{1,2},{2,1},{3,0},{4,7},{5,6},{6,5},{7,4},{8,11},{9,10},{10,... | collective-permute-start | bytes 393224 | tf_op jit(solution)/shard_map/ppermute | solution.py:227
  6.1 0.0 collective-permute-start.1
  6.1 0.6 %collective-permute-start = (bf16[1,256,256]{2,1,0:T(8,128)(2,1)S(1)}, bf16[1,256,256]{2,1,0:T(8,128)(2,1)S(1)}, u32[]{:S(2)}, u32[]{:S(2)}) collective-permute-start(bf16[1,256,256]{2,1,0:T(8,128)(2,1)S(1)} %bitcast.11), channel_id=1, source_target_pairs={{0,1},{1,0},{2,3},{3,2},{4,5},{5,4},{6,7},{7,6},{8,9},{9,8},{10,11... | collective-permute-start | bytes 393224 | tf_op jit(solution)/shard_map/ppermute | solution.py:227
  6.8 1.7 %collective-permute-start.9 = (bf16[1,128,256]{2,1,0:T(8,128)(2,1)S(1)}, bf16[1,128,256]{2,1,0:T(8,128)(2,1)S(1)}, u32[]{:S(2)}, u32[]{:S(2)}) collective-permute-start(bf16[1,128,256]{2,1,0:T(8,128)(2,1)S(1)} %get-tuple-element.26), channel_id=1, source_target_pairs={{0,4},{4,0},{1,5},{5,1},{2,6},{6,2},{3,7},{7,3},{8,12},{12,8},{9,1... | collective-permute-start | bytes 196616 | tf_op jit(solution)/shard_map/ppermute | solution.py:230
  8.5 2.1 %copy.5 = bf16[128,8,4,256]{3,1,2,0:T(8,128)(2,1)S(1)} copy(bf16[128,8,4,256]{3,2,1,0:T(4,128)(2,1)} %bitcast.15) | data formatting | bytes 4194304
  10.6 0.0 collective-permute-done.2.refs_3_
  10.6 6.6 %collective-permute-done.1.refs_2_ = bf16[1,256,256]{2,1,0:T(8,128)(2,1)S(1)} collective-permute-done((bf16[1,256,256]{2,1,0:T(8,128)(2,1)S(1)}, bf16[1,256,256]{2,1,0:T(8,128)(2,1)S(1)}, u32[]{:S(2)}, u32[]{:S(2)}) %collective-permute-start.1) | collective-permute-done | bytes 131104 | tf_op jit(solution)/shard_map/ppermute | solution.py:227
  17.2 0.0 collective-permute-done.refs_1_
  17.2 0.8 %shard_map.46.refs_0_ = bf16[2,256,256]{2,1,0:T(8,128)(2,1)S(1)} custom-call(bf16[1,256,256]{2,1,0:T(8,128)(2,1)S(1)} %bitcast.12, bf16[1,256,256]{2,1,0:T(8,128)(2,1)S(1)} %collective-permute-done.refs_1_, bf16[1,256,256]{2,1,0:T(8,128)(2,1)S(1)} %collective-permute-done.1.refs_2_, bf16[1,256,256]{2,1,0:T(8,128)(2,1)S(1)} %collective-permute-done.2.refs_3_, ...), custom_call_target="tpu_custom_call" | custom-call | flops 268435456 | bytes 1048576 | tf_op jit(solution)/shard_map/pallas_call | solution.py:233
  18.0 0.0 copy-start.1
  18.0 0.0 copy-start
  18.0 1.6 %collective-permute-start.3 = (bf16[2,256,256]{2,1,0:T(8,128)(2,1)S(1)}, bf16[2,256,256]{2,1,0:T(8,128)(2,1)S(1)}, u32[]{:S(2)}, u32[]{:S(2)}) collective-permute-start(bf16[2,256,256]{2,1,0:T(8,128)(2,1)S(1)} %shard_map.46.refs_0_), channel_id=1, source_target_pairs={{0,4},{4,0},{1,5},{5,1},{2,6},{6,2},{3,7},{7,3},{8,12},{12,8},{9,1... | collective-permute-start | bytes 786440 | tf_op jit(solution)/shard_map/ppermute | solution.py:230
  19.6 0.0 collective-permute-done.9
  19.6 2.5 %collective-permute-start.12 = (bf16[1,256,256]{2,1,0:T(8,128)(2,1)S(1)}, bf16[1,256,256]{2,1,0:T(8,128)(2,1)S(1)}, u32[]{:S(2)}, u32[]{:S(2)}) collective-permute-start(bf16[1,256,256]{2,1,0:T(8,128)(2,1)S(1)} %pad_maximum_fusion.1.refs_0_.share), channel_id=1, source_target_pairs={{0,3},{1,2},{2,1},{3,0},{4,7},{5,6},{6,5},{7,4},{8,11},{9,10},{10,... | collective-permute-start | bytes 393224 | tf_op jit(solution)/shard_map/ppermute | solution.py:227
  22.1 0.0 collective-permute-start.11
  22.1 1.9 %collective-permute-start.10 = (bf16[1,256,256]{2,1,0:T(8,128)(2,1)S(1)}, bf16[1,256,256]{2,1,0:T(8,128)(2,1)S(1)}, u32[]{:S(2)}, u32[]{:S(2)}) collective-permute-start(bf16[1,256,256]{2,1,0:T(8,128)(2,1)S(1)} %pad_maximum_fusion.1.refs_0_.share), channel_id=1, source_target_pairs={{0,1},{1,0},{2,3},{3,2},{4,5},{5,4},{6,7},{7,6},{8,9},{9,8},{10,11... | collective-permute-start | bytes 393224 | tf_op jit(solution)/shard_map/ppermute | solution.py:227
  24.1 0.8 %shard_map.47.refs_1_.gateq = bf16[2,256,256]{2,1,0:T(8,128)(2,1)S(1)} custom-call(bf16[1,256,256]{2,1,0:T(8,128)(2,1)S(1)} %bitcast.13, bf16[1,256,256]{2,1,0:T(8,128)(2,1)S(1)} %collective-permute-done.refs_1_, bf16[1,256,256]{2,1,0:T(8,128)(2,1)S(1)} %collective-permute-done.1.refs_2_, bf16[1,256,256]{2,1,0:T(8,128)(2,1)S(1)} %collective-permute-done.2.refs_3_, ...), custom_call_target="tpu_custom_call" | custom-call | flops 268435456 | bytes 1048576 | tf_op jit(solution)/shard_map/pallas_call | solution.py:233
  24.8 0.1 broadcast_in_dim.19.lengths
  24.9 0.6 %shard_map.48.partial = f32[256,256]{1,0:T(8,128)S(1)} custom-call(s32[4,128]{1,0:T(4,128)S(1)} %broadcast_in_dim.19.lengths, bf16[2,256,256]{2,1,0:T(8,128)(2,1)S(1)} %shard_map.46.refs_0_, bf16[2,256,256]{2,1,0:T(8,128)(2,1)S(1)} %shard_map.47.refs_1_.gateq), custom_call_target="tpu_custom_call" | custom-call | flops 67108864 | bytes 1048576 | tf_op jit(solution)/shard_map/pallas_call | solution.py:233
  25.5 0.0 collective-permute-done.3.keyval.refs_1_
  25.5 1.0 %shard_map.49 = (f32[256,256]{1,0:T(8,128)S(1)}, bf16[256,256]{1,0:T(8,128)(2,1)S(1)}, bf16[256,256]{1,0:T(8,128)(2,1)S(1)}, bf16[256,256]{1,0:T(8,128)(2,1)S(1)}) custom-call(s32[4,128]{1,0:T(4,128)S(1)} %broadcast_in_dim.19.lengths, bf16[2,256,256]{2,1,0:T(8,128)(2,1)S(1)} %collective-permute-done.3.keyval.refs_1_, f32[256,256]{1,0:T(8,128)S(1)} %shard_map.48.partial, ...), custom_call_target="tpu_custom_call" | custom-call | flops 201326592 | bytes 1048576 | tf_op jit(solution)/shard_map/pallas_call | solution.py:233
  26.6 2.0 %collective-permute-start.6 = (bf16[256,256]{1,0:T(8,128)(2,1)S(1)}, bf16[256,256]{1,0:T(8,128)(2,1)S(1)}, u32[]{:S(2)}, u32[]{:S(2)}) collective-permute-start(bf16[256,256]{1,0:T(8,128)(2,1)S(1)} %get-tuple-element.14), channel_id=1, source_target_pairs={{0,1},{3,2},{4,5},{7,6},{8,9},{11,10},{12,13},{15,14},{16,17},{19,... | collective-permute-start | bytes 393224 | tf_op jit(solution)/shard_map/ppermute | solution.py:227
  28.6 0.0 collective-permute-done.12.refs_3_
  28.6 3.7 %collective-permute-done.11.refs_2_ = bf16[1,256,256]{2,1,0:T(8,128)(2,1)S(1)} collective-permute-done((bf16[1,256,256]{2,1,0:T(8,128)(2,1)S(1)}, bf16[1,256,256]{2,1,0:T(8,128)(2,1)S(1)}, u32[]{:S(2)}, u32[]{:S(2)}) %collective-permute-start.11) | collective-permute-done | bytes 131104 | tf_op jit(solution)/shard_map/ppermute | solution.py:227
  32.3 0.0 collective-permute-done.10.refs_1_
  32.3 0.8 %shard_map.50.refs_2_ = bf16[2,256,256]{2,1,0:T(8,128)(2,1)S(1)} custom-call(bf16[1,256,256]{2,1,0:T(8,128)(2,1)S(1)} %pad_maximum_fusion.1.refs_0_.share, bf16[1,256,256]{2,1,0:T(8,128)(2,1)S(1)} %collective-permute-done.10.refs_1_, bf16[1,256,256]{2,1,0:T(8,128)(2,1)S(1)} %collective-permute-done.11.refs_2_, ...), custom_call_target="tpu_custom_call" | custom-call | flops 268435456 | bytes 1048576 | tf_op jit(solution)/shard_map/pallas_call | solution.py:233
  33.1 0.6 %collective-permute-start.13 = (bf16[2,256,256]{2,1,0:T(8,128)(2,1)S(1)}, bf16[2,256,256]{2,1,0:T(8,128)(2,1)S(1)}, u32[]{:S(2)}, u32[]{:S(2)}) collective-permute-start(bf16[2,256,256]{2,1,0:T(8,128)(2,1)S(1)} %shard_map.50.refs_2_), channel_id=1, source_target_pairs={{0,4},{4,0},{1,5},{5,1},{2,6},{6,2},{3,7},{7,3},{8,12},{12,8},{9,1... | collective-permute-start | bytes 786440 | tf_op jit(solution)/shard_map/ppermute | solution.py:230
  33.7 0.7 %collective-permute-start.4 = (bf16[256,256]{1,0:T(8,128)(2,1)S(1)}, bf16[256,256]{1,0:T(8,128)(2,1)S(1)}, u32[]{:S(2)}, u32[]{:S(2)}) collective-permute-start(bf16[256,256]{1,0:T(8,128)(2,1)S(1)} %get-tuple-element.14), channel_id=1, source_target_pairs={{1,2},{2,1},{5,6},{6,5},{9,10},{10,9},{13,14},{14,13},{17,18},{18,... | collective-permute-start | bytes 393224 | tf_op jit(solution)/shard_map/ppermute | solution.py:227
  34.3 2.9 %collective-permute-start.5 = (bf16[256,256]{1,0:T(8,128)(2,1)S(1)}, bf16[256,256]{1,0:T(8,128)(2,1)S(1)}, u32[]{:S(2)}, u32[]{:S(2)}) collective-permute-start(bf16[256,256]{1,0:T(8,128)(2,1)S(1)} %get-tuple-element.15), channel_id=1, source_target_pairs={{0,1},{1,0},{2,3},{3,2},{4,5},{5,4},{6,7},{7,6},{8,9},{9,8},{10,11... | collective-permute-start | bytes 393224 | tf_op jit(solution)/shard_map/ppermute | solution.py:227
  37.3 0.9 %collective-permute-start.7 = (bf16[256,256]{1,0:T(8,128)(2,1)S(1)}, bf16[256,256]{1,0:T(8,128)(2,1)S(1)}, u32[]{:S(2)}, u32[]{:S(2)}) collective-permute-start(bf16[256,256]{1,0:T(8,128)(2,1)S(1)} %add.31), channel_id=1, source_target_pairs={{0,2},{1,3},{2,0},{3,1},{4,6},{5,7},{6,4},{7,5},{8,10},{9,11},{10,... | collective-permute-start | bytes 393224 | tf_op jit(solution)/shard_map/ppermute | solution.py:227
  38.2 0.8 %shard_map.51.refs_3_.gateq = bf16[2,256,256]{2,1,0:T(8,128)(2,1)S(1)} custom-call(bf16[1,256,256]{2,1,0:T(8,128)(2,1)S(1)} %pad_maximum_fusion.1.refs_0_.share, bf16[1,256,256]{2,1,0:T(8,128)(2,1)S(1)} %collective-permute-done.10.refs_1_, bf16[1,256,256]{2,1,0:T(8,128)(2,1)S(1)} %collective-permute-done.11.refs_2_, ...), custom_call_target="tpu_custom_call" | custom-call | flops 268435456 | bytes 1048576 | tf_op jit(solution)/shard_map/pallas_call | solution.py:233
  39.0 1.1 %shard_map.52.partial = f32[256,256]{1,0:T(8,128)S(1)} custom-call(s32[4,128]{1,0:T(4,128)S(1)} %broadcast_in_dim.19.lengths, bf16[2,256,256]{2,1,0:T(8,128)(2,1)S(1)} %shard_map.46.refs_0_, bf16[2,256,256]{2,1,0:T(8,128)(2,1)S(1)} %collective-permute-done.3.keyval.refs_1_, bf16[2,256,256]{2,1,0:T(8,128)(2,1)S(1)} %shard_map.50.refs_2_, ...), custom_call_target="tpu_custom_call" | custom-call | flops 201326592 | bytes 1048576 | tf_op jit(solution)/shard_map/pallas_call | solution.py:233
  40.1 0.5 collective-permute-done.13.keyval
  40.6 1.0 %shard_map.53 = (f32[256,256]{1,0:T(8,128)S(1)}, bf16[256,256]{1,0:T(8,128)(2,1)S(1)}, bf16[256,256]{1,0:T(8,128)(2,1)S(1)}, bf16[256,256]{1,0:T(8,128)(2,1)S(1)}) custom-call(s32[4,128]{1,0:T(4,128)S(1)} %broadcast_in_dim.19.lengths, bf16[2,256,256]{2,1,0:T(8,128)(2,1)S(1)} %collective-permute-done.13.keyval, f32[256,256]{1,0:T(8,128)S(1)} %shard_map.52.partial, ...), custom_call_target="tpu_custom_call" | custom-call | flops 201326592 | bytes 1048576 | tf_op jit(solution)/shard_map/pallas_call | solution.py:233
  41.7 1.6 %collective-permute-start.14 = (bf16[256,256]{1,0:T(8,128)(2,1)S(1)}, bf16[256,256]{1,0:T(8,128)(2,1)S(1)}, u32[]{:S(2)}, u32[]{:S(2)}) collective-permute-start(bf16[256,256]{1,0:T(8,128)(2,1)S(1)} %get-tuple-element.18), channel_id=1, source_target_pairs={{0,2},{1,3},{2,0},{3,1},{4,6},{5,7},{6,4},{7,5},{8,10},{9,11},{10,... | collective-permute-start | bytes 393224 | tf_op jit(solution)/shard_map/ppermute | solution.py:227
  43.3 2.3 %collective-permute-start.15 = (bf16[256,256]{1,0:T(8,128)(2,1)S(1)}, bf16[256,256]{1,0:T(8,128)(2,1)S(1)}, u32[]{:S(2)}, u32[]{:S(2)}) collective-permute-start(bf16[256,256]{1,0:T(8,128)(2,1)S(1)} %get-tuple-element.19), channel_id=1, source_target_pairs={{0,3},{1,2},{2,1},{3,0},{4,7},{5,6},{6,5},{7,4},{8,11},{9,10},{10,... | collective-permute-start | bytes 393224 | tf_op jit(solution)/shard_map/ppermute | solution.py:227
  45.6 0.0 collective-permute-start.16
  45.6 0.0 collective-permute-done.4
  45.6 5.6 %collective-permute-done.7 = bf16[256,256]{1,0:T(8,128)(2,1)S(1)} collective-permute-done((bf16[256,256]{1,0:T(8,128)(2,1)S(1)}, bf16[256,256]{1,0:T(8,128)(2,1)S(1)}, u32[]{:S(2)}, u32[]{:S(2)}) %collective-permute-start.7) | collective-permute-done | bytes 131104 | tf_op jit(solution)/shard_map/ppermute | solution.py:227
  51.2 0.1 add_convert_fusion.1
  51.3 1.6 %collective-permute-start.8 = (bf16[128,256]{1,0:T(8,128)(2,1)S(1)}, bf16[128,256]{1,0:T(8,128)(2,1)S(1)}, u32[]{:S(2)}, u32[]{:S(2)}) collective-permute-start(bf16[128,256]{1,0:T(8,128)(2,1)S(1)} %get-tuple-element.24), channel_id=1, source_target_pairs={{0,4},{4,0},{1,5},{5,1},{2,6},{6,2},{3,7},{7,3},{8,12},{12,8},{9,1... | collective-permute-start | bytes 196616 | tf_op jit(solution)/shard_map/ppermute | solution.py:230
  52.9 1.1 %collective-permute-done.14 = bf16[256,256]{1,0:T(8,128)(2,1)S(1)} collective-permute-done((bf16[256,256]{1,0:T(8,128)(2,1)S(1)}, bf16[256,256]{1,0:T(8,128)(2,1)S(1)}, u32[]{:S(2)}, u32[]{:S(2)}) %collective-permute-start.14) | collective-permute-done | bytes 131104 | tf_op jit(solution)/shard_map/ppermute | solution.py:227
  54.0 0.0 collective-permute-done.15
  54.0 0.6 %collective-permute-done.16 = bf16[256,256]{1,0:T(8,128)(2,1)S(1)} collective-permute-done((bf16[256,256]{1,0:T(8,128)(2,1)S(1)}, bf16[256,256]{1,0:T(8,128)(2,1)S(1)}, u32[]{:S(2)}, u32[]{:S(2)}) %collective-permute-start.16) | collective-permute-done | bytes 131104 | tf_op jit(solution)/shard_map/ppermute | solution.py:227
  54.6 0.1 add_convert_fusion
  54.7 0.9 %collective-permute-done.8 = bf16[128,256]{1,0:T(8,128)(2,1)S(1)} collective-permute-done((bf16[128,256]{1,0:T(8,128)(2,1)S(1)}, bf16[128,256]{1,0:T(8,128)(2,1)S(1)}, u32[]{:S(2)}, u32[]{:S(2)}) %collective-permute-start.8) | collective-permute-done | bytes 65568 | tf_op jit(solution)/shard_map/ppermute | solution.py:230
  55.6 0.8 %reverse_select_fusion = bf16[2,2,128,256]{3,2,1,0:T(8,128)(2,1)} fusion(bf16[2,2,128,256]{3,2,1,0:T(8,128)(2,1)S(1)} %bitcast.16, pred[256]{0:T(512)(128)(4,1)S(1)} %compare_reduce_fusion), kind=kLoop, calls=%fused_computation | loop fusion | flops 131072 | bytes 524544 | tf_op jit(solution)/shard_map/jit(_where)/select_n | solution.py:309
  (11 shorter events, 0.1 us)
Async XLA Ops:
  1.0 9.6 %collective-permute-start.2 = (bf16[1,256,256]{2,1,0:T(8,128)(2,1)S(1)}, bf16[1,256,256]{2,1,0:T(8,128)(2,1)S(1)}, u32[]{:S(2)}, u32[]{:S(2)}) collective-permute-start(bf16[1,256,256]{2,1,0:T(8,128)(2,1)S(1)} %bitcast.9), channel_id=1, source_target_pairs={{0,3},{1,2},{2,1},{3,0},{4,7},{5,6},{6,5},{7,4},{8,11},{9,10},{10,... | collective-permute-start | bytes 393224 | tf_op jit(solution)/shard_map/ppermute | solution.py:227
  6.1 11.1 %collective-permute-start.1 = (bf16[1,256,256]{2,1,0:T(8,128)(2,1)S(1)}, bf16[1,256,256]{2,1,0:T(8,128)(2,1)S(1)}, u32[]{:S(2)}, u32[]{:S(2)}) collective-permute-start(bf16[1,256,256]{2,1,0:T(8,128)(2,1)S(1)} %bitcast.10), channel_id=1, source_target_pairs={{0,2},{1,3},{2,0},{3,1},{4,6},{5,7},{6,4},{7,5},{8,10},{9,11},{10,... | collective-permute-start | bytes 393224 | tf_op jit(solution)/shard_map/ppermute | solution.py:227
  6.1 11.1 %collective-permute-start = (bf16[1,256,256]{2,1,0:T(8,128)(2,1)S(1)}, bf16[1,256,256]{2,1,0:T(8,128)(2,1)S(1)}, u32[]{:S(2)}, u32[]{:S(2)}) collective-permute-start(bf16[1,256,256]{2,1,0:T(8,128)(2,1)S(1)} %bitcast.11), channel_id=1, source_target_pairs={{0,1},{1,0},{2,3},{3,2},{4,5},{5,4},{6,7},{7,6},{8,9},{9,8},{10,11... | collective-permute-start | bytes 393224 | tf_op jit(solution)/shard_map/ppermute | solution.py:227
  6.8 12.8 %collective-permute-start.9 = (bf16[1,128,256]{2,1,0:T(8,128)(2,1)S(1)}, bf16[1,128,256]{2,1,0:T(8,128)(2,1)S(1)}, u32[]{:S(2)}, u32[]{:S(2)}) collective-permute-start(bf16[1,128,256]{2,1,0:T(8,128)(2,1)S(1)} %get-tuple-element.26), channel_id=1, source_target_pairs={{0,4},{4,0},{1,5},{5,1},{2,6},{6,2},{3,7},{7,3},{8,12},{12,8},{9,1... | collective-permute-start | bytes 196616 | tf_op jit(solution)/shard_map/ppermute | solution.py:230
  18.0 6.8 %copy-start.1 = (s32[4]{0:T(128)S(1)}, s32[4]{0:T(128)}, u32[]{:S(2)}) copy-start(s32[4]{0:T(128)} %param.5) | copy-start | bytes 52
  18.0 7.5 %copy-start = (bf16[256,1024]{1,0:T(8,128)(2,1)S(1)}, bf16[256,1024]{1,0:T(8,128)(2,1)}, u32[]{:S(2)}) copy-start(bf16[256,1024]{1,0:T(8,128)(2,1)} %weight.3) | copy-start | bytes 1572868
  18.0 7.5 %collective-permute-start.3 = (bf16[2,256,256]{2,1,0:T(8,128)(2,1)S(1)}, bf16[2,256,256]{2,1,0:T(8,128)(2,1)S(1)}, u32[]{:S(2)}, u32[]{:S(2)}) collective-permute-start(bf16[2,256,256]{2,1,0:T(8,128)(2,1)S(1)} %shard_map.46.refs_0_), channel_id=1, source_target_pairs={{0,4},{4,0},{1,5},{5,1},{2,6},{6,2},{3,7},{7,3},{8,12},{12,8},{9,1... | collective-permute-start | bytes 786440 | tf_op jit(solution)/shard_map/ppermute | solution.py:230
  19.6 9.0 %collective-permute-start.12 = (bf16[1,256,256]{2,1,0:T(8,128)(2,1)S(1)}, bf16[1,256,256]{2,1,0:T(8,128)(2,1)S(1)}, u32[]{:S(2)}, u32[]{:S(2)}) collective-permute-start(bf16[1,256,256]{2,1,0:T(8,128)(2,1)S(1)} %pad_maximum_fusion.1.refs_0_.share), channel_id=1, source_target_pairs={{0,3},{1,2},{2,1},{3,0},{4,7},{5,6},{6,5},{7,4},{8,11},{9,10},{10,... | collective-permute-start | bytes 393224 | tf_op jit(solution)/shard_map/ppermute | solution.py:227
  22.1 10.2 %collective-permute-start.11 = (bf16[1,256,256]{2,1,0:T(8,128)(2,1)S(1)}, bf16[1,256,256]{2,1,0:T(8,128)(2,1)S(1)}, u32[]{:S(2)}, u32[]{:S(2)}) collective-permute-start(bf16[1,256,256]{2,1,0:T(8,128)(2,1)S(1)} %pad_maximum_fusion.1.refs_0_.share), channel_id=1, source_target_pairs={{0,2},{1,3},{2,0},{3,1},{4,6},{5,7},{6,4},{7,5},{8,10},{9,11},{10,... | collective-permute-start | bytes 393224 | tf_op jit(solution)/shard_map/ppermute | solution.py:227
  22.1 10.2 %collective-permute-start.10 = (bf16[1,256,256]{2,1,0:T(8,128)(2,1)S(1)}, bf16[1,256,256]{2,1,0:T(8,128)(2,1)S(1)}, u32[]{:S(2)}, u32[]{:S(2)}) collective-permute-start(bf16[1,256,256]{2,1,0:T(8,128)(2,1)S(1)} %pad_maximum_fusion.1.refs_0_.share), channel_id=1, source_target_pairs={{0,1},{1,0},{2,3},{3,2},{4,5},{5,4},{6,7},{7,6},{8,9},{9,8},{10,11... | collective-permute-start | bytes 393224 | tf_op jit(solution)/shard_map/ppermute | solution.py:227
  26.6 10.7 %collective-permute-start.6 = (bf16[256,256]{1,0:T(8,128)(2,1)S(1)}, bf16[256,256]{1,0:T(8,128)(2,1)S(1)}, u32[]{:S(2)}, u32[]{:S(2)}) collective-permute-start(bf16[256,256]{1,0:T(8,128)(2,1)S(1)} %get-tuple-element.14), channel_id=1, source_target_pairs={{0,1},{3,2},{4,5},{7,6},{8,9},{11,10},{12,13},{15,14},{16,17},{19,... | collective-permute-start | bytes 393224 | tf_op jit(solution)/shard_map/ppermute | solution.py:227
  33.1 7.5 %collective-permute-start.13 = (bf16[2,256,256]{2,1,0:T(8,128)(2,1)S(1)}, bf16[2,256,256]{2,1,0:T(8,128)(2,1)S(1)}, u32[]{:S(2)}, u32[]{:S(2)}) collective-permute-start(bf16[2,256,256]{2,1,0:T(8,128)(2,1)S(1)} %shard_map.50.refs_2_), channel_id=1, source_target_pairs={{0,4},{4,0},{1,5},{5,1},{2,6},{6,2},{3,7},{7,3},{8,12},{12,8},{9,1... | collective-permute-start | bytes 786440 | tf_op jit(solution)/shard_map/ppermute | solution.py:230
  33.7 12.0 %collective-permute-start.4 = (bf16[256,256]{1,0:T(8,128)(2,1)S(1)}, bf16[256,256]{1,0:T(8,128)(2,1)S(1)}, u32[]{:S(2)}, u32[]{:S(2)}) collective-permute-start(bf16[256,256]{1,0:T(8,128)(2,1)S(1)} %get-tuple-element.14), channel_id=1, source_target_pairs={{1,2},{2,1},{5,6},{6,5},{9,10},{10,9},{13,14},{14,13},{17,18},{18,... | collective-permute-start | bytes 393224 | tf_op jit(solution)/shard_map/ppermute | solution.py:227
  34.3 11.3 %collective-permute-start.5 = (bf16[256,256]{1,0:T(8,128)(2,1)S(1)}, bf16[256,256]{1,0:T(8,128)(2,1)S(1)}, u32[]{:S(2)}, u32[]{:S(2)}) collective-permute-start(bf16[256,256]{1,0:T(8,128)(2,1)S(1)} %get-tuple-element.15), channel_id=1, source_target_pairs={{0,1},{1,0},{2,3},{3,2},{4,5},{5,4},{6,7},{7,6},{8,9},{9,8},{10,11... | collective-permute-start | bytes 393224 | tf_op jit(solution)/shard_map/ppermute | solution.py:227
  37.3 13.9 %collective-permute-start.7 = (bf16[256,256]{1,0:T(8,128)(2,1)S(1)}, bf16[256,256]{1,0:T(8,128)(2,1)S(1)}, u32[]{:S(2)}, u32[]{:S(2)}) collective-permute-start(bf16[256,256]{1,0:T(8,128)(2,1)S(1)} %add.31), channel_id=1, source_target_pairs={{0,2},{1,3},{2,0},{3,1},{4,6},{5,7},{6,4},{7,5},{8,10},{9,11},{10,... | collective-permute-start | bytes 393224 | tf_op jit(solution)/shard_map/ppermute | solution.py:227
  41.7 12.3 %collective-permute-start.14 = (bf16[256,256]{1,0:T(8,128)(2,1)S(1)}, bf16[256,256]{1,0:T(8,128)(2,1)S(1)}, u32[]{:S(2)}, u32[]{:S(2)}) collective-permute-start(bf16[256,256]{1,0:T(8,128)(2,1)S(1)} %get-tuple-element.18), channel_id=1, source_target_pairs={{0,2},{1,3},{2,0},{3,1},{4,6},{5,7},{6,4},{7,5},{8,10},{9,11},{10,... | collective-permute-start | bytes 393224 | tf_op jit(solution)/shard_map/ppermute | solution.py:227
  43.3 10.7 %collective-permute-start.15 = (bf16[256,256]{1,0:T(8,128)(2,1)S(1)}, bf16[256,256]{1,0:T(8,128)(2,1)S(1)}, u32[]{:S(2)}, u32[]{:S(2)}) collective-permute-start(bf16[256,256]{1,0:T(8,128)(2,1)S(1)} %get-tuple-element.19), channel_id=1, source_target_pairs={{0,3},{1,2},{2,1},{3,0},{4,7},{5,6},{6,5},{7,4},{8,11},{9,10},{10,... | collective-permute-start | bytes 393224 | tf_op jit(solution)/shard_map/ppermute | solution.py:227
  45.6 9.0 %collective-permute-start.16 = (bf16[256,256]{1,0:T(8,128)(2,1)S(1)}, bf16[256,256]{1,0:T(8,128)(2,1)S(1)}, u32[]{:S(2)}, u32[]{:S(2)}) collective-permute-start(bf16[256,256]{1,0:T(8,128)(2,1)S(1)} %get-tuple-element.20), channel_id=1, source_target_pairs={{0,1},{1,0},{2,3},{3,2},{4,5},{5,4},{6,7},{7,6},{8,9},{9,8},{10,11... | collective-permute-start | bytes 393224 | tf_op jit(solution)/shard_map/ppermute | solution.py:227
  51.3 4.3 %collective-permute-start.8 = (bf16[128,256]{1,0:T(8,128)(2,1)S(1)}, bf16[128,256]{1,0:T(8,128)(2,1)S(1)}, u32[]{:S(2)}, u32[]{:S(2)}) collective-permute-start(bf16[128,256]{1,0:T(8,128)(2,1)S(1)} %get-tuple-element.24), channel_id=1, source_target_pairs={{0,4},{4,0},{1,5},{5,1},{2,6},{6,2},{3,7},{7,3},{8,12},{12,8},{9,1... | collective-permute-start | bytes 196616 | tf_op jit(solution)/shard_map/ppermute | solution.py:230
